TPU v7x, 256 devices: a whole 4x4x8 slice. The times are simulated.
256 devices in a mesh: row: 8 (over x, y_lo), col: 32 (over z, y_hi, core).
Axes of the slice: x: 4, y: 4 (y_hi: 2, y_lo: 2; y = y_hi * 2 + y_lo), z: 8, core: 2. Of those that a mesh axis runs over, the one named last changes fastest.
Arguments:
- matrix: bfloat16 [3584, 18432], P('row', 'col'), may hold values from -0.046875 to 0.046875
Outputs:
- update: bfloat16 [3584, 18432], P('row', 'col')
All inputs are finite; a program needn't handle non-finite values.
Results may differ from a plain program's by a relative error of at most 0.0092.
Values may be sent and summed in bfloat16 or wider, within the bound.
No kernel may reach another device: no remote copies, remote signals or barrier semaphores. Data moves between devices by JAX's collectives and lax.ppermute only.
A program may use at most 64 MiB of HBM per device.

v0:
```python
import itertools
import math

import jax
import jax.numpy as jnp
from jax import lax
from jax.experimental import pallas as pl
from jax.experimental.pallas import tpu as pltpu
from jax.sharding import Mesh
from jax.sharding import PartitionSpec as P


coef_a = 3.4445
coef_b = -4.775
coef_c = 2.0315


SIZES = {"x": 4, "yl": 2, "z": 8, "yh": 2, "c": 2}
AXES = tuple(SIZES)
ROW = ("x", "yl")
COL = ("z", "yh", "c")
RING = SIZES["z"]
PANEL = SIZES["x"] * SIZES["yl"]
FAR = RING // 2
LANES = 128
VMEM_LIMIT = 14 << 20

F32 = jnp.float32
BF16 = jnp.bfloat16
VMEM = pl.BlockSpec(memory_space=pltpu.VMEM)
SMEM = pl.BlockSpec(memory_space=pltpu.SMEM)


def array(shape, kind=BF16):
    return jax.ShapeDtypeStruct(shape, kind)


def shift(value, axis, step):
    size = SIZES[axis]
    return lax.ppermute(value, axis, [((i + step) % size, i) for i in range(size)])


def fetch(value, axes, source):
    sizes = [SIZES[a] for a in axes]

    def flat(position):
        index = 0
        for p, n in zip(position, sizes, strict=True):
            index = index * n + p % n
        return index

    places = list(itertools.product(*(range(n) for n in sizes)))
    return lax.ppermute(value, axes, [(flat(source(*p)), flat(p)) for p in places])


def call(body, place, operands, outs, flops=0, scratch=(), fixed=True, home=False, alias=None):
    if fixed:
        operands = [pltpu.with_memory_space_constraint(a, pltpu.VMEM) for a in operands]
    single = not isinstance(outs, list)
    outs = [outs] if single else outs
    moved = sum(math.prod(a.shape) * 2 for a in (*operands, *outs))
    got = pl.pallas_call(
        body,
        out_shape=outs if home else [pltpu.VMEM(o.shape, o.dtype) for o in outs],
        in_specs=[SMEM] + [VMEM] * len(operands),
        out_specs=[VMEM] * len(outs),
        scratch_shapes=list(scratch),
        input_output_aliases=alias or {},
        cost_estimate=pl.CostEstimate(flops=flops, bytes_accessed=moved, transcendentals=0),
        compiler_params=pltpu.CompilerParams(vmem_limit_bytes=VMEM_LIMIT),
    )(place, *operands)
    return got[0] if single else got


def near_blocks(own):
    return lax.optimization_barrier((shift(own, "x", 1), shift(own, "x", -1), shift(own, "yl", 1)))


def halves_of(near_up, near_down):
    half = (near_up.shape[0] // 2 + 15) // 16 * 16
    first = shift(near_up[:half], "x", 1)
    return first, shift(near_down[half:], "x", -1)


def packing(rows, cols):
    width = cols // LANES * LANES
    rest = cols - width
    groups = width // rest
    return width, rest, groups, rows // groups


def pack(block, out):
    rows, cols = block.shape
    width, rest, groups, height = packing(rows, cols)
    out[:rows] = block[:, :width].astype(BF16)
    for g in range(groups):
        out[rows:, g * rest : (g + 1) * rest] = block[g * height : (g + 1) * height, width:].astype(BF16)


def copy_rows(panel, i, begin, ref, rows, width):
    step = math.gcd(math.gcd(rows, begin), 64)

    @pl.loop(0, rows // step)
    def _(k):
        at = pl.multiple_of(k * step, step)
        panel[i, pl.ds(begin + at, step), :width] = ref[pl.ds(at, step), :]


def fill(panel, refs):
    half, cols = panel.shape[1:]
    rows = half // 2
    width, rest, groups, height = packing(rows, cols)
    total = rows + height
    at = 0
    for ref in refs:
        size = ref.shape[0]
        block, begin = divmod(at, total)
        i, base = divmod(block * rows, half)
        main = min(size, rows - begin)
        copy_rows(panel, i, base + begin, ref, main, width)
        if begin + size == total:
            for g in range(groups):
                low = base + g * height
                panel[i, low : low + height, width:] = ref[main:, g * rest : (g + 1) * rest]
        at += size


def pack_body(place, own, packed, copy):
    value = own[...]
    copy[...] = value
    pack(value.astype(F32), packed)


def chunk(z, far, size):
    return pl.ds(pl.multiple_of(lax.rem(z + far, RING) * size, 8), size)


DIMS = (((1,), (1,)), ((), ()))


def gram_body(place, own, *refs):
    *blocks, keep, send, panel, partner, rows, left = refs
    fill(panel, blocks)
    z, c = place[0], place[1]
    height = own.shape[0]
    panel[2, :height] = panel[0, height:]
    panel[2, height:] = panel[1, :height]
    left[0], left[1] = own[...], panel[1, height:]

    @pl.loop(0, 3)
    def _(i):
        rows[i] = lax.dot_general(left[jnp.where(i == 2, 1, 0)], panel[i], DIMS, preferred_element_type=F32)

    partner[...] = rows[2]
    split_units(z, c, rows, keep, send)


def split_units(z, c, rows, keep, send):
    size = keep.shape[1]

    @pl.loop(0, RING)
    def _(far):
        for side, out in ((c, keep), (1 - c, send)):
            out[far] = rows[side, chunk(z, far, size), :].astype(BF16)


def late_body(place, own, low, partner, top, bottom, keep, send, rows, panel, left, blocks):
    z, c = place[0], place[1]
    height = own.shape[0]
    fill(panel, [top, bottom])
    rows[0] = partner[...]
    left[0], left[1] = low[1, height:], own[...]

    @pl.loop(0, 2)
    def _(i):
        blocks[i] = lax.dot_general(left[i], panel[0, :height], DIMS, preferred_element_type=F32)

    rows[1, :, :height] = blocks[0]
    rows[1, :, height:] = blocks[1]
    split_units(z, c, rows, keep, send)


def panel_body(place, low, *refs):
    *blocks, panel, high = refs
    fill(high, blocks)

    @pl.loop(0, 2)
    def _(i):
        panel[i] = low[i]
        panel[i + 2] = high[i]


def pair_body(place, low, low_other, high, high_other, *outs):
    size = low.shape[1]
    for d in range(RING):
        lower = (low[d].astype(F32) + low_other[d].astype(F32)).astype(BF16)
        upper = (high[d].astype(F32) + high_other[d].astype(F32)).astype(BF16)
        if d == FAR:
            outs[d][...] = lower
            outs[d + 1][...] = upper
        else:
            out = outs[d if d < FAR else d + 1]
            out[:size] = lower
            out[size:] = upper


def add(a, b):
    return (a.astype(F32) + b.astype(F32)).astype(BF16)


def ring_sum(part, up, down):
    size = up.shape[0]
    for step in range(FAR - 1, -1, -1):
        up = shift(up, "z", -1)
        down = shift(down, "z", 1)
        if step == 0:
            total = part[0].astype(F32) + up.astype(F32) + down.astype(F32)
        elif step == FAR - 1:
            one, two = part[step], part[RING - step]
            up = jnp.concatenate([add(one[:size], up), one[size:]], 0)
            down = jnp.concatenate([two[:size], add(two[size:], down)], 0)
        else:
            up, down = add(part[step], up), add(part[RING - step], down)
    return total.astype(BF16)


def group_body(place, *refs):
    *pieces, out = refs
    for i, ref in enumerate(pieces):
        out[i] = ref[...]


def lay(gram, side, group, z):
    size = gram.shape[1] // RING

    @pl.loop(0, RING - 1)
    def _(i):
        where = chunk(z, i + jnp.where(i >= FAR, 1, 0), size)
        gram[side, where, :] = group[i, :size]
        gram[side + 2, where, :] = group[i, size:]

    @pl.loop(0, 2)
    def _(i):
        gram[side + 2 * i, chunk(z, FAR, size), :] = jnp.zeros((size, gram.shape[2]), BF16)


def own_rows_body(place, panel, group, gram, total):
    z, c = place[0], place[1]
    lay(gram, c, group, z)
    total[...] = jnp.zeros(total.shape, F32)

    @pl.loop(0, 2)
    def _(i):
        total[...] += jnp.dot(gram[c + 2 * i], panel[c + 2 * i], preferred_element_type=F32)


def other_rows_body(place, panel, group, before_gram, before, gram, total):
    z, side = place[0], 1 - place[1]
    lay(gram, side, group, z)

    @pl.loop(0, 2)
    def _(i):
        total[...] += jnp.dot(gram[side + 2 * i], panel[side + 2 * i], preferred_element_type=F32)


def update_body(place, own, panel, before_gram, before, mine, other, gram, w_high, w_low, total, acc):
    z, c = place[0], place[1]
    size = gram.shape[1] // RING
    where = chunk(z, FAR, size)
    for side, ref in ((c, mine), (1 - c, other)):
        gram[side, where, :] = ref[:size]
        gram[side + 2, where, :] = ref[size:]
    acc[...] = jnp.zeros(acc.shape, F32)

    @pl.loop(0, 4)
    def _(i):
        acc[...] += jnp.dot(gram[i, where, :], panel[i], preferred_element_type=F32)

    total[...] = before[...]
    total[where, :] = acc[...]
    w = coef_b * own[...].astype(F32) + coef_c * total[...]
    pack(w, w_high)
    w_low[...] = (w - w.astype(BF16).astype(F32)).astype(BF16)


def near_body(place, own, w_low, gram, *refs):
    *blocks, total, panel = refs
    rows = own.shape[0]
    fill(panel, blocks)
    panel[3, :rows] = w_low[...]
    panel[3, rows:] = jnp.zeros((rows, own.shape[1]), BF16)
    total[...] = coef_a * own[...].astype(F32)

    @pl.loop(0, 4)
    def _(i):
        total[...] += jnp.dot(gram[jnp.where(i == 3, 0, i)], panel[i], preferred_element_type=F32)


def far_body(place, before, gram, *refs):
    *blocks, out, panel = refs
    rows, cols = out.shape
    fill(panel, blocks)
    acc = before[...] + jnp.dot(gram[3], panel[0], preferred_element_type=F32)
    factor = 0.2 * math.sqrt(max(rows * PANEL, cols * math.prod(SIZES[n] for n in COL)))
    out[...] = (acc * factor).astype(BF16)


def newton_step(matrix):
    rows, cols = matrix.shape
    size = rows // RING
    place = jnp.stack([lax.axis_index("z"), lax.axis_index("c")]).astype(jnp.int32)
    width, _, _, height = packing(rows, cols)
    flat = array((rows + height, width))
    block = array((rows, cols))

    packed, own = call(pack_body, place, (matrix,), [flat, block], fixed=False)
    near = near_blocks(packed)
    r20 = halves_of(near[0], near[1])
    part = array((RING, size, 2 * rows))
    wide = array((4, rows, 2 * rows))
    sums = array((rows, cols), F32)
    work = 4 * rows * rows * cols

    def room(count, kind=BF16, width=cols):
        return pltpu.VMEM((count, 2 * rows, width), kind)

    pairs = pltpu.VMEM((2, rows, 2 * rows), F32)
    keep, send, low, partner = call(
        gram_body,
        place,
        (own, packed, *near),
        [part, part, array((3, 2 * rows, cols)), array((rows, 2 * rows), F32)],
        3 * work,
        [pltpu.VMEM((3, rows, 2 * rows), F32), pltpu.VMEM((2, rows, cols), BF16)],
    )
    halves = [keep, shift(send, "c", 1)]
    scratch = [pairs, room(1), pltpu.VMEM((2, rows, cols), BF16), pltpu.VMEM((2, rows, rows), F32)]
    keep, send = call(late_body, place, (own, low, partner, *r20), [part, part], work, scratch)
    halves += [keep, shift(send, "c", 1)]
    r11 = shift(near[2], "x", 1)
    r31 = shift(near[2], "x", -1)
    r21 = shift(jnp.concatenate(r20, 0), "yl", 1)
    panel = call(panel_body, place, (low, r11, r31, r21, *r20), array((4, 2 * rows, cols)), 0, [room(2)])
    one, two = array((size, 2 * rows)), array((2 * size, 2 * rows))
    parts = call(pair_body, place, halves, [two] * FAR + [one] * 2 + [two] * (FAR - 1))
    part = {d: parts[d if d < FAR else d + 1] for d in range(RING) if d != FAR}
    mine = ring_sum(part, parts[FAR], parts[FAR + 1])
    ahead = mine[size:]
    same = shift(ahead, "yl", 1)
    cross = fetch(ahead, ("yl", "yh"), lambda y, h: (y + 1, h + 1))
    mine = add(mine, shift(mine, "yh", 1))
    ahead = add(same, cross)
    right = lax.broadcasted_iota(jnp.int32, ahead.shape, 1) >= rows
    ahead = jnp.where((place[1] == 1) & right, mine[size:], ahead)
    mine = jnp.concatenate([mine[:size], ahead], 0)

    ring = {0: mine}
    up, down = mine, mine
    for step in range(1, FAR):
        up = shift(up, "z", 1)
        down = shift(down, "z", -1)
        ring[step], ring[RING - step] = up, down
    ends = [shift(up[:size], "z", 1)]
    ends.append(shift(down[size:], "z", -1))
    pieces = [ring[d] for d in range(RING) if d != FAR]
    group = call(group_body, place, pieces, array((RING - 1, 2 * size, 2 * rows)))
    ends = jnp.concatenate(ends, 0)

    other = shift(group, "c", 1)
    gram, total = call(own_rows_body, place, (panel, group), [wide, sums], 2 * work)
    gram, total = call(other_rows_body, place, (panel, other, gram, total), [wide, sums], 2 * work, alias={3: 0, 4: 1})
    gram, w_high, w_low = call(
        update_body,
        place,
        (own, panel, gram, total, ends, shift(ends, "c", 1)),
        [wide, flat, block],
        work // 2,
        [pltpu.VMEM((rows, cols), F32), pltpu.VMEM((size, cols), F32)],
        alias={3: 0},
    )

    near = near_blocks(w_high)
    _, r30, r01 = near
    r20, r11, r31 = lax.optimization_barrier((shift(r30, "x", -1), shift(r01, "x", 1), shift(r30, "yl", 1)))
    blocks = (own, w_low, gram, w_high, *near, r11, r31)
    total = call(near_body, place, blocks, sums, 4 * work, [room(4)])
    r21 = halves_of(r11, r31)
    return call(far_body, place, (total, gram, *r21, r20), block, work, [room(1)], home=True)


def solution(mesh):
    fine = Mesh(mesh.devices.reshape(tuple(SIZES.values())), AXES)
    return jax.shard_map(newton_step, mesh=fine, in_specs=(P(ROW, COL),), out_specs=P(ROW, COL), check_vma=False)
```

profile of v0, /device:TPU:1, one launch (start us, length us, event | category | flops | bytes accessed | tf_op | source)
XLA Modules:
  0.0 168.3 jit_solution(14713941219818935376)
XLA Ops:
  0.1 1.1 copy-done.6
  1.1 0.6 shard_map.17
  1.8 2.2 %collective-permute-start.2 = (bf16[504,512]{1,0:T(8,128)(2,1)S(1)}, bf16[504,512]{1,0:T(8,128)(2,1)S(1)}, u32[]{:S(2)}, u32[]{:S(2)}) collective-permute-start(bf16[504,512]{1,0:T(8,128)(2,1)S(1)} %get-tuple-element.39.refs_0_), channel_id=1, source_target_pairs={{32,0},{0,32},{33,1},{1,33},{34,2},{2,34},{35,3},{3,35},{36,4},{4,... | collective-permute-start | bytes 1548296 | tf_op jit(solution)/shard_map/ppermute | solution.py:40
  4.0 1.2 collective-permute-start.1
  5.2 1.5 collective-permute-start
  6.7 7.6 %collective-permute-done.2.refs_3_ = bf16[504,512]{1,0:T(8,128)(2,1)S(1)} collective-permute-done((bf16[504,512]{1,0:T(8,128)(2,1)S(1)}, bf16[504,512]{1,0:T(8,128)(2,1)S(1)}, u32[]{:S(2)}, u32[]{:S(2)}) %collective-permute-start.2) | collective-permute-done | bytes 516128 | tf_op jit(solution)/shard_map/ppermute | solution.py:40
  14.3 3.0 %collective-permute-done.1.refs_2_ = bf16[504,512]{1,0:T(8,128)(2,1)S(1)} collective-permute-done((bf16[504,512]{1,0:T(8,128)(2,1)S(1)}, bf16[504,512]{1,0:T(8,128)(2,1)S(1)}, u32[]{:S(2)}, u32[]{:S(2)}) %collective-permute-start.1) | collective-permute-done | bytes 516128 | tf_op jit(solution)/shard_map/ppermute | solution.py:40
  17.4 2.5 %collective-permute-start.5 = (bf16[256,512]{1,0:T(8,128)(2,1)S(1)}, bf16[256,512]{1,0:T(8,128)(2,1)S(1)}, u32[]{:S(2)}, u32[]{:S(2)}) collective-permute-start(bf16[256,512]{1,0:T(8,128)(2,1)S(1)} %slice.39), channel_id=1, source_target_pairs={{64,0},{128,64},{192,128},{0,192},{65,1},{129,65},{193,129},{1,193... | collective-permute-start | bytes 786440 | tf_op jit(solution)/shard_map/ppermute | solution.py:40
  19.9 4.2 %shard_map.18 = (bf16[8,56,896]{2,1,0:T(8,128)(2,1)S(1)}, bf16[8,56,896]{2,1,0:T(8,128)(2,1)S(1)}, bf16[3,896,576]{2,1,0:T(8,128)(2,1)S(1)}, f32[448,896]{1,0:T(8,128)S(1)}) custom-call(s32[2]{0:T(128)S(1)} %pad_add_fusion.place, bf16[448,576]{1,0:T(8,128)(2,1)S(1)} %get-tuple-element.38.own, bf16[504,512]{1,0:T(8,128)(2,1)S(1)} %get-tuple-element.39.refs_0_, ...), custom_call_target="tpu_custom_call" | custom-call | flops 1387266048 | bytes 8085504 | tf_op jit(solution)/shard_map/pallas_call | solution.py:62
  24.1 2.7 %collective-permute-start.8 = (bf16[8,56,896]{2,1,0:T(8,128)(2,1)S(1)}, bf16[8,56,896]{2,1,0:T(8,128)(2,1)S(1)}, u32[]{:S(2)}, u32[]{:S(2)}) collective-permute-start(bf16[8,56,896]{2,1,0:T(8,128)(2,1)S(1)} %get-tuple-element.45), channel_id=1, source_target_pairs={{1,0},{0,1},{3,2},{2,3},{5,4},{4,5},{7,6},{6,7},{9,8},{8,9},{11,10... | collective-permute-start | bytes 2408456 | tf_op jit(solution)/shard_map/ppermute | solution.py:40
  26.8 2.4 %shard_map.20 = (bf16[8,56,896]{2,1,0:T(8,128)(2,1)S(1)}, bf16[8,56,896]{2,1,0:T(8,128)(2,1)S(1)}) custom-call(s32[2]{0:T(128)S(1)} %pad_add_fusion.place, bf16[448,576]{1,0:T(8,128)(2,1)S(1)} %get-tuple-element.38.own, bf16[3,896,576]{2,1,0:T(8,128)(2,1)S(1)} %get-tuple-element.43.low, f32[448,896]{1,0:T(8,128)S(1)} %get-tuple-element.46.partner, ...), custom_call_target="tpu_custom_call" | custom-call | flops 462422016 | bytes 6537216 | tf_op jit(solution)/shard_map/pallas_call | solution.py:62
  29.3 3.3 %collective-permute-start.9 = (bf16[8,56,896]{2,1,0:T(8,128)(2,1)S(1)}, bf16[8,56,896]{2,1,0:T(8,128)(2,1)S(1)}, u32[]{:S(2)}, u32[]{:S(2)}) collective-permute-start(bf16[8,56,896]{2,1,0:T(8,128)(2,1)S(1)} %get-tuple-element.48), channel_id=1, source_target_pairs={{1,0},{0,1},{3,2},{2,3},{5,4},{4,5},{7,6},{6,7},{9,8},{8,9},{11,10... | collective-permute-start | bytes 2408456 | tf_op jit(solution)/shard_map/ppermute | solution.py:40
  32.6 1.9 %collective-permute-done.9.high_other = bf16[8,56,896]{2,1,0:T(8,128)(2,1)S(1)} collective-permute-done((bf16[8,56,896]{2,1,0:T(8,128)(2,1)S(1)}, bf16[8,56,896]{2,1,0:T(8,128)(2,1)S(1)}, u32[]{:S(2)}, u32[]{:S(2)}) %collective-permute-start.9) | collective-permute-done | bytes 802848 | tf_op jit(solution)/shard_map/ppermute | solution.py:40
  34.5 0.9 shard_map.21
  35.4 5.7 %collective-permute-start.14 = (bf16[56,896]{1,0:T(8,128)(2,1)S(1)}, bf16[56,896]{1,0:T(8,128)(2,1)S(1)}, u32[]{:S(2)}, u32[]{:S(2)}) collective-permute-start(bf16[56,896]{1,0:T(8,128)(2,1)S(1)} %get-tuple-element.57), channel_id=1, source_target_pairs={{4,0},{8,4},{12,8},{16,12},{20,16},{24,20},{28,24},{0,28},{5,1},{9... | collective-permute-start | bytes 301064 | tf_op jit(solution)/shard_map/ppermute | solution.py:40
  41.2 1.7 %collective-permute-done.14 = bf16[56,896]{1,0:T(8,128)(2,1)S(1)} collective-permute-done((bf16[56,896]{1,0:T(8,128)(2,1)S(1)}, bf16[56,896]{1,0:T(8,128)(2,1)S(1)}, u32[]{:S(2)}, u32[]{:S(2)}) %collective-permute-start.14) | collective-permute-done | bytes 100384 | tf_op jit(solution)/shard_map/ppermute | solution.py:40
  43.0 3.5 %collective-permute-start.15 = (bf16[112,896]{1,0:T(8,128)(2,1)S(1)}, bf16[112,896]{1,0:T(8,128)(2,1)S(1)}, u32[]{:S(2)}, u32[]{:S(2)}) collective-permute-start(bf16[112,896]{1,0:T(8,128)(2,1)S(1)} %pad_maximum_fusion.2), channel_id=1, source_target_pairs={{4,0},{8,4},{12,8},{16,12},{20,16},{24,20},{28,24},{0,28},{5,1},{9... | collective-permute-start | bytes 602120 | tf_op jit(solution)/shard_map/ppermute | solution.py:40
  46.6 3.0 %collective-permute-done.15 = bf16[112,896]{1,0:T(8,128)(2,1)S(1)} collective-permute-done((bf16[112,896]{1,0:T(8,128)(2,1)S(1)}, bf16[112,896]{1,0:T(8,128)(2,1)S(1)}, u32[]{:S(2)}, u32[]{:S(2)}) %collective-permute-start.15) | collective-permute-done | bytes 200736 | tf_op jit(solution)/shard_map/ppermute | solution.py:40
  49.6 3.5 %collective-permute-start.16 = (bf16[112,896]{1,0:T(8,128)(2,1)S(1)}, bf16[112,896]{1,0:T(8,128)(2,1)S(1)}, u32[]{:S(2)}, u32[]{:S(2)}) collective-permute-start(bf16[112,896]{1,0:T(8,128)(2,1)S(1)} %add_convert_fusion.3), channel_id=1, source_target_pairs={{4,0},{8,4},{12,8},{16,12},{20,16},{24,20},{28,24},{0,28},{5,1},{9... | collective-permute-start | bytes 602120 | tf_op jit(solution)/shard_map/ppermute | solution.py:40
  53.2 0.3 collective-permute-start.12
  53.4 2.3 %collective-permute-done.16 = bf16[112,896]{1,0:T(8,128)(2,1)S(1)} collective-permute-done((bf16[112,896]{1,0:T(8,128)(2,1)S(1)}, bf16[112,896]{1,0:T(8,128)(2,1)S(1)}, u32[]{:S(2)}, u32[]{:S(2)}) %collective-permute-start.16) | collective-permute-done | bytes 200736 | tf_op jit(solution)/shard_map/ppermute | solution.py:40
  55.8 3.2 %collective-permute-start.17 = (bf16[112,896]{1,0:T(8,128)(2,1)S(1)}, bf16[112,896]{1,0:T(8,128)(2,1)S(1)}, u32[]{:S(2)}, u32[]{:S(2)}) collective-permute-start(bf16[112,896]{1,0:T(8,128)(2,1)S(1)} %add_convert_fusion.2), channel_id=1, source_target_pairs={{4,0},{8,4},{12,8},{16,12},{20,16},{24,20},{28,24},{0,28},{5,1},{9... | collective-permute-start | bytes 602120 | tf_op jit(solution)/shard_map/ppermute | solution.py:40
  59.0 0.2 collective-permute-done.12
  59.4 2.3 %collective-permute-done.17 = bf16[112,896]{1,0:T(8,128)(2,1)S(1)} collective-permute-done((bf16[112,896]{1,0:T(8,128)(2,1)S(1)}, bf16[112,896]{1,0:T(8,128)(2,1)S(1)}, u32[]{:S(2)}, u32[]{:S(2)}) %collective-permute-start.17) | collective-permute-done | bytes 200736 | tf_op jit(solution)/shard_map/ppermute | solution.py:40
  61.7 3.4 %collective-permute-done.13 = bf16[112,896]{1,0:T(8,128)(2,1)S(1)} collective-permute-done((bf16[112,896]{1,0:T(8,128)(2,1)S(1)}, bf16[112,896]{1,0:T(8,128)(2,1)S(1)}, u32[]{:S(2)}, u32[]{:S(2)}) %collective-permute-start.13) | collective-permute-done | bytes 200736 | tf_op jit(solution)/shard_map/ppermute | solution.py:40
  65.1 0.8 add_convert_fusion.1
  65.9 2.6 %collective-permute-start.18 = (bf16[112,896]{1,0:T(8,128)(2,1)}, bf16[112,896]{1,0:T(8,128)(2,1)}, u32[]{:S(2)}, u32[]{:S(2)}) collective-permute-start(bf16[112,896]{1,0:T(8,128)(2,1)} %add_convert_fusion.1), channel_id=1, source_target_pairs={{2,0},{0,2},{3,1},{1,3},{6,4},{4,6},{7,5},{5,7},{10,8},{8,10},{11,... | collective-permute-start | bytes 602120 | tf_op jit(solution)/shard_map/ppermute | solution.py:40
  68.5 0.9 slice.54
  69.4 0.1 collective-permute-start.20
  69.5 0.1 collective-permute-start.19
  69.6 2.6 %collective-permute-done.18 = bf16[112,896]{1,0:T(8,128)(2,1)} collective-permute-done((bf16[112,896]{1,0:T(8,128)(2,1)}, bf16[112,896]{1,0:T(8,128)(2,1)}, u32[]{:S(2)}, u32[]{:S(2)}) %collective-permute-start.18) | collective-permute-done | bytes 200736 | tf_op jit(solution)/shard_map/ppermute | solution.py:40
  72.3 1.1 add_convert_fusion
  73.3 0.9 collective-permute-done.20
  74.4 2.7 %collective-permute-start.21 = (bf16[112,896]{1,0:T(8,128)(2,1)S(1)}, bf16[112,896]{1,0:T(8,128)(2,1)S(1)}, u32[]{:S(2)}, u32[]{:S(2)}) collective-permute-start(bf16[112,896]{1,0:T(8,128)(2,1)S(1)} %pad_maximum_fusion.3.refs_0_), channel_id=1, source_target_pairs={{4,0},{8,4},{12,8},{16,12},{20,16},{24,20},{28,24},{0,28},{5,1},{9... | collective-permute-start | bytes 602120 | tf_op jit(solution)/shard_map/ppermute | solution.py:40
  77.1 3.1 %collective-permute-done.24.refs_6_ = bf16[112,896]{1,0:T(8,128)(2,1)S(1)} collective-permute-done((bf16[112,896]{1,0:T(8,128)(2,1)S(1)}, bf16[112,896]{1,0:T(8,128)(2,1)S(1)}, u32[]{:S(2)}, u32[]{:S(2)}) %collective-permute-start.24) | collective-permute-done | bytes 200736 | tf_op jit(solution)/shard_map/ppermute | solution.py:40
  80.2 2.7 %collective-permute-start.22 = (bf16[112,896]{1,0:T(8,128)(2,1)S(1)}, bf16[112,896]{1,0:T(8,128)(2,1)S(1)}, u32[]{:S(2)}, u32[]{:S(2)}) collective-permute-start(bf16[112,896]{1,0:T(8,128)(2,1)S(1)} %collective-permute-done.21.refs_1_), channel_id=1, source_target_pairs={{4,0},{8,4},{12,8},{16,12},{20,16},{24,20},{28,24},{0,28},{5,1},{9... | collective-permute-start | bytes 602120 | tf_op jit(solution)/shard_map/ppermute | solution.py:40
  82.9 4.8 %collective-permute-done.25.refs_5_ = bf16[112,896]{1,0:T(8,128)(2,1)S(1)} collective-permute-done((bf16[112,896]{1,0:T(8,128)(2,1)S(1)}, bf16[112,896]{1,0:T(8,128)(2,1)S(1)}, u32[]{:S(2)}, u32[]{:S(2)}) %collective-permute-start.25) | collective-permute-done | bytes 200736 | tf_op jit(solution)/shard_map/ppermute | solution.py:40
  87.6 2.7 %collective-permute-start.23 = (bf16[112,896]{1,0:T(8,128)(2,1)S(1)}, bf16[112,896]{1,0:T(8,128)(2,1)S(1)}, u32[]{:S(2)}, u32[]{:S(2)}) collective-permute-start(bf16[112,896]{1,0:T(8,128)(2,1)S(1)} %collective-permute-done.22.refs_2_), channel_id=1, source_target_pairs={{4,0},{8,4},{12,8},{16,12},{20,16},{24,20},{28,24},{0,28},{5,1},{9... | collective-permute-start | bytes 602120 | tf_op jit(solution)/shard_map/ppermute | solution.py:40
  90.3 3.9 %collective-permute-done.26.refs_4_ = bf16[112,896]{1,0:T(8,128)(2,1)S(1)} collective-permute-done((bf16[112,896]{1,0:T(8,128)(2,1)S(1)}, bf16[112,896]{1,0:T(8,128)(2,1)S(1)}, u32[]{:S(2)}, u32[]{:S(2)}) %collective-permute-start.26) | collective-permute-done | bytes 200736 | tf_op jit(solution)/shard_map/ppermute | solution.py:40
  94.2 0.6 shard_map.22.group
  94.9 9.0 %collective-permute-start.27 = (bf16[7,112,896]{2,1,0:T(8,128)(2,1)S(1)}, bf16[7,112,896]{2,1,0:T(8,128)(2,1)S(1)}, u32[]{:S(2)}, u32[]{:S(2)}) collective-permute-start(bf16[7,112,896]{2,1,0:T(8,128)(2,1)S(1)} %shard_map.22.group), channel_id=1, source_target_pairs={{1,0},{0,1},{3,2},{2,3},{5,4},{4,5},{7,6},{6,7},{9,8},{8,9},{11,10... | collective-permute-start | bytes 4214792 | tf_op jit(solution)/shard_map/ppermute | solution.py:40
  103.9 2.7 %collective-permute-start.3 = (bf16[504,512]{1,0:T(8,128)(2,1)S(1)}, bf16[504,512]{1,0:T(8,128)(2,1)S(1)}, u32[]{:S(2)}, u32[]{:S(2)}) collective-permute-start(bf16[504,512]{1,0:T(8,128)(2,1)S(1)} %copy-done.8), channel_id=1, source_target_pairs={{64,0},{128,64},{192,128},{0,192},{65,1},{129,65},{193,129},{1,193... | collective-permute-start | bytes 1548296 | tf_op jit(solution)/shard_map/ppermute | solution.py:40
  106.6 0.5 collective-permute-start.7
  107.2 3.0 %collective-permute-start.28 = (bf16[56,896]{1,0:T(8,128)(2,1)S(1)}, bf16[56,896]{1,0:T(8,128)(2,1)S(1)}, u32[]{:S(2)}, u32[]{:S(2)}) collective-permute-start(bf16[56,896]{1,0:T(8,128)(2,1)S(1)} %slice.55), channel_id=1, source_target_pairs={{4,0},{8,4},{12,8},{16,12},{20,16},{24,20},{28,24},{0,28},{5,1},{9... | collective-permute-start | bytes 301064 | tf_op jit(solution)/shard_map/ppermute | solution.py:40
  110.2 1.6 collective-permute-done.28
  111.9 5.6 %collective-permute-done.29 = bf16[56,896]{1,0:T(8,128)(2,1)S(1)} collective-permute-done((bf16[56,896]{1,0:T(8,128)(2,1)S(1)}, bf16[56,896]{1,0:T(8,128)(2,1)S(1)}, u32[]{:S(2)}, u32[]{:S(2)}) %collective-permute-start.29) | collective-permute-done | bytes 100384 | tf_op jit(solution)/shard_map/ppermute | solution.py:40
  117.5 2.5 %collective-permute-start.30 = (bf16[112,896]{1,0:T(8,128)(2,1)S(1)}, bf16[112,896]{1,0:T(8,128)(2,1)S(1)}, u32[]{:S(2)}, u32[]{:S(2)}) collective-permute-start(bf16[112,896]{1,0:T(8,128)(2,1)S(1)} %constant_dynamic-update-slice_fusion.mine), channel_id=1, source_target_pairs={{1,0},{0,1},{3,2},{2,3},{5,4},{4,5},{7,6},{6,7},{9,8},{8,9},{11,10... | collective-permute-start | bytes 602120 | tf_op jit(solution)/shard_map/ppermute | solution.py:40
  120.0 1.5 shard_map.19.panel
  121.5 2.6 %shard_map.23 = (bf16[4,448,896]{2,1,0:T(8,128)(2,1)S(1)}, f32[448,576]{1,0:T(8,128)S(1)}) custom-call(s32[2]{0:T(128)S(1)} %pad_add_fusion.place, bf16[4,896,576]{2,1,0:T(8,128)(2,1)S(1)} %shard_map.19.panel, bf16[7,112,896]{2,1,0:T(8,128)(2,1)S(1)} %shard_map.22.group), custom_call_target="tpu_custom_call" | custom-call | flops 924844032 | bytes 9261056 | tf_op jit(solution)/shard_map/pallas_call | solution.py:62
  124.1 2.5 %shard_map.24 = (bf16[4,448,896]{2,1,0:T(8,128)(2,1)S(1)}, f32[448,576]{1,0:T(8,128)S(1)}) custom-call(s32[2]{0:T(128)S(1)} %pad_add_fusion.place, bf16[4,896,576]{2,1,0:T(8,128)(2,1)S(1)} %shard_map.19.panel, bf16[7,112,896]{2,1,0:T(8,128)(2,1)S(1)} %collective-permute-done.27.group, ...), custom_call_target="tpu_custom_call", output_to_operand_aliasing={{0}: (3, {}), {1}: (4, {})} | custom-call | flops 924844032 | bytes 12988416 | tf_op jit(solution)/shard_map/pallas_call | solution.py:62
  126.6 2.5 %shard_map.25 = (bf16[4,448,896]{2,1,0:T(8,128)(2,1)S(1)}, bf16[504,512]{1,0:T(8,128)(2,1)S(1)}, bf16[448,576]{1,0:T(8,128)(2,1)S(1)}) custom-call(s32[2]{0:T(128)S(1)} %pad_add_fusion.place, bf16[448,576]{1,0:T(8,128)(2,1)S(1)} %copy-done.1, bf16[4,896,576]{2,1,0:T(8,128)(2,1)S(1)} %shard_map.19.panel, ...), custom_call_target="tpu_custom_call", output_to_operand_aliasing={{0}: (3, {})} | custom-call | flops 231211008 | bytes 13017088 | tf_op jit(solution)/shard_map/pallas_call | solution.py:62
  129.1 1.1 collective-permute-start.33
  130.2 2.7 %collective-permute-start.31 = (bf16[504,512]{1,0:T(8,128)(2,1)S(1)}, bf16[504,512]{1,0:T(8,128)(2,1)S(1)}, u32[]{:S(2)}, u32[]{:S(2)}) collective-permute-start(bf16[504,512]{1,0:T(8,128)(2,1)S(1)} %get-tuple-element.64.refs_0_), channel_id=1, source_target_pairs={{64,0},{128,64},{192,128},{0,192},{65,1},{129,65},{193,129},{1,193... | collective-permute-start | bytes 1548296 | tf_op jit(solution)/shard_map/ppermute | solution.py:40
  132.9 8.8 %collective-permute-done.33.refs_3_ = bf16[504,512]{1,0:T(8,128)(2,1)S(1)} collective-permute-done((bf16[504,512]{1,0:T(8,128)(2,1)S(1)}, bf16[504,512]{1,0:T(8,128)(2,1)S(1)}, u32[]{:S(2)}, u32[]{:S(2)}) %collective-permute-start.33) | collective-permute-done | bytes 516128 | tf_op jit(solution)/shard_map/ppermute | solution.py:40
  141.6 2.5 %collective-permute-done.32.refs_2_ = bf16[504,512]{1,0:T(8,128)(2,1)S(1)} collective-permute-done((bf16[504,512]{1,0:T(8,128)(2,1)S(1)}, bf16[504,512]{1,0:T(8,128)(2,1)S(1)}, u32[]{:S(2)}, u32[]{:S(2)}) %collective-permute-start.32) | collective-permute-done | bytes 516128 | tf_op jit(solution)/shard_map/ppermute | solution.py:40
  144.1 2.4 %collective-permute-start.35 = (bf16[504,512]{1,0:T(8,128)(2,1)S(1)}, bf16[504,512]{1,0:T(8,128)(2,1)S(1)}, u32[]{:S(2)}, u32[]{:S(2)}) collective-permute-start(bf16[504,512]{1,0:T(8,128)(2,1)S(1)} %collective-permute-done.33.refs_3_), channel_id=1, source_target_pairs={{64,0},{128,64},{192,128},{0,192},{65,1},{129,65},{193,129},{1,193... | collective-permute-start | bytes 1548296 | tf_op jit(solution)/shard_map/ppermute | solution.py:40
  146.5 9.5 %collective-permute-done.35.refs_4_ = bf16[504,512]{1,0:T(8,128)(2,1)S(1)} collective-permute-done((bf16[504,512]{1,0:T(8,128)(2,1)S(1)}, bf16[504,512]{1,0:T(8,128)(2,1)S(1)}, u32[]{:S(2)}, u32[]{:S(2)}) %collective-permute-start.35) | collective-permute-done | bytes 516128 | tf_op jit(solution)/shard_map/ppermute | solution.py:40
  156.0 1.8 %collective-permute-done.36.refs_5_ = bf16[504,512]{1,0:T(8,128)(2,1)S(1)} collective-permute-done((bf16[504,512]{1,0:T(8,128)(2,1)S(1)}, bf16[504,512]{1,0:T(8,128)(2,1)S(1)}, u32[]{:S(2)}, u32[]{:S(2)}) %collective-permute-start.36) | collective-permute-done | bytes 516128 | tf_op jit(solution)/shard_map/ppermute | solution.py:40
  157.8 0.5 collective-permute-done.34.refs_2_
  158.3 1.1 collective-permute-start.37
  159.4 0.5 collective-permute-start.38
  160.0 5.0 %shard_map.26.before = f32[448,576]{1,0:T(8,128)S(1)} custom-call(s32[2]{0:T(128)S(1)} %pad_add_fusion.place, bf16[448,576]{1,0:T(8,128)(2,1)S(1)} %copy-done.1, bf16[448,576]{1,0:T(8,128)(2,1)S(1)} %get-tuple-element.62.w_low, bf16[4,448,896]{2,1,0:T(8,128)(2,1)S(1)} %get-tuple-element.63.gram, bf16[504,512]{1,0:T(8,128)(2,1)S(1)} %get-tuple-element.64.refs_0_, ...), custom_call_target="tpu_custom_call" | custom-call | flops 1849688064 | bytes 7856128 | tf_op jit(solution)/shard_map/pallas_call | solution.py:62
  165.0 0.9 collective-permute-done.38.refs_1_
  165.9 2.4 %shard_map.27 = bf16[448,576]{1,0:T(8,128)(2,1)} custom-call(s32[2]{0:T(128)S(1)} %pad_add_fusion.place, f32[448,576]{1,0:T(8,128)S(1)} %shard_map.26.before, bf16[4,448,896]{2,1,0:T(8,128)(2,1)S(1)} %get-tuple-element.63.gram, bf16[256,512]{1,0:T(8,128)(2,1)S(1)} %collective-permute-done.37.refs_0_, bf16[248,512]{1,0:T(8,128)(2,1)S(1)} %collective-permute-done.38.refs_1_, ...), custom_call_target="tpu_custom_call" | custom-call | flops 462422016 | bytes 5275648 | tf_op jit(solution)/shard_map/pallas_call | solution.py:62
  (69 shorter events, 1.2 us)
Async XLA Ops:
  0.1 1.1 copy-start.6
  1.8 25.1 %copy-start = (bf16[448,576]{1,0:T(8,128)(2,1)}, bf16[448,576]{1,0:T(8,128)(2,1)S(1)}, u32[]{:S(2)}) copy-start(bf16[448,576]{1,0:T(8,128)(2,1)S(1)} %get-tuple-element.38.own) | copy-start | bytes 1548292
  1.8 12.5 %collective-permute-start.2 = (bf16[504,512]{1,0:T(8,128)(2,1)S(1)}, bf16[504,512]{1,0:T(8,128)(2,1)S(1)}, u32[]{:S(2)}, u32[]{:S(2)}) collective-permute-start(bf16[504,512]{1,0:T(8,128)(2,1)S(1)} %get-tuple-element.39.refs_0_), channel_id=1, source_target_pairs={{32,0},{0,32},{33,1},{1,33},{34,2},{2,34},{35,3},{3,35},{36,4},{4,... | collective-permute-start | bytes 1548296 | tf_op jit(solution)/shard_map/ppermute | solution.py:40
  4.0 13.3 %collective-permute-start.1 = (bf16[504,512]{1,0:T(8,128)(2,1)S(1)}, bf16[504,512]{1,0:T(8,128)(2,1)S(1)}, u32[]{:S(2)}, u32[]{:S(2)}) collective-permute-start(bf16[504,512]{1,0:T(8,128)(2,1)S(1)} %get-tuple-element.39.refs_0_), channel_id=1, source_target_pairs={{192,0},{0,64},{64,128},{128,192},{193,1},{1,65},{65,129},{129,193... | collective-permute-start | bytes 1548296 | tf_op jit(solution)/shard_map/ppermute | solution.py:40
  5.2 12.1 %collective-permute-start = (bf16[504,512]{1,0:T(8,128)(2,1)S(1)}, bf16[504,512]{1,0:T(8,128)(2,1)S(1)}, u32[]{:S(2)}, u32[]{:S(2)}) collective-permute-start(bf16[504,512]{1,0:T(8,128)(2,1)S(1)} %get-tuple-element.39.refs_0_), channel_id=1, source_target_pairs={{64,0},{128,64},{192,128},{0,192},{65,1},{129,65},{193,129},{1,193... | collective-permute-start | bytes 1548296 | tf_op jit(solution)/shard_map/ppermute | solution.py:40
  14.3 9.8 %copy-start.7 = (bf16[504,512]{1,0:T(8,128)(2,1)}, bf16[504,512]{1,0:T(8,128)(2,1)S(1)}, u32[]{:S(2)}) copy-start(bf16[504,512]{1,0:T(8,128)(2,1)S(1)} %collective-permute-done.2.refs_3_) | copy-start | bytes 1548292
  17.4 9.5 %collective-permute-start.5 = (bf16[256,512]{1,0:T(8,128)(2,1)S(1)}, bf16[256,512]{1,0:T(8,128)(2,1)S(1)}, u32[]{:S(2)}, u32[]{:S(2)}) collective-permute-start(bf16[256,512]{1,0:T(8,128)(2,1)S(1)} %slice.39), channel_id=1, source_target_pairs={{64,0},{128,64},{192,128},{0,192},{65,1},{129,65},{193,129},{1,193... | collective-permute-start | bytes 786440 | tf_op jit(solution)/shard_map/ppermute | solution.py:40
  19.8 7.0 %collective-permute-start.6 = (bf16[248,512]{1,0:T(8,128)(2,1)S(1)}, bf16[248,512]{1,0:T(8,128)(2,1)S(1)}, u32[]{:S(2)}, u32[]{:S(2)}) collective-permute-start(bf16[248,512]{1,0:T(8,128)(2,1)S(1)} %slice.40), channel_id=1, source_target_pairs={{192,0},{0,64},{64,128},{128,192},{193,1},{1,65},{65,129},{129,193... | collective-permute-start | bytes 761864 | tf_op jit(solution)/shard_map/ppermute | solution.py:40
  24.1 8.4 %collective-permute-start.8 = (bf16[8,56,896]{2,1,0:T(8,128)(2,1)S(1)}, bf16[8,56,896]{2,1,0:T(8,128)(2,1)S(1)}, u32[]{:S(2)}, u32[]{:S(2)}) collective-permute-start(bf16[8,56,896]{2,1,0:T(8,128)(2,1)S(1)} %get-tuple-element.45), channel_id=1, source_target_pairs={{1,0},{0,1},{3,2},{2,3},{5,4},{4,5},{7,6},{6,7},{9,8},{8,9},{11,10... | collective-permute-start | bytes 2408456 | tf_op jit(solution)/shard_map/ppermute | solution.py:40
  26.8 2.5 %copy-start.4 = (bf16[248,512]{1,0:T(8,128)(2,1)}, bf16[248,512]{1,0:T(8,128)(2,1)S(1)}, u32[]{:S(2)}) copy-start(bf16[248,512]{1,0:T(8,128)(2,1)S(1)} %collective-permute-done.6.refs_4_.bottom) | copy-start | bytes 761860
  26.8 2.5 %copy-start.2 = (bf16[256,512]{1,0:T(8,128)(2,1)}, bf16[256,512]{1,0:T(8,128)(2,1)S(1)}, u32[]{:S(2)}) copy-start(bf16[256,512]{1,0:T(8,128)(2,1)S(1)} %collective-permute-done.5.refs_3_.top) | copy-start | bytes 786436
  29.3 5.2 %collective-permute-start.9 = (bf16[8,56,896]{2,1,0:T(8,128)(2,1)S(1)}, bf16[8,56,896]{2,1,0:T(8,128)(2,1)S(1)}, u32[]{:S(2)}, u32[]{:S(2)}) collective-permute-start(bf16[8,56,896]{2,1,0:T(8,128)(2,1)S(1)} %get-tuple-element.48), channel_id=1, source_target_pairs={{1,0},{0,1},{3,2},{2,3},{5,4},{4,5},{7,6},{6,7},{9,8},{8,9},{11,10... | collective-permute-start | bytes 2408456 | tf_op jit(solution)/shard_map/ppermute | solution.py:40
  35.4 7.5 %collective-permute-start.14 = (bf16[56,896]{1,0:T(8,128)(2,1)S(1)}, bf16[56,896]{1,0:T(8,128)(2,1)S(1)}, u32[]{:S(2)}, u32[]{:S(2)}) collective-permute-start(bf16[56,896]{1,0:T(8,128)(2,1)S(1)} %get-tuple-element.57), channel_id=1, source_target_pairs={{4,0},{8,4},{12,8},{16,12},{20,16},{24,20},{28,24},{0,28},{5,1},{9... | collective-permute-start | bytes 301064 | tf_op jit(solution)/shard_map/ppermute | solution.py:40
  41.1 5.3 %collective-permute-start.10 = (bf16[56,896]{1,0:T(8,128)(2,1)S(1)}, bf16[56,896]{1,0:T(8,128)(2,1)S(1)}, u32[]{:S(2)}, u32[]{:S(2)}) collective-permute-start(bf16[56,896]{1,0:T(8,128)(2,1)S(1)} %get-tuple-element.53), channel_id=1, source_target_pairs={{28,0},{0,4},{4,8},{8,12},{12,16},{16,20},{20,24},{24,28},{29,1},{... | collective-permute-start | bytes 301064 | tf_op jit(solution)/shard_map/ppermute | solution.py:40
  43.0 6.6 %collective-permute-start.15 = (bf16[112,896]{1,0:T(8,128)(2,1)S(1)}, bf16[112,896]{1,0:T(8,128)(2,1)S(1)}, u32[]{:S(2)}, u32[]{:S(2)}) collective-permute-start(bf16[112,896]{1,0:T(8,128)(2,1)S(1)} %pad_maximum_fusion.2), channel_id=1, source_target_pairs={{4,0},{8,4},{12,8},{16,12},{20,16},{24,20},{28,24},{0,28},{5,1},{9... | collective-permute-start | bytes 602120 | tf_op jit(solution)/shard_map/ppermute | solution.py:40
  46.5 6.6 %collective-permute-start.11 = (bf16[112,896]{1,0:T(8,128)(2,1)S(1)}, bf16[112,896]{1,0:T(8,128)(2,1)S(1)}, u32[]{:S(2)}, u32[]{:S(2)}) collective-permute-start(bf16[112,896]{1,0:T(8,128)(2,1)S(1)} %pad_maximum_fusion.1), channel_id=1, source_target_pairs={{28,0},{0,4},{4,8},{8,12},{12,16},{16,20},{20,24},{24,28},{29,1},{... | collective-permute-start | bytes 602120 | tf_op jit(solution)/shard_map/ppermute | solution.py:40
  49.6 6.1 %collective-permute-start.16 = (bf16[112,896]{1,0:T(8,128)(2,1)S(1)}, bf16[112,896]{1,0:T(8,128)(2,1)S(1)}, u32[]{:S(2)}, u32[]{:S(2)}) collective-permute-start(bf16[112,896]{1,0:T(8,128)(2,1)S(1)} %add_convert_fusion.3), channel_id=1, source_target_pairs={{4,0},{8,4},{12,8},{16,12},{20,16},{24,20},{28,24},{0,28},{5,1},{9... | collective-permute-start | bytes 602120 | tf_op jit(solution)/shard_map/ppermute | solution.py:40
  53.2 6.0 %collective-permute-start.12 = (bf16[112,896]{1,0:T(8,128)(2,1)S(1)}, bf16[112,896]{1,0:T(8,128)(2,1)S(1)}, u32[]{:S(2)}, u32[]{:S(2)}) collective-permute-start(bf16[112,896]{1,0:T(8,128)(2,1)S(1)} %add_convert_fusion.5), channel_id=1, source_target_pairs={{28,0},{0,4},{4,8},{8,12},{12,16},{16,20},{20,24},{24,28},{29,1},{... | collective-permute-start | bytes 602120 | tf_op jit(solution)/shard_map/ppermute | solution.py:40
  55.8 5.9 %collective-permute-start.17 = (bf16[112,896]{1,0:T(8,128)(2,1)S(1)}, bf16[112,896]{1,0:T(8,128)(2,1)S(1)}, u32[]{:S(2)}, u32[]{:S(2)}) collective-permute-start(bf16[112,896]{1,0:T(8,128)(2,1)S(1)} %add_convert_fusion.2), channel_id=1, source_target_pairs={{4,0},{8,4},{12,8},{16,12},{20,16},{24,20},{28,24},{0,28},{5,1},{9... | collective-permute-start | bytes 602120 | tf_op jit(solution)/shard_map/ppermute | solution.py:40
  59.3 5.9 %collective-permute-start.13 = (bf16[112,896]{1,0:T(8,128)(2,1)S(1)}, bf16[112,896]{1,0:T(8,128)(2,1)S(1)}, u32[]{:S(2)}, u32[]{:S(2)}) collective-permute-start(bf16[112,896]{1,0:T(8,128)(2,1)S(1)} %add_convert_fusion.4), channel_id=1, source_target_pairs={{28,0},{0,4},{4,8},{8,12},{12,16},{16,20},{20,24},{24,28},{29,1},{... | collective-permute-start | bytes 602120 | tf_op jit(solution)/shard_map/ppermute | solution.py:40
  65.9 6.4 %collective-permute-start.18 = (bf16[112,896]{1,0:T(8,128)(2,1)}, bf16[112,896]{1,0:T(8,128)(2,1)}, u32[]{:S(2)}, u32[]{:S(2)}) collective-permute-start(bf16[112,896]{1,0:T(8,128)(2,1)} %add_convert_fusion.1), channel_id=1, source_target_pairs={{2,0},{0,2},{3,1},{1,3},{6,4},{4,6},{7,5},{5,7},{10,8},{8,10},{11,... | collective-permute-start | bytes 602120 | tf_op jit(solution)/shard_map/ppermute | solution.py:40
  69.4 4.8 %collective-permute-start.20 = (bf16[56,896]{1,0:T(8,128)(2,1)S(1)}, bf16[56,896]{1,0:T(8,128)(2,1)S(1)}, u32[]{:S(2)}, u32[]{:S(2)}) collective-permute-start(bf16[56,896]{1,0:T(8,128)(2,1)S(1)} %slice.54), channel_id=1, source_target_pairs={{34,0},{32,2},{2,32},{0,34},{35,1},{33,3},{3,33},{1,35},{38,4},{36... | collective-permute-start | bytes 301064 | tf_op jit(solution)/shard_map/ppermute | solution.py:53
  69.5 4.7 %collective-permute-start.19 = (bf16[56,896]{1,0:T(8,128)(2,1)S(1)}, bf16[56,896]{1,0:T(8,128)(2,1)S(1)}, u32[]{:S(2)}, u32[]{:S(2)}) collective-permute-start(bf16[56,896]{1,0:T(8,128)(2,1)S(1)} %slice.54), channel_id=1, source_target_pairs={{32,0},{0,32},{33,1},{1,33},{34,2},{2,34},{35,3},{3,35},{36,4},{4,... | collective-permute-start | bytes 301064 | tf_op jit(solution)/shard_map/ppermute | solution.py:40
  74.3 29.6 %copy-start.8 = (bf16[504,512]{1,0:T(8,128)(2,1)S(1)}, bf16[504,512]{1,0:T(8,128)(2,1)}, u32[]{:S(2)}) copy-start(bf16[504,512]{1,0:T(8,128)(2,1)} %copy-done.7) | copy-start | bytes 1548292
  74.3 32.3 %copy-start.3 = (bf16[256,512]{1,0:T(8,128)(2,1)S(1)}, bf16[256,512]{1,0:T(8,128)(2,1)}, u32[]{:S(2)}) copy-start(bf16[256,512]{1,0:T(8,128)(2,1)} %copy-done.2) | copy-start | bytes 786436
  74.3 32.3 %copy-start.5 = (bf16[248,512]{1,0:T(8,128)(2,1)S(1)}, bf16[248,512]{1,0:T(8,128)(2,1)}, u32[]{:S(2)}) copy-start(bf16[248,512]{1,0:T(8,128)(2,1)} %copy-done.4) | copy-start | bytes 761860
  74.3 5.9 %collective-permute-start.24 = (bf16[112,896]{1,0:T(8,128)(2,1)S(1)}, bf16[112,896]{1,0:T(8,128)(2,1)S(1)}, u32[]{:S(2)}, u32[]{:S(2)}) collective-permute-start(bf16[112,896]{1,0:T(8,128)(2,1)S(1)} %pad_maximum_fusion.3.refs_0_), channel_id=1, source_target_pairs={{28,0},{0,4},{4,8},{8,12},{12,16},{16,20},{20,24},{24,28},{29,1},{... | collective-permute-start | bytes 602120 | tf_op jit(solution)/shard_map/ppermute | solution.py:40
  74.4 5.8 %collective-permute-start.21 = (bf16[112,896]{1,0:T(8,128)(2,1)S(1)}, bf16[112,896]{1,0:T(8,128)(2,1)S(1)}, u32[]{:S(2)}, u32[]{:S(2)}) collective-permute-start(bf16[112,896]{1,0:T(8,128)(2,1)S(1)} %pad_maximum_fusion.3.refs_0_), channel_id=1, source_target_pairs={{4,0},{8,4},{12,8},{16,12},{20,16},{24,20},{28,24},{0,28},{5,1},{9... | collective-permute-start | bytes 602120 | tf_op jit(solution)/shard_map/ppermute | solution.py:40
  80.2 7.4 %collective-permute-start.25 = (bf16[112,896]{1,0:T(8,128)(2,1)S(1)}, bf16[112,896]{1,0:T(8,128)(2,1)S(1)}, u32[]{:S(2)}, u32[]{:S(2)}) collective-permute-start(bf16[112,896]{1,0:T(8,128)(2,1)S(1)} %collective-permute-done.24.refs_6_), channel_id=1, source_target_pairs={{28,0},{0,4},{4,8},{8,12},{12,16},{16,20},{20,24},{24,28},{29,1},{... | collective-permute-start | bytes 602120 | tf_op jit(solution)/shard_map/ppermute | solution.py:40
  80.2 7.4 %collective-permute-start.22 = (bf16[112,896]{1,0:T(8,128)(2,1)S(1)}, bf16[112,896]{1,0:T(8,128)(2,1)S(1)}, u32[]{:S(2)}, u32[]{:S(2)}) collective-permute-start(bf16[112,896]{1,0:T(8,128)(2,1)S(1)} %collective-permute-done.21.refs_1_), channel_id=1, source_target_pairs={{4,0},{8,4},{12,8},{16,12},{20,16},{24,20},{28,24},{0,28},{5,1},{9... | collective-permute-start | bytes 602120 | tf_op jit(solution)/shard_map/ppermute | solution.py:40
  87.6 6.6 %collective-permute-start.26 = (bf16[112,896]{1,0:T(8,128)(2,1)S(1)}, bf16[112,896]{1,0:T(8,128)(2,1)S(1)}, u32[]{:S(2)}, u32[]{:S(2)}) collective-permute-start(bf16[112,896]{1,0:T(8,128)(2,1)S(1)} %collective-permute-done.25.refs_5_), channel_id=1, source_target_pairs={{28,0},{0,4},{4,8},{8,12},{12,16},{16,20},{20,24},{24,28},{29,1},{... | collective-permute-start | bytes 602120 | tf_op jit(solution)/shard_map/ppermute | solution.py:40
  87.6 6.6 %collective-permute-start.23 = (bf16[112,896]{1,0:T(8,128)(2,1)S(1)}, bf16[112,896]{1,0:T(8,128)(2,1)S(1)}, u32[]{:S(2)}, u32[]{:S(2)}) collective-permute-start(bf16[112,896]{1,0:T(8,128)(2,1)S(1)} %collective-permute-done.22.refs_2_), channel_id=1, source_target_pairs={{4,0},{8,4},{12,8},{16,12},{20,16},{24,20},{28,24},{0,28},{5,1},{9... | collective-permute-start | bytes 602120 | tf_op jit(solution)/shard_map/ppermute | solution.py:40
  94.9 29.2 %collective-permute-start.27 = (bf16[7,112,896]{2,1,0:T(8,128)(2,1)S(1)}, bf16[7,112,896]{2,1,0:T(8,128)(2,1)S(1)}, u32[]{:S(2)}, u32[]{:S(2)}) collective-permute-start(bf16[7,112,896]{2,1,0:T(8,128)(2,1)S(1)} %shard_map.22.group), channel_id=1, source_target_pairs={{1,0},{0,1},{3,2},{2,3},{5,4},{4,5},{7,6},{6,7},{9,8},{8,9},{11,10... | collective-permute-start | bytes 4214792 | tf_op jit(solution)/shard_map/ppermute | solution.py:40
  103.9 16.1 %collective-permute-start.4 = (bf16[504,512]{1,0:T(8,128)(2,1)S(1)}, bf16[504,512]{1,0:T(8,128)(2,1)S(1)}, u32[]{:S(2)}, u32[]{:S(2)}) collective-permute-start(bf16[504,512]{1,0:T(8,128)(2,1)S(1)} %copy-done.8), channel_id=1, source_target_pairs={{192,0},{0,64},{64,128},{128,192},{193,1},{1,65},{65,129},{129,193... | collective-permute-start | bytes 1548296 | tf_op jit(solution)/shard_map/ppermute | solution.py:40
  103.9 16.1 %collective-permute-start.3 = (bf16[504,512]{1,0:T(8,128)(2,1)S(1)}, bf16[504,512]{1,0:T(8,128)(2,1)S(1)}, u32[]{:S(2)}, u32[]{:S(2)}) collective-permute-start(bf16[504,512]{1,0:T(8,128)(2,1)S(1)} %copy-done.8), channel_id=1, source_target_pairs={{64,0},{128,64},{192,128},{0,192},{65,1},{129,65},{193,129},{1,193... | collective-permute-start | bytes 1548296 | tf_op jit(solution)/shard_map/ppermute | solution.py:40
  106.6 13.4 %collective-permute-start.7 = (bf16[504,512]{1,0:T(8,128)(2,1)S(1)}, bf16[504,512]{1,0:T(8,128)(2,1)S(1)}, u32[]{:S(2)}, u32[]{:S(2)}) collective-permute-start(bf16[504,512]{1,0:T(8,128)(2,1)S(1)} %pad_maximum_fusion), channel_id=1, source_target_pairs={{32,0},{0,32},{33,1},{1,33},{34,2},{2,34},{35,3},{3,35},{36,4},{4,... | collective-permute-start | bytes 1548296 | tf_op jit(solution)/shard_map/ppermute | solution.py:40
  107.2 4.7 %collective-permute-start.28 = (bf16[56,896]{1,0:T(8,128)(2,1)S(1)}, bf16[56,896]{1,0:T(8,128)(2,1)S(1)}, u32[]{:S(2)}, u32[]{:S(2)}) collective-permute-start(bf16[56,896]{1,0:T(8,128)(2,1)S(1)} %slice.55), channel_id=1, source_target_pairs={{4,0},{8,4},{12,8},{16,12},{20,16},{24,20},{28,24},{0,28},{5,1},{9... | collective-permute-start | bytes 301064 | tf_op jit(solution)/shard_map/ppermute | solution.py:40
  111.9 5.7 %collective-permute-start.29 = (bf16[56,896]{1,0:T(8,128)(2,1)S(1)}, bf16[56,896]{1,0:T(8,128)(2,1)S(1)}, u32[]{:S(2)}, u32[]{:S(2)}) collective-permute-start(bf16[56,896]{1,0:T(8,128)(2,1)S(1)} %slice.56), channel_id=1, source_target_pairs={{28,0},{0,4},{4,8},{8,12},{12,16},{16,20},{20,24},{24,28},{29,1},{... | collective-permute-start | bytes 301064 | tf_op jit(solution)/shard_map/ppermute | solution.py:40
  117.5 9.0 %collective-permute-start.30 = (bf16[112,896]{1,0:T(8,128)(2,1)S(1)}, bf16[112,896]{1,0:T(8,128)(2,1)S(1)}, u32[]{:S(2)}, u32[]{:S(2)}) collective-permute-start(bf16[112,896]{1,0:T(8,128)(2,1)S(1)} %constant_dynamic-update-slice_fusion.mine), channel_id=1, source_target_pairs={{1,0},{0,1},{3,2},{2,3},{5,4},{4,5},{7,6},{6,7},{9,8},{8,9},{11,10... | collective-permute-start | bytes 602120 | tf_op jit(solution)/shard_map/ppermute | solution.py:40
  124.1 2.5 %copy-start.1 = (bf16[448,576]{1,0:T(8,128)(2,1)S(1)}, bf16[448,576]{1,0:T(8,128)(2,1)}, u32[]{:S(2)}) copy-start(bf16[448,576]{1,0:T(8,128)(2,1)} %copy-done) | copy-start | bytes 1548292
  129.1 12.5 %collective-permute-start.33 = (bf16[504,512]{1,0:T(8,128)(2,1)S(1)}, bf16[504,512]{1,0:T(8,128)(2,1)S(1)}, u32[]{:S(2)}, u32[]{:S(2)}) collective-permute-start(bf16[504,512]{1,0:T(8,128)(2,1)S(1)} %get-tuple-element.64.refs_0_), channel_id=1, source_target_pairs={{32,0},{0,32},{33,1},{1,33},{34,2},{2,34},{35,3},{3,35},{36,4},{4,... | collective-permute-start | bytes 1548296 | tf_op jit(solution)/shard_map/ppermute | solution.py:40
  130.2 13.9 %collective-permute-start.32 = (bf16[504,512]{1,0:T(8,128)(2,1)S(1)}, bf16[504,512]{1,0:T(8,128)(2,1)S(1)}, u32[]{:S(2)}, u32[]{:S(2)}) collective-permute-start(bf16[504,512]{1,0:T(8,128)(2,1)S(1)} %get-tuple-element.64.refs_0_), channel_id=1, source_target_pairs={{192,0},{0,64},{64,128},{128,192},{193,1},{1,65},{65,129},{129,193... | collective-permute-start | bytes 1548296 | tf_op jit(solution)/shard_map/ppermute | solution.py:40
  130.2 13.9 %collective-permute-start.31 = (bf16[504,512]{1,0:T(8,128)(2,1)S(1)}, bf16[504,512]{1,0:T(8,128)(2,1)S(1)}, u32[]{:S(2)}, u32[]{:S(2)}) collective-permute-start(bf16[504,512]{1,0:T(8,128)(2,1)S(1)} %get-tuple-element.64.refs_0_), channel_id=1, source_target_pairs={{64,0},{128,64},{192,128},{0,192},{65,1},{129,65},{193,129},{1,193... | collective-permute-start | bytes 1548296 | tf_op jit(solution)/shard_map/ppermute | solution.py:40
  144.1 11.9 %collective-permute-start.35 = (bf16[504,512]{1,0:T(8,128)(2,1)S(1)}, bf16[504,512]{1,0:T(8,128)(2,1)S(1)}, u32[]{:S(2)}, u32[]{:S(2)}) collective-permute-start(bf16[504,512]{1,0:T(8,128)(2,1)S(1)} %collective-permute-done.33.refs_3_), channel_id=1, source_target_pairs={{64,0},{128,64},{192,128},{0,192},{65,1},{129,65},{193,129},{1,193... | collective-permute-start | bytes 1548296 | tf_op jit(solution)/shard_map/ppermute | solution.py:40
  146.5 11.3 %collective-permute-start.36 = (bf16[504,512]{1,0:T(8,128)(2,1)S(1)}, bf16[504,512]{1,0:T(8,128)(2,1)S(1)}, u32[]{:S(2)}, u32[]{:S(2)}) collective-permute-start(bf16[504,512]{1,0:T(8,128)(2,1)S(1)} %collective-permute-done.32.refs_2_), channel_id=1, source_target_pairs={{32,0},{0,32},{33,1},{1,33},{34,2},{2,34},{35,3},{3,35},{36,4},{4,... | collective-permute-start | bytes 1548296 | tf_op jit(solution)/shard_map/ppermute | solution.py:40
  146.5 11.8 %collective-permute-start.34 = (bf16[504,512]{1,0:T(8,128)(2,1)S(1)}, bf16[504,512]{1,0:T(8,128)(2,1)S(1)}, u32[]{:S(2)}, u32[]{:S(2)}) collective-permute-start(bf16[504,512]{1,0:T(8,128)(2,1)S(1)} %collective-permute-done.32.refs_2_), channel_id=1, source_target_pairs={{192,0},{0,64},{64,128},{128,192},{193,1},{1,65},{65,129},{129,193... | collective-permute-start | bytes 1548296 | tf_op jit(solution)/shard_map/ppermute | solution.py:40
  158.3 7.5 %collective-permute-start.37 = (bf16[256,512]{1,0:T(8,128)(2,1)S(1)}, bf16[256,512]{1,0:T(8,128)(2,1)S(1)}, u32[]{:S(2)}, u32[]{:S(2)}) collective-permute-start(bf16[256,512]{1,0:T(8,128)(2,1)S(1)} %slice.50), channel_id=1, source_target_pairs={{64,0},{128,64},{192,128},{0,192},{65,1},{129,65},{193,129},{1,193... | collective-permute-start | bytes 786440 | tf_op jit(solution)/shard_map/ppermute | solution.py:40
  159.4 6.4 %collective-permute-start.38 = (bf16[248,512]{1,0:T(8,128)(2,1)S(1)}, bf16[248,512]{1,0:T(8,128)(2,1)S(1)}, u32[]{:S(2)}, u32[]{:S(2)}) collective-permute-start(bf16[248,512]{1,0:T(8,128)(2,1)S(1)} %slice.51), channel_id=1, source_target_pairs={{192,0},{0,64},{64,128},{128,192},{193,1},{1,65},{65,129},{129,193... | collective-permute-start | bytes 761864 | tf_op jit(solution)/shard_map/ppermute | solution.py:40
where the time goes:
time: 171 us; the launch traced here: 168 us
  waiting for transfers between devices  72 us (42%)
  starting transfers between devices  66.2 us (39%)
  Pallas kernels  25.3 us (15%)
  other arithmetic  2.34 us (1%)
  local copies, waits for them, and re-layouts  2.15 us (1%)
    ppermute x38, waiting for transfers between devices, shift(): lax.ppermute(value, axis, [((i + step) % size, i) for i in range(size)])  71.2 us
    ppermute x38, starting transfers between devices, shift(): lax.ppermute(value, axis, [((i + step) % size, i) for i in range(size)])  66.1 us
    pallas_call x11, Pallas kernels, call(): pl.pallas_call(body, out_shape=outs if home else [pltpu.VMEM(o.shape, o.d...  25.3 us
  transfers between devices with their start and end apart: 39, of which 22 were waited for; matrix products, arithmetic and copies ran while one was open for 1% of the time, Pallas kernels for 11%

commit v1 on v0

--- a/solution.py
+++ b/solution.py
@@ -106,12 +106,12 @@
         panel[i, pl.ds(begin + at, step), :width] = ref[pl.ds(at, step), :]
 
 
-def fill(panel, refs):
+def fill(panel, refs, skip=0):
     half, cols = panel.shape[1:]
     rows = half // 2
     width, rest, groups, height = packing(rows, cols)
     total = rows + height
-    at = 0
+    at = skip * total
     for ref in refs:
         size = ref.shape[0]
         block, begin = divmod(at, total)
@@ -208,20 +208,35 @@
     return (a.astype(F32) + b.astype(F32)).astype(BF16)
 
 
-def ring_sum(part, up, down):
+def ring_sum(place, part, up, down):
     size = up.shape[0]
     for step in range(FAR - 1, -1, -1):
         up = shift(up, "z", -1)
         down = shift(down, "z", 1)
         if step == 0:
-            total = part[0].astype(F32) + up.astype(F32) + down.astype(F32)
+            return call(sum_body, place, (part[0], up, down), [array(part[0].shape), array((size, up.shape[1]))])
         elif step == FAR - 1:
             one, two = part[step], part[RING - step]
             up = jnp.concatenate([add(one[:size], up), one[size:]], 0)
             down = jnp.concatenate([two[:size], add(two[size:], down)], 0)
         else:
             up, down = add(part[step], up), add(part[RING - step], down)
-    return total.astype(BF16)
+
+
+def sum_body(place, near, up, down, mine, ahead):
+    size = ahead.shape[0]
+    total = near[...].astype(F32) + up[...].astype(F32) + down[...].astype(F32)
+    mine[...] = total.astype(BF16)
+    ahead[...] = total[size:].astype(BF16)
+
+
+def join_body(place, mine, across, same, cross, out):
+    size, width = same.shape
+    own = mine[...].astype(F32) + across[...].astype(F32)
+    ahead = same[...].astype(F32) + cross[...].astype(F32)
+    right = lax.broadcasted_iota(jnp.int32, (size, width), 1) >= width // 2
+    out[:size] = own[:size].astype(BF16)
+    out[size:] = jnp.where(right & (place[1] == 1), own[size:], ahead).astype(BF16)
 
 
 def group_body(place, *refs):
@@ -284,23 +299,26 @@
 
 
 def near_body(place, own, w_low, gram, *refs):
-    *blocks, total, panel = refs
+    *blocks, r20, total, panel = refs
     rows = own.shape[0]
     fill(panel, blocks)
+    fill(panel, [r20], 9)
     panel[3, :rows] = w_low[...]
     panel[3, rows:] = jnp.zeros((rows, own.shape[1]), BF16)
+    panel[4, :rows] = jnp.zeros((rows, own.shape[1]), BF16)
     total[...] = coef_a * own[...].astype(F32)
 
-    @pl.loop(0, 4)
-    def _(i):
-        total[...] += jnp.dot(gram[jnp.where(i == 3, 0, i)], panel[i], preferred_element_type=F32)
+    @pl.loop(0, 5)
+    def _(i):
+        side = jnp.where(i == 3, 0, jnp.minimum(i, 3))
+        total[...] += jnp.dot(gram[side], panel[i], preferred_element_type=F32)
 
 
 def far_body(place, before, gram, *refs):
-    *blocks, out, panel = refs
+    *pieces, out, panel = refs
     rows, cols = out.shape
-    fill(panel, blocks)
-    acc = before[...] + jnp.dot(gram[3], panel[0], preferred_element_type=F32)
+    fill(panel, pieces)
+    acc = before[...] + jnp.dot(gram[3][:, :rows], panel[0, :rows], preferred_element_type=F32)
     factor = 0.2 * math.sqrt(max(rows * PANEL, cols * math.prod(SIZES[n] for n in COL)))
     out[...] = (acc * factor).astype(BF16)
 
@@ -339,20 +357,17 @@
     halves += [keep, shift(send, "c", 1)]
     r11 = shift(near[2], "x", 1)
     r31 = shift(near[2], "x", -1)
-    r21 = shift(jnp.concatenate(r20, 0), "yl", 1)
+    r21 = jnp.concatenate(r20, 0)
+    r21 = shift(r21, "yl", 1)
     panel = call(panel_body, place, (low, r11, r31, r21, *r20), array((4, 2 * rows, cols)), 0, [room(2)])
     one, two = array((size, 2 * rows)), array((2 * size, 2 * rows))
     parts = call(pair_body, place, halves, [two] * FAR + [one] * 2 + [two] * (FAR - 1))
     part = {d: parts[d if d < FAR else d + 1] for d in range(RING) if d != FAR}
-    mine = ring_sum(part, parts[FAR], parts[FAR + 1])
-    ahead = mine[size:]
+    mine, ahead = ring_sum(place, part, parts[FAR], parts[FAR + 1])
+    across = shift(mine, "yh", 1)
     same = shift(ahead, "yl", 1)
     cross = fetch(ahead, ("yl", "yh"), lambda y, h: (y + 1, h + 1))
-    mine = add(mine, shift(mine, "yh", 1))
-    ahead = add(same, cross)
-    right = lax.broadcasted_iota(jnp.int32, ahead.shape, 1) >= rows
-    ahead = jnp.where((place[1] == 1) & right, mine[size:], ahead)
-    mine = jnp.concatenate([mine[:size], ahead], 0)
+    mine = call(join_body, place, (mine, across, same, cross), array(mine.shape))
 
     ring = {0: mine}
     up, down = mine, mine
@@ -382,10 +397,10 @@
     near = near_blocks(w_high)
     _, r30, r01 = near
     r20, r11, r31 = lax.optimization_barrier((shift(r30, "x", -1), shift(r01, "x", 1), shift(r30, "yl", 1)))
-    blocks = (own, w_low, gram, w_high, *near, r11, r31)
-    total = call(near_body, place, blocks, sums, 4 * work, [room(4)])
+    blocks = (own, w_low, gram, w_high, *near, r11, r31, r20)
+    total = call(near_body, place, blocks, sums, 5 * work, [room(5)])
     r21 = halves_of(r11, r31)
-    return call(far_body, place, (total, gram, *r21, r20), block, work, [room(1)], home=True)
+    return call(far_body, place, (total, gram, *r21), block, work // 2, [room(1)], home=True)
 
 
 def solution(mesh):

time: 171 us -> 170 us (level); the launches traced: 168 us -> 169 us
  other arithmetic: 2.34 us -> 0.41 us
  starting transfers between devices: 66.2 us -> 68.1 us
    ppermute x1, waiting for transfers between devices: 0.87 us -> 4.67 us  [fetch(): lax.ppermute(value, axes, [(flat(source(*p)), flat(p)) for p in places])]
    ppermute x38, waiting for transfers between devices: 71.2 us -> 67.5 us  [shift(): lax.ppermute(value, axis, [((i + step) % size, i) for i in range(size)])]
    ppermute x38, starting transfers between devices: 66.1 us -> 68.1 us  [shift(): lax.ppermute(value, axis, [((i + step) % size, i) for i in range(size)])]
    pallas_call x11 -> x13, Pallas kernels: 25.3 us -> 27 us  [call(): pl.pallas_call(body, out_shape=outs if home else [pltpu.VMEM(o.shape, o.d...]
  transfers between devices with their start and end apart: 39 -> 39, of which waited for: 22 -> 20; matrix products, arithmetic and copies ran while one was open for 1% -> 0% of each run, Pallas kernels for 11% -> 11%
where the time goes in v1:
time: 170 us; the launch traced here: 169 us
  waiting for transfers between devices  72.2 us (42%)
  starting transfers between devices  68.1 us (40%)
  Pallas kernels  27 us (16%)
    ppermute x38, starting transfers between devices, shift(): lax.ppermute(value, axis, [((i + step) % size, i) for i in range(size)])  68.1 us
    ppermute x38, waiting for transfers between devices, shift(): lax.ppermute(value, axis, [((i + step) % size, i) for i in range(size)])  67.5 us
    pallas_call x13, Pallas kernels, call(): pl.pallas_call(body, out_shape=outs if home else [pltpu.VMEM(o.shape, o.d...  27 us
    ppermute x1, waiting for transfers between devices, fetch(): lax.ppermute(value, axes, [(flat(source(*p)), flat(p)) for p in places])  4.67 us
  transfers between devices with their start and end apart: 39, of which 20 were waited for; matrix products, arithmetic and copies ran while one was open for 0% of the time, Pallas kernels for 11%

profile of v1, /device:TPU:1, one launch (start us, length us, event | category | flops | bytes accessed | tf_op | source)
XLA Modules:
  0.0 169.2 jit_solution(1853525588815820429)
XLA Ops:
  0.1 1.1 copy-done
  1.1 0.6 shard_map.17
  1.8 2.2 %collective-permute-start.2 = (bf16[504,512]{1,0:T(8,128)(2,1)S(1)}, bf16[504,512]{1,0:T(8,128)(2,1)S(1)}, u32[]{:S(2)}, u32[]{:S(2)}) collective-permute-start(bf16[504,512]{1,0:T(8,128)(2,1)S(1)} %get-tuple-element.41.refs_0_), channel_id=1, source_target_pairs={{32,0},{0,32},{33,1},{1,33},{34,2},{2,34},{35,3},{3,35},{36,4},{4,... | collective-permute-start | bytes 1548296 | tf_op jit(solution)/shard_map/ppermute | solution.py:40
  4.0 1.2 collective-permute-start.1
  5.2 1.5 collective-permute-start
  6.7 7.6 %collective-permute-done.2.refs_3_ = bf16[504,512]{1,0:T(8,128)(2,1)S(1)} collective-permute-done((bf16[504,512]{1,0:T(8,128)(2,1)S(1)}, bf16[504,512]{1,0:T(8,128)(2,1)S(1)}, u32[]{:S(2)}, u32[]{:S(2)}) %collective-permute-start.2) | collective-permute-done | bytes 516128 | tf_op jit(solution)/shard_map/ppermute | solution.py:40
  14.3 3.0 %collective-permute-done.1.refs_2_ = bf16[504,512]{1,0:T(8,128)(2,1)S(1)} collective-permute-done((bf16[504,512]{1,0:T(8,128)(2,1)S(1)}, bf16[504,512]{1,0:T(8,128)(2,1)S(1)}, u32[]{:S(2)}, u32[]{:S(2)}) %collective-permute-start.1) | collective-permute-done | bytes 516128 | tf_op jit(solution)/shard_map/ppermute | solution.py:40
  17.3 2.5 %collective-permute-start.5 = (bf16[256,512]{1,0:T(8,128)(2,1)S(1)}, bf16[256,512]{1,0:T(8,128)(2,1)S(1)}, u32[]{:S(2)}, u32[]{:S(2)}) collective-permute-start(bf16[256,512]{1,0:T(8,128)(2,1)S(1)} %slice.30), channel_id=1, source_target_pairs={{64,0},{128,64},{192,128},{0,192},{65,1},{129,65},{193,129},{1,193... | collective-permute-start | bytes 786440 | tf_op jit(solution)/shard_map/ppermute | solution.py:40
  19.8 0.1 collective-permute-start.6
  19.9 4.2 %shard_map.18 = (bf16[8,56,896]{2,1,0:T(8,128)(2,1)S(1)}, bf16[8,56,896]{2,1,0:T(8,128)(2,1)S(1)}, bf16[3,896,576]{2,1,0:T(8,128)(2,1)S(1)}, f32[448,896]{1,0:T(8,128)S(1)}) custom-call(s32[2]{0:T(128)S(1)} %pad_add_fusion.place, bf16[448,576]{1,0:T(8,128)(2,1)S(1)} %get-tuple-element.40.own, bf16[504,512]{1,0:T(8,128)(2,1)S(1)} %get-tuple-element.41.refs_0_, ...), custom_call_target="tpu_custom_call" | custom-call | flops 1387266048 | bytes 8085504 | tf_op jit(solution)/shard_map/pallas_call | solution.py:62
  24.1 2.7 %collective-permute-start.8 = (bf16[8,56,896]{2,1,0:T(8,128)(2,1)S(1)}, bf16[8,56,896]{2,1,0:T(8,128)(2,1)S(1)}, u32[]{:S(2)}, u32[]{:S(2)}) collective-permute-start(bf16[8,56,896]{2,1,0:T(8,128)(2,1)S(1)} %get-tuple-element.47), channel_id=1, source_target_pairs={{1,0},{0,1},{3,2},{2,3},{5,4},{4,5},{7,6},{6,7},{9,8},{8,9},{11,10... | collective-permute-start | bytes 2408456 | tf_op jit(solution)/shard_map/ppermute | solution.py:40
  26.8 2.4 %shard_map.20 = (bf16[8,56,896]{2,1,0:T(8,128)(2,1)S(1)}, bf16[8,56,896]{2,1,0:T(8,128)(2,1)S(1)}) custom-call(s32[2]{0:T(128)S(1)} %pad_add_fusion.place, bf16[448,576]{1,0:T(8,128)(2,1)S(1)} %get-tuple-element.40.own, bf16[3,896,576]{2,1,0:T(8,128)(2,1)S(1)} %get-tuple-element.45.low, f32[448,896]{1,0:T(8,128)S(1)} %get-tuple-element.48.partner, ...), custom_call_target="tpu_custom_call" | custom-call | flops 462422016 | bytes 6537216 | tf_op jit(solution)/shard_map/pallas_call | solution.py:62
  29.2 3.3 %collective-permute-start.9 = (bf16[8,56,896]{2,1,0:T(8,128)(2,1)S(1)}, bf16[8,56,896]{2,1,0:T(8,128)(2,1)S(1)}, u32[]{:S(2)}, u32[]{:S(2)}) collective-permute-start(bf16[8,56,896]{2,1,0:T(8,128)(2,1)S(1)} %get-tuple-element.50), channel_id=1, source_target_pairs={{1,0},{0,1},{3,2},{2,3},{5,4},{4,5},{7,6},{6,7},{9,8},{8,9},{11,10... | collective-permute-start | bytes 2408456 | tf_op jit(solution)/shard_map/ppermute | solution.py:40
  32.5 1.9 %collective-permute-done.9.high_other = bf16[8,56,896]{2,1,0:T(8,128)(2,1)S(1)} collective-permute-done((bf16[8,56,896]{2,1,0:T(8,128)(2,1)S(1)}, bf16[8,56,896]{2,1,0:T(8,128)(2,1)S(1)}, u32[]{:S(2)}, u32[]{:S(2)}) %collective-permute-start.9) | collective-permute-done | bytes 802848 | tf_op jit(solution)/shard_map/ppermute | solution.py:40
  34.5 0.9 shard_map.21
  35.4 5.7 %collective-permute-start.14 = (bf16[56,896]{1,0:T(8,128)(2,1)S(1)}, bf16[56,896]{1,0:T(8,128)(2,1)S(1)}, u32[]{:S(2)}, u32[]{:S(2)}) collective-permute-start(bf16[56,896]{1,0:T(8,128)(2,1)S(1)} %get-tuple-element.59), channel_id=1, source_target_pairs={{4,0},{8,4},{12,8},{16,12},{20,16},{24,20},{28,24},{0,28},{5,1},{9... | collective-permute-start | bytes 301064 | tf_op jit(solution)/shard_map/ppermute | solution.py:40
  41.1 0.1 collective-permute-start.10
  41.2 1.7 %collective-permute-done.14 = bf16[56,896]{1,0:T(8,128)(2,1)S(1)} collective-permute-done((bf16[56,896]{1,0:T(8,128)(2,1)S(1)}, bf16[56,896]{1,0:T(8,128)(2,1)S(1)}, u32[]{:S(2)}, u32[]{:S(2)}) %collective-permute-start.14) | collective-permute-done | bytes 100384 | tf_op jit(solution)/shard_map/ppermute | solution.py:40
  42.9 3.5 %collective-permute-start.15 = (bf16[112,896]{1,0:T(8,128)(2,1)S(1)}, bf16[112,896]{1,0:T(8,128)(2,1)S(1)}, u32[]{:S(2)}, u32[]{:S(2)}) collective-permute-start(bf16[112,896]{1,0:T(8,128)(2,1)S(1)} %pad_maximum_fusion.2), channel_id=1, source_target_pairs={{4,0},{8,4},{12,8},{16,12},{20,16},{24,20},{28,24},{0,28},{5,1},{9... | collective-permute-start | bytes 602120 | tf_op jit(solution)/shard_map/ppermute | solution.py:40
  46.5 0.1 collective-permute-start.11
  46.6 3.0 %collective-permute-done.15 = bf16[112,896]{1,0:T(8,128)(2,1)S(1)} collective-permute-done((bf16[112,896]{1,0:T(8,128)(2,1)S(1)}, bf16[112,896]{1,0:T(8,128)(2,1)S(1)}, u32[]{:S(2)}, u32[]{:S(2)}) %collective-permute-start.15) | collective-permute-done | bytes 200736 | tf_op jit(solution)/shard_map/ppermute | solution.py:40
  49.6 3.5 %collective-permute-start.16 = (bf16[112,896]{1,0:T(8,128)(2,1)S(1)}, bf16[112,896]{1,0:T(8,128)(2,1)S(1)}, u32[]{:S(2)}, u32[]{:S(2)}) collective-permute-start(bf16[112,896]{1,0:T(8,128)(2,1)S(1)} %add_convert_fusion.1), channel_id=1, source_target_pairs={{4,0},{8,4},{12,8},{16,12},{20,16},{24,20},{28,24},{0,28},{5,1},{9... | collective-permute-start | bytes 602120 | tf_op jit(solution)/shard_map/ppermute | solution.py:40
  53.1 0.3 collective-permute-start.12
  53.4 2.3 %collective-permute-done.16 = bf16[112,896]{1,0:T(8,128)(2,1)S(1)} collective-permute-done((bf16[112,896]{1,0:T(8,128)(2,1)S(1)}, bf16[112,896]{1,0:T(8,128)(2,1)S(1)}, u32[]{:S(2)}, u32[]{:S(2)}) %collective-permute-start.16) | collective-permute-done | bytes 200736 | tf_op jit(solution)/shard_map/ppermute | solution.py:40
  55.8 3.2 %collective-permute-start.17 = (bf16[112,896]{1,0:T(8,128)(2,1)S(1)}, bf16[112,896]{1,0:T(8,128)(2,1)S(1)}, u32[]{:S(2)}, u32[]{:S(2)}) collective-permute-start(bf16[112,896]{1,0:T(8,128)(2,1)S(1)} %add_convert_fusion), channel_id=1, source_target_pairs={{4,0},{8,4},{12,8},{16,12},{20,16},{24,20},{28,24},{0,28},{5,1},{9... | collective-permute-start | bytes 602120 | tf_op jit(solution)/shard_map/ppermute | solution.py:40
  59.0 0.2 collective-permute-done.12
  59.2 0.1 collective-permute-start.13
  59.3 2.3 %collective-permute-done.17.down = bf16[112,896]{1,0:T(8,128)(2,1)S(1)} collective-permute-done((bf16[112,896]{1,0:T(8,128)(2,1)S(1)}, bf16[112,896]{1,0:T(8,128)(2,1)S(1)}, u32[]{:S(2)}, u32[]{:S(2)}) %collective-permute-start.17) | collective-permute-done | bytes 200736 | tf_op jit(solution)/shard_map/ppermute | solution.py:40
  61.6 3.4 %collective-permute-done.13.up = bf16[112,896]{1,0:T(8,128)(2,1)S(1)} collective-permute-done((bf16[112,896]{1,0:T(8,128)(2,1)S(1)}, bf16[112,896]{1,0:T(8,128)(2,1)S(1)}, u32[]{:S(2)}, u32[]{:S(2)}) %collective-permute-start.13) | collective-permute-done | bytes 200736 | tf_op jit(solution)/shard_map/ppermute | solution.py:40
  65.1 0.6 shard_map.22
  65.7 2.7 %collective-permute-start.18 = (bf16[112,896]{1,0:T(8,128)(2,1)S(1)}, bf16[112,896]{1,0:T(8,128)(2,1)S(1)}, u32[]{:S(2)}, u32[]{:S(2)}) collective-permute-start(bf16[112,896]{1,0:T(8,128)(2,1)S(1)} %get-tuple-element.60.mine), channel_id=1, source_target_pairs={{2,0},{0,2},{3,1},{1,3},{6,4},{4,6},{7,5},{5,7},{10,8},{8,10},{11,... | collective-permute-start | bytes 602120 | tf_op jit(solution)/shard_map/ppermute | solution.py:40
  68.4 4.7 %collective-permute-done.20.cross = bf16[56,896]{1,0:T(8,128)(2,1)S(1)} collective-permute-done((bf16[56,896]{1,0:T(8,128)(2,1)S(1)}, bf16[56,896]{1,0:T(8,128)(2,1)S(1)}, u32[]{:S(2)}, u32[]{:S(2)}) %collective-permute-start.20) | collective-permute-done | bytes 100384 | tf_op jit(solution)/shard_map/ppermute | solution.py:53
  73.1 0.6 shard_map.23.refs_0_
  73.7 0.1 collective-permute-start.24
  73.8 2.7 %collective-permute-start.21 = (bf16[112,896]{1,0:T(8,128)(2,1)S(1)}, bf16[112,896]{1,0:T(8,128)(2,1)S(1)}, u32[]{:S(2)}, u32[]{:S(2)}) collective-permute-start(bf16[112,896]{1,0:T(8,128)(2,1)S(1)} %shard_map.23.refs_0_), channel_id=1, source_target_pairs={{4,0},{8,4},{12,8},{16,12},{20,16},{24,20},{28,24},{0,28},{5,1},{9... | collective-permute-start | bytes 602120 | tf_op jit(solution)/shard_map/ppermute | solution.py:40
  76.5 3.1 %collective-permute-done.24.refs_6_ = bf16[112,896]{1,0:T(8,128)(2,1)S(1)} collective-permute-done((bf16[112,896]{1,0:T(8,128)(2,1)S(1)}, bf16[112,896]{1,0:T(8,128)(2,1)S(1)}, u32[]{:S(2)}, u32[]{:S(2)}) %collective-permute-start.24) | collective-permute-done | bytes 200736 | tf_op jit(solution)/shard_map/ppermute | solution.py:40
  79.6 2.7 %collective-permute-start.22 = (bf16[112,896]{1,0:T(8,128)(2,1)S(1)}, bf16[112,896]{1,0:T(8,128)(2,1)S(1)}, u32[]{:S(2)}, u32[]{:S(2)}) collective-permute-start(bf16[112,896]{1,0:T(8,128)(2,1)S(1)} %collective-permute-done.21.refs_1_), channel_id=1, source_target_pairs={{4,0},{8,4},{12,8},{16,12},{20,16},{24,20},{28,24},{0,28},{5,1},{9... | collective-permute-start | bytes 602120 | tf_op jit(solution)/shard_map/ppermute | solution.py:40
  82.3 4.8 %collective-permute-done.25.refs_5_ = bf16[112,896]{1,0:T(8,128)(2,1)S(1)} collective-permute-done((bf16[112,896]{1,0:T(8,128)(2,1)S(1)}, bf16[112,896]{1,0:T(8,128)(2,1)S(1)}, u32[]{:S(2)}, u32[]{:S(2)}) %collective-permute-start.25) | collective-permute-done | bytes 200736 | tf_op jit(solution)/shard_map/ppermute | solution.py:40
  87.0 2.7 %collective-permute-start.23 = (bf16[112,896]{1,0:T(8,128)(2,1)S(1)}, bf16[112,896]{1,0:T(8,128)(2,1)S(1)}, u32[]{:S(2)}, u32[]{:S(2)}) collective-permute-start(bf16[112,896]{1,0:T(8,128)(2,1)S(1)} %collective-permute-done.22.refs_2_), channel_id=1, source_target_pairs={{4,0},{8,4},{12,8},{16,12},{20,16},{24,20},{28,24},{0,28},{5,1},{9... | collective-permute-start | bytes 602120 | tf_op jit(solution)/shard_map/ppermute | solution.py:40
  89.7 3.9 %collective-permute-done.26.refs_4_ = bf16[112,896]{1,0:T(8,128)(2,1)S(1)} collective-permute-done((bf16[112,896]{1,0:T(8,128)(2,1)S(1)}, bf16[112,896]{1,0:T(8,128)(2,1)S(1)}, u32[]{:S(2)}, u32[]{:S(2)}) %collective-permute-start.26) | collective-permute-done | bytes 200736 | tf_op jit(solution)/shard_map/ppermute | solution.py:40
  93.6 0.6 shard_map.24.group
  94.3 9.0 %collective-permute-start.27 = (bf16[7,112,896]{2,1,0:T(8,128)(2,1)S(1)}, bf16[7,112,896]{2,1,0:T(8,128)(2,1)S(1)}, u32[]{:S(2)}, u32[]{:S(2)}) collective-permute-start(bf16[7,112,896]{2,1,0:T(8,128)(2,1)S(1)} %shard_map.24.group), channel_id=1, source_target_pairs={{1,0},{0,1},{3,2},{2,3},{5,4},{4,5},{7,6},{6,7},{9,8},{8,9},{11,10... | collective-permute-start | bytes 4214792 | tf_op jit(solution)/shard_map/ppermute | solution.py:40
  103.3 2.7 %collective-permute-start.3 = (bf16[504,512]{1,0:T(8,128)(2,1)S(1)}, bf16[504,512]{1,0:T(8,128)(2,1)S(1)}, u32[]{:S(2)}, u32[]{:S(2)}) collective-permute-start(bf16[504,512]{1,0:T(8,128)(2,1)S(1)} %collective-permute-done.2.refs_3_), channel_id=1, source_target_pairs={{64,0},{128,64},{192,128},{0,192},{65,1},{129,65},{193,129},{1,193... | collective-permute-start | bytes 1548296 | tf_op jit(solution)/shard_map/ppermute | solution.py:40
  106.0 1.3 collective-permute-start.7
  107.3 3.0 %collective-permute-start.28 = (bf16[56,896]{1,0:T(8,128)(2,1)S(1)}, bf16[56,896]{1,0:T(8,128)(2,1)S(1)}, u32[]{:S(2)}, u32[]{:S(2)}) collective-permute-start(bf16[56,896]{1,0:T(8,128)(2,1)S(1)} %slice.40), channel_id=1, source_target_pairs={{4,0},{8,4},{12,8},{16,12},{20,16},{24,20},{28,24},{0,28},{5,1},{9... | collective-permute-start | bytes 301064 | tf_op jit(solution)/shard_map/ppermute | solution.py:40
  110.3 1.6 collective-permute-done.28
  112.0 5.6 %collective-permute-done.29 = bf16[56,896]{1,0:T(8,128)(2,1)S(1)} collective-permute-done((bf16[56,896]{1,0:T(8,128)(2,1)S(1)}, bf16[56,896]{1,0:T(8,128)(2,1)S(1)}, u32[]{:S(2)}, u32[]{:S(2)}) %collective-permute-start.29) | collective-permute-done | bytes 100384 | tf_op jit(solution)/shard_map/ppermute | solution.py:40
  117.6 2.4 %collective-permute-start.30 = (bf16[112,896]{1,0:T(8,128)(2,1)S(1)}, bf16[112,896]{1,0:T(8,128)(2,1)S(1)}, u32[]{:S(2)}, u32[]{:S(2)}) collective-permute-start(bf16[112,896]{1,0:T(8,128)(2,1)S(1)} %constant_dynamic-update-slice_fusion.mine), channel_id=1, source_target_pairs={{1,0},{0,1},{3,2},{2,3},{5,4},{4,5},{7,6},{6,7},{9,8},{8,9},{11,10... | collective-permute-start | bytes 602120 | tf_op jit(solution)/shard_map/ppermute | solution.py:40
  120.1 1.5 shard_map.19.panel
  121.6 2.5 %shard_map.25 = (bf16[4,448,896]{2,1,0:T(8,128)(2,1)S(1)}, f32[448,576]{1,0:T(8,128)S(1)}) custom-call(s32[2]{0:T(128)S(1)} %pad_add_fusion.place, bf16[4,896,576]{2,1,0:T(8,128)(2,1)S(1)} %shard_map.19.panel, bf16[7,112,896]{2,1,0:T(8,128)(2,1)S(1)} %shard_map.24.group), custom_call_target="tpu_custom_call" | custom-call | flops 924844032 | bytes 9261056 | tf_op jit(solution)/shard_map/pallas_call | solution.py:62
  124.1 2.5 %shard_map.26 = (bf16[4,448,896]{2,1,0:T(8,128)(2,1)S(1)}, f32[448,576]{1,0:T(8,128)S(1)}) custom-call(s32[2]{0:T(128)S(1)} %pad_add_fusion.place, bf16[4,896,576]{2,1,0:T(8,128)(2,1)S(1)} %shard_map.19.panel, bf16[7,112,896]{2,1,0:T(8,128)(2,1)S(1)} %collective-permute-done.27.group, ...), custom_call_target="tpu_custom_call", output_to_operand_aliasing={{0}: (3, {}), {1}: (4, {})} | custom-call | flops 924844032 | bytes 12988416 | tf_op jit(solution)/shard_map/pallas_call | solution.py:62
  126.6 2.5 %shard_map.27 = (bf16[4,448,896]{2,1,0:T(8,128)(2,1)S(1)}, bf16[504,512]{1,0:T(8,128)(2,1)S(1)}, bf16[448,576]{1,0:T(8,128)(2,1)S(1)}) custom-call(s32[2]{0:T(128)S(1)} %pad_add_fusion.place, bf16[448,576]{1,0:T(8,128)(2,1)S(1)} %get-tuple-element.40.own, bf16[4,896,576]{2,1,0:T(8,128)(2,1)S(1)} %shard_map.19.panel, ...), custom_call_target="tpu_custom_call", output_to_operand_aliasing={{0}: (3, {})} | custom-call | flops 231211008 | bytes 13017088 | tf_op jit(solution)/shard_map/pallas_call | solution.py:62
  129.1 0.4 collective-permute-start.33
  129.5 2.7 %collective-permute-start.31 = (bf16[504,512]{1,0:T(8,128)(2,1)S(1)}, bf16[504,512]{1,0:T(8,128)(2,1)S(1)}, u32[]{:S(2)}, u32[]{:S(2)}) collective-permute-start(bf16[504,512]{1,0:T(8,128)(2,1)S(1)} %get-tuple-element.68.refs_0_), channel_id=1, source_target_pairs={{64,0},{128,64},{192,128},{0,192},{65,1},{129,65},{193,129},{1,193... | collective-permute-start | bytes 1548296 | tf_op jit(solution)/shard_map/ppermute | solution.py:40
  132.2 10.2 %collective-permute-done.33.refs_3_ = bf16[504,512]{1,0:T(8,128)(2,1)S(1)} collective-permute-done((bf16[504,512]{1,0:T(8,128)(2,1)S(1)}, bf16[504,512]{1,0:T(8,128)(2,1)S(1)}, u32[]{:S(2)}, u32[]{:S(2)}) %collective-permute-start.33) | collective-permute-done | bytes 516128 | tf_op jit(solution)/shard_map/ppermute | solution.py:40
  142.3 0.4 collective-permute-done.32.refs_2_
  142.7 2.4 %collective-permute-start.35 = (bf16[504,512]{1,0:T(8,128)(2,1)S(1)}, bf16[504,512]{1,0:T(8,128)(2,1)S(1)}, u32[]{:S(2)}, u32[]{:S(2)}) collective-permute-start(bf16[504,512]{1,0:T(8,128)(2,1)S(1)} %collective-permute-done.33.refs_3_), channel_id=1, source_target_pairs={{64,0},{128,64},{192,128},{0,192},{65,1},{129,65},{193,129},{1,193... | collective-permute-start | bytes 1548296 | tf_op jit(solution)/shard_map/ppermute | solution.py:40
  145.1 2.0 %collective-permute-start.36 = (bf16[504,512]{1,0:T(8,128)(2,1)S(1)}, bf16[504,512]{1,0:T(8,128)(2,1)S(1)}, u32[]{:S(2)}, u32[]{:S(2)}) collective-permute-start(bf16[504,512]{1,0:T(8,128)(2,1)S(1)} %collective-permute-done.32.refs_2_), channel_id=1, source_target_pairs={{32,0},{0,32},{33,1},{1,33},{34,2},{2,34},{35,3},{3,35},{36,4},{4,... | collective-permute-start | bytes 1548296 | tf_op jit(solution)/shard_map/ppermute | solution.py:40
  147.1 6.7 %collective-permute-done.35.refs_4_ = bf16[504,512]{1,0:T(8,128)(2,1)S(1)} collective-permute-done((bf16[504,512]{1,0:T(8,128)(2,1)S(1)}, bf16[504,512]{1,0:T(8,128)(2,1)S(1)}, u32[]{:S(2)}, u32[]{:S(2)}) %collective-permute-start.35) | collective-permute-done | bytes 516128 | tf_op jit(solution)/shard_map/ppermute | solution.py:40
  153.8 3.0 %collective-permute-done.36.refs_5_ = bf16[504,512]{1,0:T(8,128)(2,1)S(1)} collective-permute-done((bf16[504,512]{1,0:T(8,128)(2,1)S(1)}, bf16[504,512]{1,0:T(8,128)(2,1)S(1)}, u32[]{:S(2)}, u32[]{:S(2)}) %collective-permute-start.36) | collective-permute-done | bytes 516128 | tf_op jit(solution)/shard_map/ppermute | solution.py:40
  156.8 2.7 %collective-permute-done.34.refs_6_ = bf16[504,512]{1,0:T(8,128)(2,1)S(1)} collective-permute-done((bf16[504,512]{1,0:T(8,128)(2,1)S(1)}, bf16[504,512]{1,0:T(8,128)(2,1)S(1)}, u32[]{:S(2)}, u32[]{:S(2)}) %collective-permute-start.34) | collective-permute-done | bytes 516128 | tf_op jit(solution)/shard_map/ppermute | solution.py:40
  159.6 1.5 collective-permute-start.38
  161.2 6.1 %shard_map.28.before = f32[448,576]{1,0:T(8,128)S(1)} custom-call(s32[2]{0:T(128)S(1)} %pad_add_fusion.place, bf16[448,576]{1,0:T(8,128)(2,1)S(1)} %get-tuple-element.40.own, bf16[448,576]{1,0:T(8,128)(2,1)S(1)} %get-tuple-element.66.w_low, bf16[4,448,896]{2,1,0:T(8,128)(2,1)S(1)} %get-tuple-element.67.gram, bf16[504,512]{1,0:T(8,128)(2,1)S(1)} %get-tuple-element.68.refs_0_, ...), custom_call_target="tpu_custom_call" | custom-call | flops 2312110080 | bytes 8372224 | tf_op jit(solution)/shard_map/pallas_call | solution.py:62
  167.3 1.9 %shard_map.29 = bf16[448,576]{1,0:T(8,128)(2,1)} custom-call(s32[2]{0:T(128)S(1)} %pad_add_fusion.place, f32[448,576]{1,0:T(8,128)S(1)} %shard_map.28.before, bf16[4,448,896]{2,1,0:T(8,128)(2,1)S(1)} %get-tuple-element.67.gram, bf16[256,512]{1,0:T(8,128)(2,1)S(1)} %collective-permute-done.37.refs_0_, bf16[248,512]{1,0:T(8,128)(2,1)S(1)} %collective-permute-done.38.refs_1_), custom_call_target="tpu_custom_call" | custom-call | flops 231211008 | bytes 4759552 | tf_op jit(solution)/shard_map/pallas_call | solution.py:62
  (49 shorter events, 0.7 us)
Async XLA Ops:
  0.1 1.1 copy-start
  1.8 12.5 %collective-permute-start.2 = (bf16[504,512]{1,0:T(8,128)(2,1)S(1)}, bf16[504,512]{1,0:T(8,128)(2,1)S(1)}, u32[]{:S(2)}, u32[]{:S(2)}) collective-permute-start(bf16[504,512]{1,0:T(8,128)(2,1)S(1)} %get-tuple-element.41.refs_0_), channel_id=1, source_target_pairs={{32,0},{0,32},{33,1},{1,33},{34,2},{2,34},{35,3},{3,35},{36,4},{4,... | collective-permute-start | bytes 1548296 | tf_op jit(solution)/shard_map/ppermute | solution.py:40
  4.0 13.3 %collective-permute-start.1 = (bf16[504,512]{1,0:T(8,128)(2,1)S(1)}, bf16[504,512]{1,0:T(8,128)(2,1)S(1)}, u32[]{:S(2)}, u32[]{:S(2)}) collective-permute-start(bf16[504,512]{1,0:T(8,128)(2,1)S(1)} %get-tuple-element.41.refs_0_), channel_id=1, source_target_pairs={{192,0},{0,64},{64,128},{128,192},{193,1},{1,65},{65,129},{129,193... | collective-permute-start | bytes 1548296 | tf_op jit(solution)/shard_map/ppermute | solution.py:40
  5.2 12.1 %collective-permute-start = (bf16[504,512]{1,0:T(8,128)(2,1)S(1)}, bf16[504,512]{1,0:T(8,128)(2,1)S(1)}, u32[]{:S(2)}, u32[]{:S(2)}) collective-permute-start(bf16[504,512]{1,0:T(8,128)(2,1)S(1)} %get-tuple-element.41.refs_0_), channel_id=1, source_target_pairs={{64,0},{128,64},{192,128},{0,192},{65,1},{129,65},{193,129},{1,193... | collective-permute-start | bytes 1548296 | tf_op jit(solution)/shard_map/ppermute | solution.py:40
  17.3 9.5 %collective-permute-start.5 = (bf16[256,512]{1,0:T(8,128)(2,1)S(1)}, bf16[256,512]{1,0:T(8,128)(2,1)S(1)}, u32[]{:S(2)}, u32[]{:S(2)}) collective-permute-start(bf16[256,512]{1,0:T(8,128)(2,1)S(1)} %slice.30), channel_id=1, source_target_pairs={{64,0},{128,64},{192,128},{0,192},{65,1},{129,65},{193,129},{1,193... | collective-permute-start | bytes 786440 | tf_op jit(solution)/shard_map/ppermute | solution.py:40
  19.8 7.0 %collective-permute-start.6 = (bf16[248,512]{1,0:T(8,128)(2,1)S(1)}, bf16[248,512]{1,0:T(8,128)(2,1)S(1)}, u32[]{:S(2)}, u32[]{:S(2)}) collective-permute-start(bf16[248,512]{1,0:T(8,128)(2,1)S(1)} %slice.31), channel_id=1, source_target_pairs={{192,0},{0,64},{64,128},{128,192},{193,1},{1,65},{65,129},{129,193... | collective-permute-start | bytes 761864 | tf_op jit(solution)/shard_map/ppermute | solution.py:40
  24.1 8.4 %collective-permute-start.8 = (bf16[8,56,896]{2,1,0:T(8,128)(2,1)S(1)}, bf16[8,56,896]{2,1,0:T(8,128)(2,1)S(1)}, u32[]{:S(2)}, u32[]{:S(2)}) collective-permute-start(bf16[8,56,896]{2,1,0:T(8,128)(2,1)S(1)} %get-tuple-element.47), channel_id=1, source_target_pairs={{1,0},{0,1},{3,2},{2,3},{5,4},{4,5},{7,6},{6,7},{9,8},{8,9},{11,10... | collective-permute-start | bytes 2408456 | tf_op jit(solution)/shard_map/ppermute | solution.py:40
  29.2 5.2 %collective-permute-start.9 = (bf16[8,56,896]{2,1,0:T(8,128)(2,1)S(1)}, bf16[8,56,896]{2,1,0:T(8,128)(2,1)S(1)}, u32[]{:S(2)}, u32[]{:S(2)}) collective-permute-start(bf16[8,56,896]{2,1,0:T(8,128)(2,1)S(1)} %get-tuple-element.50), channel_id=1, source_target_pairs={{1,0},{0,1},{3,2},{2,3},{5,4},{4,5},{7,6},{6,7},{9,8},{8,9},{11,10... | collective-permute-start | bytes 2408456 | tf_op jit(solution)/shard_map/ppermute | solution.py:40
  35.4 7.5 %collective-permute-start.14 = (bf16[56,896]{1,0:T(8,128)(2,1)S(1)}, bf16[56,896]{1,0:T(8,128)(2,1)S(1)}, u32[]{:S(2)}, u32[]{:S(2)}) collective-permute-start(bf16[56,896]{1,0:T(8,128)(2,1)S(1)} %get-tuple-element.59), channel_id=1, source_target_pairs={{4,0},{8,4},{12,8},{16,12},{20,16},{24,20},{28,24},{0,28},{5,1},{9... | collective-permute-start | bytes 301064 | tf_op jit(solution)/shard_map/ppermute | solution.py:40
  41.1 5.3 %collective-permute-start.10 = (bf16[56,896]{1,0:T(8,128)(2,1)S(1)}, bf16[56,896]{1,0:T(8,128)(2,1)S(1)}, u32[]{:S(2)}, u32[]{:S(2)}) collective-permute-start(bf16[56,896]{1,0:T(8,128)(2,1)S(1)} %get-tuple-element.55), channel_id=1, source_target_pairs={{28,0},{0,4},{4,8},{8,12},{12,16},{16,20},{20,24},{24,28},{29,1},{... | collective-permute-start | bytes 301064 | tf_op jit(solution)/shard_map/ppermute | solution.py:40
  42.9 6.6 %collective-permute-start.15 = (bf16[112,896]{1,0:T(8,128)(2,1)S(1)}, bf16[112,896]{1,0:T(8,128)(2,1)S(1)}, u32[]{:S(2)}, u32[]{:S(2)}) collective-permute-start(bf16[112,896]{1,0:T(8,128)(2,1)S(1)} %pad_maximum_fusion.2), channel_id=1, source_target_pairs={{4,0},{8,4},{12,8},{16,12},{20,16},{24,20},{28,24},{0,28},{5,1},{9... | collective-permute-start | bytes 602120 | tf_op jit(solution)/shard_map/ppermute | solution.py:40
  46.5 6.6 %collective-permute-start.11 = (bf16[112,896]{1,0:T(8,128)(2,1)S(1)}, bf16[112,896]{1,0:T(8,128)(2,1)S(1)}, u32[]{:S(2)}, u32[]{:S(2)}) collective-permute-start(bf16[112,896]{1,0:T(8,128)(2,1)S(1)} %pad_maximum_fusion.1), channel_id=1, source_target_pairs={{28,0},{0,4},{4,8},{8,12},{12,16},{16,20},{20,24},{24,28},{29,1},{... | collective-permute-start | bytes 602120 | tf_op jit(solution)/shard_map/ppermute | solution.py:40
  49.6 6.1 %collective-permute-start.16 = (bf16[112,896]{1,0:T(8,128)(2,1)S(1)}, bf16[112,896]{1,0:T(8,128)(2,1)S(1)}, u32[]{:S(2)}, u32[]{:S(2)}) collective-permute-start(bf16[112,896]{1,0:T(8,128)(2,1)S(1)} %add_convert_fusion.1), channel_id=1, source_target_pairs={{4,0},{8,4},{12,8},{16,12},{20,16},{24,20},{28,24},{0,28},{5,1},{9... | collective-permute-start | bytes 602120 | tf_op jit(solution)/shard_map/ppermute | solution.py:40
  53.1 6.0 %collective-permute-start.12 = (bf16[112,896]{1,0:T(8,128)(2,1)S(1)}, bf16[112,896]{1,0:T(8,128)(2,1)S(1)}, u32[]{:S(2)}, u32[]{:S(2)}) collective-permute-start(bf16[112,896]{1,0:T(8,128)(2,1)S(1)} %add_convert_fusion.3), channel_id=1, source_target_pairs={{28,0},{0,4},{4,8},{8,12},{12,16},{16,20},{20,24},{24,28},{29,1},{... | collective-permute-start | bytes 602120 | tf_op jit(solution)/shard_map/ppermute | solution.py:40
  55.8 5.9 %collective-permute-start.17 = (bf16[112,896]{1,0:T(8,128)(2,1)S(1)}, bf16[112,896]{1,0:T(8,128)(2,1)S(1)}, u32[]{:S(2)}, u32[]{:S(2)}) collective-permute-start(bf16[112,896]{1,0:T(8,128)(2,1)S(1)} %add_convert_fusion), channel_id=1, source_target_pairs={{4,0},{8,4},{12,8},{16,12},{20,16},{24,20},{28,24},{0,28},{5,1},{9... | collective-permute-start | bytes 602120 | tf_op jit(solution)/shard_map/ppermute | solution.py:40
  59.2 5.9 %collective-permute-start.13 = (bf16[112,896]{1,0:T(8,128)(2,1)S(1)}, bf16[112,896]{1,0:T(8,128)(2,1)S(1)}, u32[]{:S(2)}, u32[]{:S(2)}) collective-permute-start(bf16[112,896]{1,0:T(8,128)(2,1)S(1)} %add_convert_fusion.2), channel_id=1, source_target_pairs={{28,0},{0,4},{4,8},{8,12},{12,16},{16,20},{20,24},{24,28},{29,1},{... | collective-permute-start | bytes 602120 | tf_op jit(solution)/shard_map/ppermute | solution.py:40
  65.7 7.4 %collective-permute-start.18 = (bf16[112,896]{1,0:T(8,128)(2,1)S(1)}, bf16[112,896]{1,0:T(8,128)(2,1)S(1)}, u32[]{:S(2)}, u32[]{:S(2)}) collective-permute-start(bf16[112,896]{1,0:T(8,128)(2,1)S(1)} %get-tuple-element.60.mine), channel_id=1, source_target_pairs={{2,0},{0,2},{3,1},{1,3},{6,4},{4,6},{7,5},{5,7},{10,8},{8,10},{11,... | collective-permute-start | bytes 602120 | tf_op jit(solution)/shard_map/ppermute | solution.py:40
  68.4 4.7 %collective-permute-start.20 = (bf16[56,896]{1,0:T(8,128)(2,1)S(1)}, bf16[56,896]{1,0:T(8,128)(2,1)S(1)}, u32[]{:S(2)}, u32[]{:S(2)}) collective-permute-start(bf16[56,896]{1,0:T(8,128)(2,1)S(1)} %get-tuple-element.61), channel_id=1, source_target_pairs={{34,0},{32,2},{2,32},{0,34},{35,1},{33,3},{3,33},{1,35},{38,4},{36... | collective-permute-start | bytes 301064 | tf_op jit(solution)/shard_map/ppermute | solution.py:53
  68.4 4.7 %collective-permute-start.19 = (bf16[56,896]{1,0:T(8,128)(2,1)S(1)}, bf16[56,896]{1,0:T(8,128)(2,1)S(1)}, u32[]{:S(2)}, u32[]{:S(2)}) collective-permute-start(bf16[56,896]{1,0:T(8,128)(2,1)S(1)} %get-tuple-element.61), channel_id=1, source_target_pairs={{32,0},{0,32},{33,1},{1,33},{34,2},{2,34},{35,3},{3,35},{36,4},{4,... | collective-permute-start | bytes 301064 | tf_op jit(solution)/shard_map/ppermute | solution.py:40
  73.7 5.9 %collective-permute-start.24 = (bf16[112,896]{1,0:T(8,128)(2,1)S(1)}, bf16[112,896]{1,0:T(8,128)(2,1)S(1)}, u32[]{:S(2)}, u32[]{:S(2)}) collective-permute-start(bf16[112,896]{1,0:T(8,128)(2,1)S(1)} %shard_map.23.refs_0_), channel_id=1, source_target_pairs={{28,0},{0,4},{4,8},{8,12},{12,16},{16,20},{20,24},{24,28},{29,1},{... | collective-permute-start | bytes 602120 | tf_op jit(solution)/shard_map/ppermute | solution.py:40
  73.8 5.8 %collective-permute-start.21 = (bf16[112,896]{1,0:T(8,128)(2,1)S(1)}, bf16[112,896]{1,0:T(8,128)(2,1)S(1)}, u32[]{:S(2)}, u32[]{:S(2)}) collective-permute-start(bf16[112,896]{1,0:T(8,128)(2,1)S(1)} %shard_map.23.refs_0_), channel_id=1, source_target_pairs={{4,0},{8,4},{12,8},{16,12},{20,16},{24,20},{28,24},{0,28},{5,1},{9... | collective-permute-start | bytes 602120 | tf_op jit(solution)/shard_map/ppermute | solution.py:40
  79.6 7.4 %collective-permute-start.25 = (bf16[112,896]{1,0:T(8,128)(2,1)S(1)}, bf16[112,896]{1,0:T(8,128)(2,1)S(1)}, u32[]{:S(2)}, u32[]{:S(2)}) collective-permute-start(bf16[112,896]{1,0:T(8,128)(2,1)S(1)} %collective-permute-done.24.refs_6_), channel_id=1, source_target_pairs={{28,0},{0,4},{4,8},{8,12},{12,16},{16,20},{20,24},{24,28},{29,1},{... | collective-permute-start | bytes 602120 | tf_op jit(solution)/shard_map/ppermute | solution.py:40
  79.6 7.4 %collective-permute-start.22 = (bf16[112,896]{1,0:T(8,128)(2,1)S(1)}, bf16[112,896]{1,0:T(8,128)(2,1)S(1)}, u32[]{:S(2)}, u32[]{:S(2)}) collective-permute-start(bf16[112,896]{1,0:T(8,128)(2,1)S(1)} %collective-permute-done.21.refs_1_), channel_id=1, source_target_pairs={{4,0},{8,4},{12,8},{16,12},{20,16},{24,20},{28,24},{0,28},{5,1},{9... | collective-permute-start | bytes 602120 | tf_op jit(solution)/shard_map/ppermute | solution.py:40
  87.0 6.6 %collective-permute-start.26 = (bf16[112,896]{1,0:T(8,128)(2,1)S(1)}, bf16[112,896]{1,0:T(8,128)(2,1)S(1)}, u32[]{:S(2)}, u32[]{:S(2)}) collective-permute-start(bf16[112,896]{1,0:T(8,128)(2,1)S(1)} %collective-permute-done.25.refs_5_), channel_id=1, source_target_pairs={{28,0},{0,4},{4,8},{8,12},{12,16},{16,20},{20,24},{24,28},{29,1},{... | collective-permute-start | bytes 602120 | tf_op jit(solution)/shard_map/ppermute | solution.py:40
  87.0 6.6 %collective-permute-start.23 = (bf16[112,896]{1,0:T(8,128)(2,1)S(1)}, bf16[112,896]{1,0:T(8,128)(2,1)S(1)}, u32[]{:S(2)}, u32[]{:S(2)}) collective-permute-start(bf16[112,896]{1,0:T(8,128)(2,1)S(1)} %collective-permute-done.22.refs_2_), channel_id=1, source_target_pairs={{4,0},{8,4},{12,8},{16,12},{20,16},{24,20},{28,24},{0,28},{5,1},{9... | collective-permute-start | bytes 602120 | tf_op jit(solution)/shard_map/ppermute | solution.py:40
  94.3 29.9 %collective-permute-start.27 = (bf16[7,112,896]{2,1,0:T(8,128)(2,1)S(1)}, bf16[7,112,896]{2,1,0:T(8,128)(2,1)S(1)}, u32[]{:S(2)}, u32[]{:S(2)}) collective-permute-start(bf16[7,112,896]{2,1,0:T(8,128)(2,1)S(1)} %shard_map.24.group), channel_id=1, source_target_pairs={{1,0},{0,1},{3,2},{2,3},{5,4},{4,5},{7,6},{6,7},{9,8},{8,9},{11,10... | collective-permute-start | bytes 4214792 | tf_op jit(solution)/shard_map/ppermute | solution.py:40
  103.3 16.8 %collective-permute-start.4 = (bf16[504,512]{1,0:T(8,128)(2,1)S(1)}, bf16[504,512]{1,0:T(8,128)(2,1)S(1)}, u32[]{:S(2)}, u32[]{:S(2)}) collective-permute-start(bf16[504,512]{1,0:T(8,128)(2,1)S(1)} %collective-permute-done.2.refs_3_), channel_id=1, source_target_pairs={{192,0},{0,64},{64,128},{128,192},{193,1},{1,65},{65,129},{129,193... | collective-permute-start | bytes 1548296 | tf_op jit(solution)/shard_map/ppermute | solution.py:40
  103.3 16.8 %collective-permute-start.3 = (bf16[504,512]{1,0:T(8,128)(2,1)S(1)}, bf16[504,512]{1,0:T(8,128)(2,1)S(1)}, u32[]{:S(2)}, u32[]{:S(2)}) collective-permute-start(bf16[504,512]{1,0:T(8,128)(2,1)S(1)} %collective-permute-done.2.refs_3_), channel_id=1, source_target_pairs={{64,0},{128,64},{192,128},{0,192},{65,1},{129,65},{193,129},{1,193... | collective-permute-start | bytes 1548296 | tf_op jit(solution)/shard_map/ppermute | solution.py:40
  106.0 14.1 %collective-permute-start.7 = (bf16[504,512]{1,0:T(8,128)(2,1)S(1)}, bf16[504,512]{1,0:T(8,128)(2,1)S(1)}, u32[]{:S(2)}, u32[]{:S(2)}) collective-permute-start(bf16[504,512]{1,0:T(8,128)(2,1)S(1)} %pad_maximum_fusion), channel_id=1, source_target_pairs={{32,0},{0,32},{33,1},{1,33},{34,2},{2,34},{35,3},{3,35},{36,4},{4,... | collective-permute-start | bytes 1548296 | tf_op jit(solution)/shard_map/ppermute | solution.py:40
  107.3 4.7 %collective-permute-start.28 = (bf16[56,896]{1,0:T(8,128)(2,1)S(1)}, bf16[56,896]{1,0:T(8,128)(2,1)S(1)}, u32[]{:S(2)}, u32[]{:S(2)}) collective-permute-start(bf16[56,896]{1,0:T(8,128)(2,1)S(1)} %slice.40), channel_id=1, source_target_pairs={{4,0},{8,4},{12,8},{16,12},{20,16},{24,20},{28,24},{0,28},{5,1},{9... | collective-permute-start | bytes 301064 | tf_op jit(solution)/shard_map/ppermute | solution.py:40
  112.0 5.7 %collective-permute-start.29 = (bf16[56,896]{1,0:T(8,128)(2,1)S(1)}, bf16[56,896]{1,0:T(8,128)(2,1)S(1)}, u32[]{:S(2)}, u32[]{:S(2)}) collective-permute-start(bf16[56,896]{1,0:T(8,128)(2,1)S(1)} %slice.41), channel_id=1, source_target_pairs={{28,0},{0,4},{4,8},{8,12},{12,16},{16,20},{20,24},{24,28},{29,1},{... | collective-permute-start | bytes 301064 | tf_op jit(solution)/shard_map/ppermute | solution.py:40
  117.6 9.0 %collective-permute-start.30 = (bf16[112,896]{1,0:T(8,128)(2,1)S(1)}, bf16[112,896]{1,0:T(8,128)(2,1)S(1)}, u32[]{:S(2)}, u32[]{:S(2)}) collective-permute-start(bf16[112,896]{1,0:T(8,128)(2,1)S(1)} %constant_dynamic-update-slice_fusion.mine), channel_id=1, source_target_pairs={{1,0},{0,1},{3,2},{2,3},{5,4},{4,5},{7,6},{6,7},{9,8},{8,9},{11,10... | collective-permute-start | bytes 602120 | tf_op jit(solution)/shard_map/ppermute | solution.py:40
  129.1 13.2 %collective-permute-start.33 = (bf16[504,512]{1,0:T(8,128)(2,1)S(1)}, bf16[504,512]{1,0:T(8,128)(2,1)S(1)}, u32[]{:S(2)}, u32[]{:S(2)}) collective-permute-start(bf16[504,512]{1,0:T(8,128)(2,1)S(1)} %get-tuple-element.68.refs_0_), channel_id=1, source_target_pairs={{32,0},{0,32},{33,1},{1,33},{34,2},{2,34},{35,3},{3,35},{36,4},{4,... | collective-permute-start | bytes 1548296 | tf_op jit(solution)/shard_map/ppermute | solution.py:40
  129.5 13.2 %collective-permute-start.32 = (bf16[504,512]{1,0:T(8,128)(2,1)S(1)}, bf16[504,512]{1,0:T(8,128)(2,1)S(1)}, u32[]{:S(2)}, u32[]{:S(2)}) collective-permute-start(bf16[504,512]{1,0:T(8,128)(2,1)S(1)} %get-tuple-element.68.refs_0_), channel_id=1, source_target_pairs={{192,0},{0,64},{64,128},{128,192},{193,1},{1,65},{65,129},{129,193... | collective-permute-start | bytes 1548296 | tf_op jit(solution)/shard_map/ppermute | solution.py:40
  129.5 13.2 %collective-permute-start.31 = (bf16[504,512]{1,0:T(8,128)(2,1)S(1)}, bf16[504,512]{1,0:T(8,128)(2,1)S(1)}, u32[]{:S(2)}, u32[]{:S(2)}) collective-permute-start(bf16[504,512]{1,0:T(8,128)(2,1)S(1)} %get-tuple-element.68.refs_0_), channel_id=1, source_target_pairs={{64,0},{128,64},{192,128},{0,192},{65,1},{129,65},{193,129},{1,193... | collective-permute-start | bytes 1548296 | tf_op jit(solution)/shard_map/ppermute | solution.py:40
  142.7 11.1 %collective-permute-start.35 = (bf16[504,512]{1,0:T(8,128)(2,1)S(1)}, bf16[504,512]{1,0:T(8,128)(2,1)S(1)}, u32[]{:S(2)}, u32[]{:S(2)}) collective-permute-start(bf16[504,512]{1,0:T(8,128)(2,1)S(1)} %collective-permute-done.33.refs_3_), channel_id=1, source_target_pairs={{64,0},{128,64},{192,128},{0,192},{65,1},{129,65},{193,129},{1,193... | collective-permute-start | bytes 1548296 | tf_op jit(solution)/shard_map/ppermute | solution.py:40
  145.1 11.7 %collective-permute-start.36 = (bf16[504,512]{1,0:T(8,128)(2,1)S(1)}, bf16[504,512]{1,0:T(8,128)(2,1)S(1)}, u32[]{:S(2)}, u32[]{:S(2)}) collective-permute-start(bf16[504,512]{1,0:T(8,128)(2,1)S(1)} %collective-permute-done.32.refs_2_), channel_id=1, source_target_pairs={{32,0},{0,32},{33,1},{1,33},{34,2},{2,34},{35,3},{3,35},{36,4},{4,... | collective-permute-start | bytes 1548296 | tf_op jit(solution)/shard_map/ppermute | solution.py:40
  147.1 12.4 %collective-permute-start.34 = (bf16[504,512]{1,0:T(8,128)(2,1)S(1)}, bf16[504,512]{1,0:T(8,128)(2,1)S(1)}, u32[]{:S(2)}, u32[]{:S(2)}) collective-permute-start(bf16[504,512]{1,0:T(8,128)(2,1)S(1)} %collective-permute-done.32.refs_2_), channel_id=1, source_target_pairs={{192,0},{0,64},{64,128},{128,192},{193,1},{1,65},{65,129},{129,193... | collective-permute-start | bytes 1548296 | tf_op jit(solution)/shard_map/ppermute | solution.py:40
  159.5 7.7 %collective-permute-start.37 = (bf16[256,512]{1,0:T(8,128)(2,1)S(1)}, bf16[256,512]{1,0:T(8,128)(2,1)S(1)}, u32[]{:S(2)}, u32[]{:S(2)}) collective-permute-start(bf16[256,512]{1,0:T(8,128)(2,1)S(1)} %slice.38), channel_id=1, source_target_pairs={{64,0},{128,64},{192,128},{0,192},{65,1},{129,65},{193,129},{1,193... | collective-permute-start | bytes 786440 | tf_op jit(solution)/shard_map/ppermute | solution.py:40
  159.6 7.6 %collective-permute-start.38 = (bf16[248,512]{1,0:T(8,128)(2,1)S(1)}, bf16[248,512]{1,0:T(8,128)(2,1)S(1)}, u32[]{:S(2)}, u32[]{:S(2)}) collective-permute-start(bf16[248,512]{1,0:T(8,128)(2,1)S(1)} %slice.39), channel_id=1, source_target_pairs={{192,0},{0,64},{64,128},{128,192},{193,1},{1,65},{65,129},{129,193... | collective-permute-start | bytes 761864 | tf_op jit(solution)/shard_map/ppermute | solution.py:40

commit v2 on v1

--- a/solution.py
+++ b/solution.py
@@ -299,19 +299,28 @@
 
 
 def near_body(place, own, w_low, gram, *refs):
-    *blocks, r20, total, panel = refs
+    *blocks, total, panel = refs
     rows = own.shape[0]
     fill(panel, blocks)
-    fill(panel, [r20], 9)
-    panel[3, :rows] = w_low[...]
-    panel[3, rows:] = jnp.zeros((rows, own.shape[1]), BF16)
-    panel[4, :rows] = jnp.zeros((rows, own.shape[1]), BF16)
+    panel[2, :rows] = w_low[...]
+    panel[2, rows:] = jnp.zeros((rows, own.shape[1]), BF16)
     total[...] = coef_a * own[...].astype(F32)
 
-    @pl.loop(0, 5)
-    def _(i):
-        side = jnp.where(i == 3, 0, jnp.minimum(i, 3))
-        total[...] += jnp.dot(gram[side], panel[i], preferred_element_type=F32)
+    @pl.loop(0, 3)
+    def _(i):
+        total[...] += jnp.dot(gram[jnp.where(i == 2, 0, i)], panel[i], preferred_element_type=F32)
+
+
+def side_body(place, before, gram, r11, r31, r20, total, panel):
+    rows = total.shape[0]
+    fill(panel, [r11, r31])
+    fill(panel, [r20], 3)
+    panel[1, :rows] = jnp.zeros((rows, total.shape[1]), BF16)
+    total[...] = before[...]
+
+    @pl.loop(0, 2)
+    def _(i):
+        total[...] += jnp.dot(gram[i + 2], panel[i], preferred_element_type=F32)
 
 
 def far_body(place, before, gram, *refs):
@@ -396,9 +405,12 @@
 
     near = near_blocks(w_high)
     _, r30, r01 = near
-    r20, r11, r31 = lax.optimization_barrier((shift(r30, "x", -1), shift(r01, "x", 1), shift(r30, "yl", 1)))
-    blocks = (own, w_low, gram, w_high, *near, r11, r31, r20)
-    total = call(near_body, place, blocks, sums, 5 * work, [room(5)])
+    r20 = shift(r30, "x", -1)
+    r11 = shift(r01, "x", 1)
+    r31 = shift(r30, "yl", 1)
+    r20, r11, r31 = lax.optimization_barrier((r20, r11, r31))
+    total = call(near_body, place, (own, w_low, gram, w_high, *near), sums, 3 * work, [room(3)])
+    total = call(side_body, place, (total, gram, r11, r31, r20), sums, 2 * work, [room(2)])
     r21 = halves_of(r11, r31)
     return call(far_body, place, (total, gram, *r21), block, work // 2, [room(1)], home=True)
 

time: 170 us -> 171 us (level)
    pallas_call x13 -> x14, Pallas kernels: 27 us -> 27.6 us  [call(): pl.pallas_call(body, out_shape=outs if home else [pltpu.VMEM(o.shape, o.d...]
  transfers between devices with their start and end apart: 39 -> 39, of which waited for: 20 -> 20; matrix products, arithmetic and copies ran while one was open for 0% -> 0% of each run, Pallas kernels for 11% -> 12%
where the time goes in v2:
time: 171 us; the launch traced here: 170 us
  waiting for transfers between devices  72.2 us (42%)
  starting transfers between devices  68.1 us (40%)
  Pallas kernels  27.6 us (16%)
    ppermute x38, starting transfers between devices, shift(): lax.ppermute(value, axis, [((i + step) % size, i) for i in range(size)])  68.1 us
    ppermute x38, waiting for transfers between devices, shift(): lax.ppermute(value, axis, [((i + step) % size, i) for i in range(size)])  67.5 us
    pallas_call x14, Pallas kernels, call(): pl.pallas_call(body, out_shape=outs if home else [pltpu.VMEM(o.shape, o.d...  27.6 us
    ppermute x1, waiting for transfers between devices, fetch(): lax.ppermute(value, axes, [(flat(source(*p)), flat(p)) for p in places])  4.67 us
  transfers between devices with their start and end apart: 39, of which 20 were waited for; matrix products, arithmetic and copies ran while one was open for 0% of the time, Pallas kernels for 12%

profile of v2, /device:TPU:1, one launch (start us, length us, event | category | flops | bytes accessed | tf_op | source)
XLA Modules:
  0.0 169.8 jit_solution(5624299481462088679)
XLA Ops:
  0.1 1.1 copy-done
  1.1 0.6 shard_map.17
  1.8 2.2 %collective-permute-start.2 = (bf16[504,512]{1,0:T(8,128)(2,1)S(1)}, bf16[504,512]{1,0:T(8,128)(2,1)S(1)}, u32[]{:S(2)}, u32[]{:S(2)}) collective-permute-start(bf16[504,512]{1,0:T(8,128)(2,1)S(1)} %get-tuple-element.41.refs_0_), channel_id=1, source_target_pairs={{32,0},{0,32},{33,1},{1,33},{34,2},{2,34},{35,3},{3,35},{36,4},{4,... | collective-permute-start | bytes 1548296 | tf_op jit(solution)/shard_map/ppermute | solution.py:40
  4.0 1.2 collective-permute-start.1
  5.2 1.5 collective-permute-start
  6.7 7.6 %collective-permute-done.2.refs_3_ = bf16[504,512]{1,0:T(8,128)(2,1)S(1)} collective-permute-done((bf16[504,512]{1,0:T(8,128)(2,1)S(1)}, bf16[504,512]{1,0:T(8,128)(2,1)S(1)}, u32[]{:S(2)}, u32[]{:S(2)}) %collective-permute-start.2) | collective-permute-done | bytes 516128 | tf_op jit(solution)/shard_map/ppermute | solution.py:40
  14.3 3.0 %collective-permute-done.1.refs_2_ = bf16[504,512]{1,0:T(8,128)(2,1)S(1)} collective-permute-done((bf16[504,512]{1,0:T(8,128)(2,1)S(1)}, bf16[504,512]{1,0:T(8,128)(2,1)S(1)}, u32[]{:S(2)}, u32[]{:S(2)}) %collective-permute-start.1) | collective-permute-done | bytes 516128 | tf_op jit(solution)/shard_map/ppermute | solution.py:40
  17.3 2.5 %collective-permute-start.5 = (bf16[256,512]{1,0:T(8,128)(2,1)S(1)}, bf16[256,512]{1,0:T(8,128)(2,1)S(1)}, u32[]{:S(2)}, u32[]{:S(2)}) collective-permute-start(bf16[256,512]{1,0:T(8,128)(2,1)S(1)} %slice.30), channel_id=1, source_target_pairs={{64,0},{128,64},{192,128},{0,192},{65,1},{129,65},{193,129},{1,193... | collective-permute-start | bytes 786440 | tf_op jit(solution)/shard_map/ppermute | solution.py:40
  19.9 4.2 %shard_map.18 = (bf16[8,56,896]{2,1,0:T(8,128)(2,1)S(1)}, bf16[8,56,896]{2,1,0:T(8,128)(2,1)S(1)}, bf16[3,896,576]{2,1,0:T(8,128)(2,1)S(1)}, f32[448,896]{1,0:T(8,128)S(1)}) custom-call(s32[2]{0:T(128)S(1)} %pad_add_fusion.place, bf16[448,576]{1,0:T(8,128)(2,1)S(1)} %get-tuple-element.40.own, bf16[504,512]{1,0:T(8,128)(2,1)S(1)} %get-tuple-element.41.refs_0_, ...), custom_call_target="tpu_custom_call" | custom-call | flops 1387266048 | bytes 8085504 | tf_op jit(solution)/shard_map/pallas_call | solution.py:62
  24.1 2.7 %collective-permute-start.8 = (bf16[8,56,896]{2,1,0:T(8,128)(2,1)S(1)}, bf16[8,56,896]{2,1,0:T(8,128)(2,1)S(1)}, u32[]{:S(2)}, u32[]{:S(2)}) collective-permute-start(bf16[8,56,896]{2,1,0:T(8,128)(2,1)S(1)} %get-tuple-element.47), channel_id=1, source_target_pairs={{1,0},{0,1},{3,2},{2,3},{5,4},{4,5},{7,6},{6,7},{9,8},{8,9},{11,10... | collective-permute-start | bytes 2408456 | tf_op jit(solution)/shard_map/ppermute | solution.py:40
  26.8 2.4 %shard_map.20 = (bf16[8,56,896]{2,1,0:T(8,128)(2,1)S(1)}, bf16[8,56,896]{2,1,0:T(8,128)(2,1)S(1)}) custom-call(s32[2]{0:T(128)S(1)} %pad_add_fusion.place, bf16[448,576]{1,0:T(8,128)(2,1)S(1)} %get-tuple-element.40.own, bf16[3,896,576]{2,1,0:T(8,128)(2,1)S(1)} %get-tuple-element.45.low, f32[448,896]{1,0:T(8,128)S(1)} %get-tuple-element.48.partner, ...), custom_call_target="tpu_custom_call" | custom-call | flops 462422016 | bytes 6537216 | tf_op jit(solution)/shard_map/pallas_call | solution.py:62
  29.2 3.3 %collective-permute-start.9 = (bf16[8,56,896]{2,1,0:T(8,128)(2,1)S(1)}, bf16[8,56,896]{2,1,0:T(8,128)(2,1)S(1)}, u32[]{:S(2)}, u32[]{:S(2)}) collective-permute-start(bf16[8,56,896]{2,1,0:T(8,128)(2,1)S(1)} %get-tuple-element.50), channel_id=1, source_target_pairs={{1,0},{0,1},{3,2},{2,3},{5,4},{4,5},{7,6},{6,7},{9,8},{8,9},{11,10... | collective-permute-start | bytes 2408456 | tf_op jit(solution)/shard_map/ppermute | solution.py:40
  32.5 1.9 %collective-permute-done.9.high_other = bf16[8,56,896]{2,1,0:T(8,128)(2,1)S(1)} collective-permute-done((bf16[8,56,896]{2,1,0:T(8,128)(2,1)S(1)}, bf16[8,56,896]{2,1,0:T(8,128)(2,1)S(1)}, u32[]{:S(2)}, u32[]{:S(2)}) %collective-permute-start.9) | collective-permute-done | bytes 802848 | tf_op jit(solution)/shard_map/ppermute | solution.py:40
  34.5 0.9 shard_map.21
  35.4 5.7 %collective-permute-start.14 = (bf16[56,896]{1,0:T(8,128)(2,1)S(1)}, bf16[56,896]{1,0:T(8,128)(2,1)S(1)}, u32[]{:S(2)}, u32[]{:S(2)}) collective-permute-start(bf16[56,896]{1,0:T(8,128)(2,1)S(1)} %get-tuple-element.59), channel_id=1, source_target_pairs={{4,0},{8,4},{12,8},{16,12},{20,16},{24,20},{28,24},{0,28},{5,1},{9... | collective-permute-start | bytes 301064 | tf_op jit(solution)/shard_map/ppermute | solution.py:40
  41.1 0.1 collective-permute-start.10
  41.2 1.7 %collective-permute-done.14 = bf16[56,896]{1,0:T(8,128)(2,1)S(1)} collective-permute-done((bf16[56,896]{1,0:T(8,128)(2,1)S(1)}, bf16[56,896]{1,0:T(8,128)(2,1)S(1)}, u32[]{:S(2)}, u32[]{:S(2)}) %collective-permute-start.14) | collective-permute-done | bytes 100384 | tf_op jit(solution)/shard_map/ppermute | solution.py:40
  42.9 3.5 %collective-permute-start.15 = (bf16[112,896]{1,0:T(8,128)(2,1)S(1)}, bf16[112,896]{1,0:T(8,128)(2,1)S(1)}, u32[]{:S(2)}, u32[]{:S(2)}) collective-permute-start(bf16[112,896]{1,0:T(8,128)(2,1)S(1)} %pad_maximum_fusion.2), channel_id=1, source_target_pairs={{4,0},{8,4},{12,8},{16,12},{20,16},{24,20},{28,24},{0,28},{5,1},{9... | collective-permute-start | bytes 602120 | tf_op jit(solution)/shard_map/ppermute | solution.py:40
  46.5 0.1 collective-permute-start.11
  46.6 3.0 %collective-permute-done.15 = bf16[112,896]{1,0:T(8,128)(2,1)S(1)} collective-permute-done((bf16[112,896]{1,0:T(8,128)(2,1)S(1)}, bf16[112,896]{1,0:T(8,128)(2,1)S(1)}, u32[]{:S(2)}, u32[]{:S(2)}) %collective-permute-start.15) | collective-permute-done | bytes 200736 | tf_op jit(solution)/shard_map/ppermute | solution.py:40
  49.6 3.5 %collective-permute-start.16 = (bf16[112,896]{1,0:T(8,128)(2,1)S(1)}, bf16[112,896]{1,0:T(8,128)(2,1)S(1)}, u32[]{:S(2)}, u32[]{:S(2)}) collective-permute-start(bf16[112,896]{1,0:T(8,128)(2,1)S(1)} %add_convert_fusion.1), channel_id=1, source_target_pairs={{4,0},{8,4},{12,8},{16,12},{20,16},{24,20},{28,24},{0,28},{5,1},{9... | collective-permute-start | bytes 602120 | tf_op jit(solution)/shard_map/ppermute | solution.py:40
  53.1 0.3 collective-permute-start.12
  53.4 2.3 %collective-permute-done.16 = bf16[112,896]{1,0:T(8,128)(2,1)S(1)} collective-permute-done((bf16[112,896]{1,0:T(8,128)(2,1)S(1)}, bf16[112,896]{1,0:T(8,128)(2,1)S(1)}, u32[]{:S(2)}, u32[]{:S(2)}) %collective-permute-start.16) | collective-permute-done | bytes 200736 | tf_op jit(solution)/shard_map/ppermute | solution.py:40
  55.8 3.2 %collective-permute-start.17 = (bf16[112,896]{1,0:T(8,128)(2,1)S(1)}, bf16[112,896]{1,0:T(8,128)(2,1)S(1)}, u32[]{:S(2)}, u32[]{:S(2)}) collective-permute-start(bf16[112,896]{1,0:T(8,128)(2,1)S(1)} %add_convert_fusion), channel_id=1, source_target_pairs={{4,0},{8,4},{12,8},{16,12},{20,16},{24,20},{28,24},{0,28},{5,1},{9... | collective-permute-start | bytes 602120 | tf_op jit(solution)/shard_map/ppermute | solution.py:40
  59.0 0.2 collective-permute-done.12
  59.2 0.1 collective-permute-start.13
  59.3 2.3 %collective-permute-done.17.down = bf16[112,896]{1,0:T(8,128)(2,1)S(1)} collective-permute-done((bf16[112,896]{1,0:T(8,128)(2,1)S(1)}, bf16[112,896]{1,0:T(8,128)(2,1)S(1)}, u32[]{:S(2)}, u32[]{:S(2)}) %collective-permute-start.17) | collective-permute-done | bytes 200736 | tf_op jit(solution)/shard_map/ppermute | solution.py:40
  61.6 3.4 %collective-permute-done.13.up = bf16[112,896]{1,0:T(8,128)(2,1)S(1)} collective-permute-done((bf16[112,896]{1,0:T(8,128)(2,1)S(1)}, bf16[112,896]{1,0:T(8,128)(2,1)S(1)}, u32[]{:S(2)}, u32[]{:S(2)}) %collective-permute-start.13) | collective-permute-done | bytes 200736 | tf_op jit(solution)/shard_map/ppermute | solution.py:40
  65.1 0.6 shard_map.22
  65.7 2.7 %collective-permute-start.18 = (bf16[112,896]{1,0:T(8,128)(2,1)S(1)}, bf16[112,896]{1,0:T(8,128)(2,1)S(1)}, u32[]{:S(2)}, u32[]{:S(2)}) collective-permute-start(bf16[112,896]{1,0:T(8,128)(2,1)S(1)} %get-tuple-element.60.mine), channel_id=1, source_target_pairs={{2,0},{0,2},{3,1},{1,3},{6,4},{4,6},{7,5},{5,7},{10,8},{8,10},{11,... | collective-permute-start | bytes 602120 | tf_op jit(solution)/shard_map/ppermute | solution.py:40
  68.4 4.7 %collective-permute-done.20.cross = bf16[56,896]{1,0:T(8,128)(2,1)S(1)} collective-permute-done((bf16[56,896]{1,0:T(8,128)(2,1)S(1)}, bf16[56,896]{1,0:T(8,128)(2,1)S(1)}, u32[]{:S(2)}, u32[]{:S(2)}) %collective-permute-start.20) | collective-permute-done | bytes 100384 | tf_op jit(solution)/shard_map/ppermute | solution.py:53
  73.1 0.6 shard_map.23.refs_0_
  73.7 0.1 collective-permute-start.24
  73.8 2.7 %collective-permute-start.21 = (bf16[112,896]{1,0:T(8,128)(2,1)S(1)}, bf16[112,896]{1,0:T(8,128)(2,1)S(1)}, u32[]{:S(2)}, u32[]{:S(2)}) collective-permute-start(bf16[112,896]{1,0:T(8,128)(2,1)S(1)} %shard_map.23.refs_0_), channel_id=1, source_target_pairs={{4,0},{8,4},{12,8},{16,12},{20,16},{24,20},{28,24},{0,28},{5,1},{9... | collective-permute-start | bytes 602120 | tf_op jit(solution)/shard_map/ppermute | solution.py:40
  76.5 3.1 %collective-permute-done.24.refs_6_ = bf16[112,896]{1,0:T(8,128)(2,1)S(1)} collective-permute-done((bf16[112,896]{1,0:T(8,128)(2,1)S(1)}, bf16[112,896]{1,0:T(8,128)(2,1)S(1)}, u32[]{:S(2)}, u32[]{:S(2)}) %collective-permute-start.24) | collective-permute-done | bytes 200736 | tf_op jit(solution)/shard_map/ppermute | solution.py:40
  79.6 2.7 %collective-permute-start.22 = (bf16[112,896]{1,0:T(8,128)(2,1)S(1)}, bf16[112,896]{1,0:T(8,128)(2,1)S(1)}, u32[]{:S(2)}, u32[]{:S(2)}) collective-permute-start(bf16[112,896]{1,0:T(8,128)(2,1)S(1)} %collective-permute-done.21.refs_1_), channel_id=1, source_target_pairs={{4,0},{8,4},{12,8},{16,12},{20,16},{24,20},{28,24},{0,28},{5,1},{9... | collective-permute-start | bytes 602120 | tf_op jit(solution)/shard_map/ppermute | solution.py:40
  82.3 4.8 %collective-permute-done.25.refs_5_ = bf16[112,896]{1,0:T(8,128)(2,1)S(1)} collective-permute-done((bf16[112,896]{1,0:T(8,128)(2,1)S(1)}, bf16[112,896]{1,0:T(8,128)(2,1)S(1)}, u32[]{:S(2)}, u32[]{:S(2)}) %collective-permute-start.25) | collective-permute-done | bytes 200736 | tf_op jit(solution)/shard_map/ppermute | solution.py:40
  87.0 2.7 %collective-permute-start.23 = (bf16[112,896]{1,0:T(8,128)(2,1)S(1)}, bf16[112,896]{1,0:T(8,128)(2,1)S(1)}, u32[]{:S(2)}, u32[]{:S(2)}) collective-permute-start(bf16[112,896]{1,0:T(8,128)(2,1)S(1)} %collective-permute-done.22.refs_2_), channel_id=1, source_target_pairs={{4,0},{8,4},{12,8},{16,12},{20,16},{24,20},{28,24},{0,28},{5,1},{9... | collective-permute-start | bytes 602120 | tf_op jit(solution)/shard_map/ppermute | solution.py:40
  89.7 3.9 %collective-permute-done.26.refs_4_ = bf16[112,896]{1,0:T(8,128)(2,1)S(1)} collective-permute-done((bf16[112,896]{1,0:T(8,128)(2,1)S(1)}, bf16[112,896]{1,0:T(8,128)(2,1)S(1)}, u32[]{:S(2)}, u32[]{:S(2)}) %collective-permute-start.26) | collective-permute-done | bytes 200736 | tf_op jit(solution)/shard_map/ppermute | solution.py:40
  93.6 0.6 shard_map.24.group
  94.3 9.0 %collective-permute-start.27 = (bf16[7,112,896]{2,1,0:T(8,128)(2,1)S(1)}, bf16[7,112,896]{2,1,0:T(8,128)(2,1)S(1)}, u32[]{:S(2)}, u32[]{:S(2)}) collective-permute-start(bf16[7,112,896]{2,1,0:T(8,128)(2,1)S(1)} %shard_map.24.group), channel_id=1, source_target_pairs={{1,0},{0,1},{3,2},{2,3},{5,4},{4,5},{7,6},{6,7},{9,8},{8,9},{11,10... | collective-permute-start | bytes 4214792 | tf_op jit(solution)/shard_map/ppermute | solution.py:40
  103.3 2.7 %collective-permute-start.3 = (bf16[504,512]{1,0:T(8,128)(2,1)S(1)}, bf16[504,512]{1,0:T(8,128)(2,1)S(1)}, u32[]{:S(2)}, u32[]{:S(2)}) collective-permute-start(bf16[504,512]{1,0:T(8,128)(2,1)S(1)} %collective-permute-done.2.refs_3_), channel_id=1, source_target_pairs={{64,0},{128,64},{192,128},{0,192},{65,1},{129,65},{193,129},{1,193... | collective-permute-start | bytes 1548296 | tf_op jit(solution)/shard_map/ppermute | solution.py:40
  106.0 1.3 collective-permute-start.7
  107.3 3.0 %collective-permute-start.28 = (bf16[56,896]{1,0:T(8,128)(2,1)S(1)}, bf16[56,896]{1,0:T(8,128)(2,1)S(1)}, u32[]{:S(2)}, u32[]{:S(2)}) collective-permute-start(bf16[56,896]{1,0:T(8,128)(2,1)S(1)} %slice.40), channel_id=1, source_target_pairs={{4,0},{8,4},{12,8},{16,12},{20,16},{24,20},{28,24},{0,28},{5,1},{9... | collective-permute-start | bytes 301064 | tf_op jit(solution)/shard_map/ppermute | solution.py:40
  110.3 1.6 collective-permute-done.28
  112.0 5.6 %collective-permute-done.29 = bf16[56,896]{1,0:T(8,128)(2,1)S(1)} collective-permute-done((bf16[56,896]{1,0:T(8,128)(2,1)S(1)}, bf16[56,896]{1,0:T(8,128)(2,1)S(1)}, u32[]{:S(2)}, u32[]{:S(2)}) %collective-permute-start.29) | collective-permute-done | bytes 100384 | tf_op jit(solution)/shard_map/ppermute | solution.py:40
  117.6 2.4 %collective-permute-start.30 = (bf16[112,896]{1,0:T(8,128)(2,1)S(1)}, bf16[112,896]{1,0:T(8,128)(2,1)S(1)}, u32[]{:S(2)}, u32[]{:S(2)}) collective-permute-start(bf16[112,896]{1,0:T(8,128)(2,1)S(1)} %constant_dynamic-update-slice_fusion.mine), channel_id=1, source_target_pairs={{1,0},{0,1},{3,2},{2,3},{5,4},{4,5},{7,6},{6,7},{9,8},{8,9},{11,10... | collective-permute-start | bytes 602120 | tf_op jit(solution)/shard_map/ppermute | solution.py:40
  120.1 1.5 shard_map.19.panel
  121.6 2.5 %shard_map.25 = (bf16[4,448,896]{2,1,0:T(8,128)(2,1)S(1)}, f32[448,576]{1,0:T(8,128)S(1)}) custom-call(s32[2]{0:T(128)S(1)} %pad_add_fusion.place, bf16[4,896,576]{2,1,0:T(8,128)(2,1)S(1)} %shard_map.19.panel, bf16[7,112,896]{2,1,0:T(8,128)(2,1)S(1)} %shard_map.24.group), custom_call_target="tpu_custom_call" | custom-call | flops 924844032 | bytes 9261056 | tf_op jit(solution)/shard_map/pallas_call | solution.py:62
  124.1 2.5 %shard_map.26 = (bf16[4,448,896]{2,1,0:T(8,128)(2,1)S(1)}, f32[448,576]{1,0:T(8,128)S(1)}) custom-call(s32[2]{0:T(128)S(1)} %pad_add_fusion.place, bf16[4,896,576]{2,1,0:T(8,128)(2,1)S(1)} %shard_map.19.panel, bf16[7,112,896]{2,1,0:T(8,128)(2,1)S(1)} %collective-permute-done.27.group, ...), custom_call_target="tpu_custom_call", output_to_operand_aliasing={{0}: (3, {}), {1}: (4, {})} | custom-call | flops 924844032 | bytes 12988416 | tf_op jit(solution)/shard_map/pallas_call | solution.py:62
  126.6 2.5 %shard_map.27 = (bf16[4,448,896]{2,1,0:T(8,128)(2,1)S(1)}, bf16[504,512]{1,0:T(8,128)(2,1)S(1)}, bf16[448,576]{1,0:T(8,128)(2,1)S(1)}) custom-call(s32[2]{0:T(128)S(1)} %pad_add_fusion.place, bf16[448,576]{1,0:T(8,128)(2,1)S(1)} %get-tuple-element.40.own, bf16[4,896,576]{2,1,0:T(8,128)(2,1)S(1)} %shard_map.19.panel, ...), custom_call_target="tpu_custom_call", output_to_operand_aliasing={{0}: (3, {})} | custom-call | flops 231211008 | bytes 13017088 | tf_op jit(solution)/shard_map/pallas_call | solution.py:62
  129.1 0.4 collective-permute-start.33
  129.5 2.7 %collective-permute-start.31 = (bf16[504,512]{1,0:T(8,128)(2,1)S(1)}, bf16[504,512]{1,0:T(8,128)(2,1)S(1)}, u32[]{:S(2)}, u32[]{:S(2)}) collective-permute-start(bf16[504,512]{1,0:T(8,128)(2,1)S(1)} %get-tuple-element.68.refs_0_), channel_id=1, source_target_pairs={{64,0},{128,64},{192,128},{0,192},{65,1},{129,65},{193,129},{1,193... | collective-permute-start | bytes 1548296 | tf_op jit(solution)/shard_map/ppermute | solution.py:40
  132.2 10.2 %collective-permute-done.33.refs_3_ = bf16[504,512]{1,0:T(8,128)(2,1)S(1)} collective-permute-done((bf16[504,512]{1,0:T(8,128)(2,1)S(1)}, bf16[504,512]{1,0:T(8,128)(2,1)S(1)}, u32[]{:S(2)}, u32[]{:S(2)}) %collective-permute-start.33) | collective-permute-done | bytes 516128 | tf_op jit(solution)/shard_map/ppermute | solution.py:40
  142.3 0.4 collective-permute-done.32.refs_2_
  142.7 2.4 %collective-permute-start.35 = (bf16[504,512]{1,0:T(8,128)(2,1)S(1)}, bf16[504,512]{1,0:T(8,128)(2,1)S(1)}, u32[]{:S(2)}, u32[]{:S(2)}) collective-permute-start(bf16[504,512]{1,0:T(8,128)(2,1)S(1)} %collective-permute-done.33.refs_3_), channel_id=1, source_target_pairs={{64,0},{128,64},{192,128},{0,192},{65,1},{129,65},{193,129},{1,193... | collective-permute-start | bytes 1548296 | tf_op jit(solution)/shard_map/ppermute | solution.py:40
  145.1 2.0 %collective-permute-start.36 = (bf16[504,512]{1,0:T(8,128)(2,1)S(1)}, bf16[504,512]{1,0:T(8,128)(2,1)S(1)}, u32[]{:S(2)}, u32[]{:S(2)}) collective-permute-start(bf16[504,512]{1,0:T(8,128)(2,1)S(1)} %collective-permute-done.32.refs_2_), channel_id=1, source_target_pairs={{32,0},{0,32},{33,1},{1,33},{34,2},{2,34},{35,3},{3,35},{36,4},{4,... | collective-permute-start | bytes 1548296 | tf_op jit(solution)/shard_map/ppermute | solution.py:40
  147.1 6.7 %collective-permute-done.35.r11 = bf16[504,512]{1,0:T(8,128)(2,1)S(1)} collective-permute-done((bf16[504,512]{1,0:T(8,128)(2,1)S(1)}, bf16[504,512]{1,0:T(8,128)(2,1)S(1)}, u32[]{:S(2)}, u32[]{:S(2)}) %collective-permute-start.35) | collective-permute-done | bytes 516128 | tf_op jit(solution)/shard_map/ppermute | solution.py:40
  153.8 3.0 %collective-permute-done.36.r31 = bf16[504,512]{1,0:T(8,128)(2,1)S(1)} collective-permute-done((bf16[504,512]{1,0:T(8,128)(2,1)S(1)}, bf16[504,512]{1,0:T(8,128)(2,1)S(1)}, u32[]{:S(2)}, u32[]{:S(2)}) %collective-permute-start.36) | collective-permute-done | bytes 516128 | tf_op jit(solution)/shard_map/ppermute | solution.py:40
  156.8 2.7 %collective-permute-done.34.r20 = bf16[504,512]{1,0:T(8,128)(2,1)S(1)} collective-permute-done((bf16[504,512]{1,0:T(8,128)(2,1)S(1)}, bf16[504,512]{1,0:T(8,128)(2,1)S(1)}, u32[]{:S(2)}, u32[]{:S(2)}) %collective-permute-start.34) | collective-permute-done | bytes 516128 | tf_op jit(solution)/shard_map/ppermute | solution.py:40
  159.6 1.5 collective-permute-start.38
  161.2 3.9 %shard_map.28.before = f32[448,576]{1,0:T(8,128)S(1)} custom-call(s32[2]{0:T(128)S(1)} %pad_add_fusion.place, bf16[448,576]{1,0:T(8,128)(2,1)S(1)} %get-tuple-element.40.own, bf16[448,576]{1,0:T(8,128)(2,1)S(1)} %get-tuple-element.66.w_low, bf16[4,448,896]{2,1,0:T(8,128)(2,1)S(1)} %get-tuple-element.67.gram, bf16[504,512]{1,0:T(8,128)(2,1)S(1)} %get-tuple-element.68.refs_0_, ...), custom_call_target="tpu_custom_call" | custom-call | flops 1387266048 | bytes 6823936 | tf_op jit(solution)/shard_map/pallas_call | solution.py:62
  165.0 2.8 %shard_map.29.before = f32[448,576]{1,0:T(8,128)S(1)} custom-call(s32[2]{0:T(128)S(1)} %pad_add_fusion.place, f32[448,576]{1,0:T(8,128)S(1)} %shard_map.28.before, bf16[4,448,896]{2,1,0:T(8,128)(2,1)S(1)} %get-tuple-element.67.gram, bf16[504,512]{1,0:T(8,128)(2,1)S(1)} %collective-permute-done.35.r11, bf16[504,512]{1,0:T(8,128)(2,1)S(1)} %collective-permute-done.36.r31, ...), custom_call_target="tpu_custom_call" | custom-call | flops 924844032 | bytes 5791744 | tf_op jit(solution)/shard_map/pallas_call | solution.py:62
  167.8 2.0 %shard_map.30 = bf16[448,576]{1,0:T(8,128)(2,1)} custom-call(s32[2]{0:T(128)S(1)} %pad_add_fusion.place, f32[448,576]{1,0:T(8,128)S(1)} %shard_map.29.before, bf16[4,448,896]{2,1,0:T(8,128)(2,1)S(1)} %get-tuple-element.67.gram, bf16[256,512]{1,0:T(8,128)(2,1)S(1)} %collective-permute-done.37.refs_0_, bf16[248,512]{1,0:T(8,128)(2,1)S(1)} %collective-permute-done.38.refs_1_), custom_call_target="tpu_custom_call" | custom-call | flops 231211008 | bytes 4759552 | tf_op jit(solution)/shard_map/pallas_call | solution.py:62
  (50 shorter events, 0.8 us)
Async XLA Ops:
  0.1 1.1 copy-start
  1.8 12.5 %collective-permute-start.2 = (bf16[504,512]{1,0:T(8,128)(2,1)S(1)}, bf16[504,512]{1,0:T(8,128)(2,1)S(1)}, u32[]{:S(2)}, u32[]{:S(2)}) collective-permute-start(bf16[504,512]{1,0:T(8,128)(2,1)S(1)} %get-tuple-element.41.refs_0_), channel_id=1, source_target_pairs={{32,0},{0,32},{33,1},{1,33},{34,2},{2,34},{35,3},{3,35},{36,4},{4,... | collective-permute-start | bytes 1548296 | tf_op jit(solution)/shard_map/ppermute | solution.py:40
  4.0 13.3 %collective-permute-start.1 = (bf16[504,512]{1,0:T(8,128)(2,1)S(1)}, bf16[504,512]{1,0:T(8,128)(2,1)S(1)}, u32[]{:S(2)}, u32[]{:S(2)}) collective-permute-start(bf16[504,512]{1,0:T(8,128)(2,1)S(1)} %get-tuple-element.41.refs_0_), channel_id=1, source_target_pairs={{192,0},{0,64},{64,128},{128,192},{193,1},{1,65},{65,129},{129,193... | collective-permute-start | bytes 1548296 | tf_op jit(solution)/shard_map/ppermute | solution.py:40
  5.2 12.1 %collective-permute-start = (bf16[504,512]{1,0:T(8,128)(2,1)S(1)}, bf16[504,512]{1,0:T(8,128)(2,1)S(1)}, u32[]{:S(2)}, u32[]{:S(2)}) collective-permute-start(bf16[504,512]{1,0:T(8,128)(2,1)S(1)} %get-tuple-element.41.refs_0_), channel_id=1, source_target_pairs={{64,0},{128,64},{192,128},{0,192},{65,1},{129,65},{193,129},{1,193... | collective-permute-start | bytes 1548296 | tf_op jit(solution)/shard_map/ppermute | solution.py:40
  17.3 9.5 %collective-permute-start.5 = (bf16[256,512]{1,0:T(8,128)(2,1)S(1)}, bf16[256,512]{1,0:T(8,128)(2,1)S(1)}, u32[]{:S(2)}, u32[]{:S(2)}) collective-permute-start(bf16[256,512]{1,0:T(8,128)(2,1)S(1)} %slice.30), channel_id=1, source_target_pairs={{64,0},{128,64},{192,128},{0,192},{65,1},{129,65},{193,129},{1,193... | collective-permute-start | bytes 786440 | tf_op jit(solution)/shard_map/ppermute | solution.py:40
  19.8 7.0 %collective-permute-start.6 = (bf16[248,512]{1,0:T(8,128)(2,1)S(1)}, bf16[248,512]{1,0:T(8,128)(2,1)S(1)}, u32[]{:S(2)}, u32[]{:S(2)}) collective-permute-start(bf16[248,512]{1,0:T(8,128)(2,1)S(1)} %slice.31), channel_id=1, source_target_pairs={{192,0},{0,64},{64,128},{128,192},{193,1},{1,65},{65,129},{129,193... | collective-permute-start | bytes 761864 | tf_op jit(solution)/shard_map/ppermute | solution.py:40
  24.1 8.4 %collective-permute-start.8 = (bf16[8,56,896]{2,1,0:T(8,128)(2,1)S(1)}, bf16[8,56,896]{2,1,0:T(8,128)(2,1)S(1)}, u32[]{:S(2)}, u32[]{:S(2)}) collective-permute-start(bf16[8,56,896]{2,1,0:T(8,128)(2,1)S(1)} %get-tuple-element.47), channel_id=1, source_target_pairs={{1,0},{0,1},{3,2},{2,3},{5,4},{4,5},{7,6},{6,7},{9,8},{8,9},{11,10... | collective-permute-start | bytes 2408456 | tf_op jit(solution)/shard_map/ppermute | solution.py:40
  29.2 5.2 %collective-permute-start.9 = (bf16[8,56,896]{2,1,0:T(8,128)(2,1)S(1)}, bf16[8,56,896]{2,1,0:T(8,128)(2,1)S(1)}, u32[]{:S(2)}, u32[]{:S(2)}) collective-permute-start(bf16[8,56,896]{2,1,0:T(8,128)(2,1)S(1)} %get-tuple-element.50), channel_id=1, source_target_pairs={{1,0},{0,1},{3,2},{2,3},{5,4},{4,5},{7,6},{6,7},{9,8},{8,9},{11,10... | collective-permute-start | bytes 2408456 | tf_op jit(solution)/shard_map/ppermute | solution.py:40
  35.4 7.5 %collective-permute-start.14 = (bf16[56,896]{1,0:T(8,128)(2,1)S(1)}, bf16[56,896]{1,0:T(8,128)(2,1)S(1)}, u32[]{:S(2)}, u32[]{:S(2)}) collective-permute-start(bf16[56,896]{1,0:T(8,128)(2,1)S(1)} %get-tuple-element.59), channel_id=1, source_target_pairs={{4,0},{8,4},{12,8},{16,12},{20,16},{24,20},{28,24},{0,28},{5,1},{9... | collective-permute-start | bytes 301064 | tf_op jit(solution)/shard_map/ppermute | solution.py:40
  41.1 5.3 %collective-permute-start.10 = (bf16[56,896]{1,0:T(8,128)(2,1)S(1)}, bf16[56,896]{1,0:T(8,128)(2,1)S(1)}, u32[]{:S(2)}, u32[]{:S(2)}) collective-permute-start(bf16[56,896]{1,0:T(8,128)(2,1)S(1)} %get-tuple-element.55), channel_id=1, source_target_pairs={{28,0},{0,4},{4,8},{8,12},{12,16},{16,20},{20,24},{24,28},{29,1},{... | collective-permute-start | bytes 301064 | tf_op jit(solution)/shard_map/ppermute | solution.py:40
  42.9 6.6 %collective-permute-start.15 = (bf16[112,896]{1,0:T(8,128)(2,1)S(1)}, bf16[112,896]{1,0:T(8,128)(2,1)S(1)}, u32[]{:S(2)}, u32[]{:S(2)}) collective-permute-start(bf16[112,896]{1,0:T(8,128)(2,1)S(1)} %pad_maximum_fusion.2), channel_id=1, source_target_pairs={{4,0},{8,4},{12,8},{16,12},{20,16},{24,20},{28,24},{0,28},{5,1},{9... | collective-permute-start | bytes 602120 | tf_op jit(solution)/shard_map/ppermute | solution.py:40
  46.5 6.6 %collective-permute-start.11 = (bf16[112,896]{1,0:T(8,128)(2,1)S(1)}, bf16[112,896]{1,0:T(8,128)(2,1)S(1)}, u32[]{:S(2)}, u32[]{:S(2)}) collective-permute-start(bf16[112,896]{1,0:T(8,128)(2,1)S(1)} %pad_maximum_fusion.1), channel_id=1, source_target_pairs={{28,0},{0,4},{4,8},{8,12},{12,16},{16,20},{20,24},{24,28},{29,1},{... | collective-permute-start | bytes 602120 | tf_op jit(solution)/shard_map/ppermute | solution.py:40
  49.6 6.1 %collective-permute-start.16 = (bf16[112,896]{1,0:T(8,128)(2,1)S(1)}, bf16[112,896]{1,0:T(8,128)(2,1)S(1)}, u32[]{:S(2)}, u32[]{:S(2)}) collective-permute-start(bf16[112,896]{1,0:T(8,128)(2,1)S(1)} %add_convert_fusion.1), channel_id=1, source_target_pairs={{4,0},{8,4},{12,8},{16,12},{20,16},{24,20},{28,24},{0,28},{5,1},{9... | collective-permute-start | bytes 602120 | tf_op jit(solution)/shard_map/ppermute | solution.py:40
  53.1 6.0 %collective-permute-start.12 = (bf16[112,896]{1,0:T(8,128)(2,1)S(1)}, bf16[112,896]{1,0:T(8,128)(2,1)S(1)}, u32[]{:S(2)}, u32[]{:S(2)}) collective-permute-start(bf16[112,896]{1,0:T(8,128)(2,1)S(1)} %add_convert_fusion.3), channel_id=1, source_target_pairs={{28,0},{0,4},{4,8},{8,12},{12,16},{16,20},{20,24},{24,28},{29,1},{... | collective-permute-start | bytes 602120 | tf_op jit(solution)/shard_map/ppermute | solution.py:40
  55.8 5.9 %collective-permute-start.17 = (bf16[112,896]{1,0:T(8,128)(2,1)S(1)}, bf16[112,896]{1,0:T(8,128)(2,1)S(1)}, u32[]{:S(2)}, u32[]{:S(2)}) collective-permute-start(bf16[112,896]{1,0:T(8,128)(2,1)S(1)} %add_convert_fusion), channel_id=1, source_target_pairs={{4,0},{8,4},{12,8},{16,12},{20,16},{24,20},{28,24},{0,28},{5,1},{9... | collective-permute-start | bytes 602120 | tf_op jit(solution)/shard_map/ppermute | solution.py:40
  59.2 5.9 %collective-permute-start.13 = (bf16[112,896]{1,0:T(8,128)(2,1)S(1)}, bf16[112,896]{1,0:T(8,128)(2,1)S(1)}, u32[]{:S(2)}, u32[]{:S(2)}) collective-permute-start(bf16[112,896]{1,0:T(8,128)(2,1)S(1)} %add_convert_fusion.2), channel_id=1, source_target_pairs={{28,0},{0,4},{4,8},{8,12},{12,16},{16,20},{20,24},{24,28},{29,1},{... | collective-permute-start | bytes 602120 | tf_op jit(solution)/shard_map/ppermute | solution.py:40
  65.7 7.4 %collective-permute-start.18 = (bf16[112,896]{1,0:T(8,128)(2,1)S(1)}, bf16[112,896]{1,0:T(8,128)(2,1)S(1)}, u32[]{:S(2)}, u32[]{:S(2)}) collective-permute-start(bf16[112,896]{1,0:T(8,128)(2,1)S(1)} %get-tuple-element.60.mine), channel_id=1, source_target_pairs={{2,0},{0,2},{3,1},{1,3},{6,4},{4,6},{7,5},{5,7},{10,8},{8,10},{11,... | collective-permute-start | bytes 602120 | tf_op jit(solution)/shard_map/ppermute | solution.py:40
  68.4 4.7 %collective-permute-start.20 = (bf16[56,896]{1,0:T(8,128)(2,1)S(1)}, bf16[56,896]{1,0:T(8,128)(2,1)S(1)}, u32[]{:S(2)}, u32[]{:S(2)}) collective-permute-start(bf16[56,896]{1,0:T(8,128)(2,1)S(1)} %get-tuple-element.61), channel_id=1, source_target_pairs={{34,0},{32,2},{2,32},{0,34},{35,1},{33,3},{3,33},{1,35},{38,4},{36... | collective-permute-start | bytes 301064 | tf_op jit(solution)/shard_map/ppermute | solution.py:53
  68.4 4.7 %collective-permute-start.19 = (bf16[56,896]{1,0:T(8,128)(2,1)S(1)}, bf16[56,896]{1,0:T(8,128)(2,1)S(1)}, u32[]{:S(2)}, u32[]{:S(2)}) collective-permute-start(bf16[56,896]{1,0:T(8,128)(2,1)S(1)} %get-tuple-element.61), channel_id=1, source_target_pairs={{32,0},{0,32},{33,1},{1,33},{34,2},{2,34},{35,3},{3,35},{36,4},{4,... | collective-permute-start | bytes 301064 | tf_op jit(solution)/shard_map/ppermute | solution.py:40
  73.7 5.9 %collective-permute-start.24 = (bf16[112,896]{1,0:T(8,128)(2,1)S(1)}, bf16[112,896]{1,0:T(8,128)(2,1)S(1)}, u32[]{:S(2)}, u32[]{:S(2)}) collective-permute-start(bf16[112,896]{1,0:T(8,128)(2,1)S(1)} %shard_map.23.refs_0_), channel_id=1, source_target_pairs={{28,0},{0,4},{4,8},{8,12},{12,16},{16,20},{20,24},{24,28},{29,1},{... | collective-permute-start | bytes 602120 | tf_op jit(solution)/shard_map/ppermute | solution.py:40
  73.8 5.8 %collective-permute-start.21 = (bf16[112,896]{1,0:T(8,128)(2,1)S(1)}, bf16[112,896]{1,0:T(8,128)(2,1)S(1)}, u32[]{:S(2)}, u32[]{:S(2)}) collective-permute-start(bf16[112,896]{1,0:T(8,128)(2,1)S(1)} %shard_map.23.refs_0_), channel_id=1, source_target_pairs={{4,0},{8,4},{12,8},{16,12},{20,16},{24,20},{28,24},{0,28},{5,1},{9... | collective-permute-start | bytes 602120 | tf_op jit(solution)/shard_map/ppermute | solution.py:40
  79.6 7.4 %collective-permute-start.25 = (bf16[112,896]{1,0:T(8,128)(2,1)S(1)}, bf16[112,896]{1,0:T(8,128)(2,1)S(1)}, u32[]{:S(2)}, u32[]{:S(2)}) collective-permute-start(bf16[112,896]{1,0:T(8,128)(2,1)S(1)} %collective-permute-done.24.refs_6_), channel_id=1, source_target_pairs={{28,0},{0,4},{4,8},{8,12},{12,16},{16,20},{20,24},{24,28},{29,1},{... | collective-permute-start | bytes 602120 | tf_op jit(solution)/shard_map/ppermute | solution.py:40
  79.6 7.4 %collective-permute-start.22 = (bf16[112,896]{1,0:T(8,128)(2,1)S(1)}, bf16[112,896]{1,0:T(8,128)(2,1)S(1)}, u32[]{:S(2)}, u32[]{:S(2)}) collective-permute-start(bf16[112,896]{1,0:T(8,128)(2,1)S(1)} %collective-permute-done.21.refs_1_), channel_id=1, source_target_pairs={{4,0},{8,4},{12,8},{16,12},{20,16},{24,20},{28,24},{0,28},{5,1},{9... | collective-permute-start | bytes 602120 | tf_op jit(solution)/shard_map/ppermute | solution.py:40
  87.0 6.6 %collective-permute-start.26 = (bf16[112,896]{1,0:T(8,128)(2,1)S(1)}, bf16[112,896]{1,0:T(8,128)(2,1)S(1)}, u32[]{:S(2)}, u32[]{:S(2)}) collective-permute-start(bf16[112,896]{1,0:T(8,128)(2,1)S(1)} %collective-permute-done.25.refs_5_), channel_id=1, source_target_pairs={{28,0},{0,4},{4,8},{8,12},{12,16},{16,20},{20,24},{24,28},{29,1},{... | collective-permute-start | bytes 602120 | tf_op jit(solution)/shard_map/ppermute | solution.py:40
  87.0 6.6 %collective-permute-start.23 = (bf16[112,896]{1,0:T(8,128)(2,1)S(1)}, bf16[112,896]{1,0:T(8,128)(2,1)S(1)}, u32[]{:S(2)}, u32[]{:S(2)}) collective-permute-start(bf16[112,896]{1,0:T(8,128)(2,1)S(1)} %collective-permute-done.22.refs_2_), channel_id=1, source_target_pairs={{4,0},{8,4},{12,8},{16,12},{20,16},{24,20},{28,24},{0,28},{5,1},{9... | collective-permute-start | bytes 602120 | tf_op jit(solution)/shard_map/ppermute | solution.py:40
  94.3 29.9 %collective-permute-start.27 = (bf16[7,112,896]{2,1,0:T(8,128)(2,1)S(1)}, bf16[7,112,896]{2,1,0:T(8,128)(2,1)S(1)}, u32[]{:S(2)}, u32[]{:S(2)}) collective-permute-start(bf16[7,112,896]{2,1,0:T(8,128)(2,1)S(1)} %shard_map.24.group), channel_id=1, source_target_pairs={{1,0},{0,1},{3,2},{2,3},{5,4},{4,5},{7,6},{6,7},{9,8},{8,9},{11,10... | collective-permute-start | bytes 4214792 | tf_op jit(solution)/shard_map/ppermute | solution.py:40
  103.3 16.8 %collective-permute-start.4 = (bf16[504,512]{1,0:T(8,128)(2,1)S(1)}, bf16[504,512]{1,0:T(8,128)(2,1)S(1)}, u32[]{:S(2)}, u32[]{:S(2)}) collective-permute-start(bf16[504,512]{1,0:T(8,128)(2,1)S(1)} %collective-permute-done.2.refs_3_), channel_id=1, source_target_pairs={{192,0},{0,64},{64,128},{128,192},{193,1},{1,65},{65,129},{129,193... | collective-permute-start | bytes 1548296 | tf_op jit(solution)/shard_map/ppermute | solution.py:40
  103.3 16.8 %collective-permute-start.3 = (bf16[504,512]{1,0:T(8,128)(2,1)S(1)}, bf16[504,512]{1,0:T(8,128)(2,1)S(1)}, u32[]{:S(2)}, u32[]{:S(2)}) collective-permute-start(bf16[504,512]{1,0:T(8,128)(2,1)S(1)} %collective-permute-done.2.refs_3_), channel_id=1, source_target_pairs={{64,0},{128,64},{192,128},{0,192},{65,1},{129,65},{193,129},{1,193... | collective-permute-start | bytes 1548296 | tf_op jit(solution)/shard_map/ppermute | solution.py:40
  106.0 14.1 %collective-permute-start.7 = (bf16[504,512]{1,0:T(8,128)(2,1)S(1)}, bf16[504,512]{1,0:T(8,128)(2,1)S(1)}, u32[]{:S(2)}, u32[]{:S(2)}) collective-permute-start(bf16[504,512]{1,0:T(8,128)(2,1)S(1)} %pad_maximum_fusion), channel_id=1, source_target_pairs={{32,0},{0,32},{33,1},{1,33},{34,2},{2,34},{35,3},{3,35},{36,4},{4,... | collective-permute-start | bytes 1548296 | tf_op jit(solution)/shard_map/ppermute | solution.py:40
  107.3 4.7 %collective-permute-start.28 = (bf16[56,896]{1,0:T(8,128)(2,1)S(1)}, bf16[56,896]{1,0:T(8,128)(2,1)S(1)}, u32[]{:S(2)}, u32[]{:S(2)}) collective-permute-start(bf16[56,896]{1,0:T(8,128)(2,1)S(1)} %slice.40), channel_id=1, source_target_pairs={{4,0},{8,4},{12,8},{16,12},{20,16},{24,20},{28,24},{0,28},{5,1},{9... | collective-permute-start | bytes 301064 | tf_op jit(solution)/shard_map/ppermute | solution.py:40
  112.0 5.7 %collective-permute-start.29 = (bf16[56,896]{1,0:T(8,128)(2,1)S(1)}, bf16[56,896]{1,0:T(8,128)(2,1)S(1)}, u32[]{:S(2)}, u32[]{:S(2)}) collective-permute-start(bf16[56,896]{1,0:T(8,128)(2,1)S(1)} %slice.41), channel_id=1, source_target_pairs={{28,0},{0,4},{4,8},{8,12},{12,16},{16,20},{20,24},{24,28},{29,1},{... | collective-permute-start | bytes 301064 | tf_op jit(solution)/shard_map/ppermute | solution.py:40
  117.6 9.0 %collective-permute-start.30 = (bf16[112,896]{1,0:T(8,128)(2,1)S(1)}, bf16[112,896]{1,0:T(8,128)(2,1)S(1)}, u32[]{:S(2)}, u32[]{:S(2)}) collective-permute-start(bf16[112,896]{1,0:T(8,128)(2,1)S(1)} %constant_dynamic-update-slice_fusion.mine), channel_id=1, source_target_pairs={{1,0},{0,1},{3,2},{2,3},{5,4},{4,5},{7,6},{6,7},{9,8},{8,9},{11,10... | collective-permute-start | bytes 602120 | tf_op jit(solution)/shard_map/ppermute | solution.py:40
  129.1 13.2 %collective-permute-start.33 = (bf16[504,512]{1,0:T(8,128)(2,1)S(1)}, bf16[504,512]{1,0:T(8,128)(2,1)S(1)}, u32[]{:S(2)}, u32[]{:S(2)}) collective-permute-start(bf16[504,512]{1,0:T(8,128)(2,1)S(1)} %get-tuple-element.68.refs_0_), channel_id=1, source_target_pairs={{32,0},{0,32},{33,1},{1,33},{34,2},{2,34},{35,3},{3,35},{36,4},{4,... | collective-permute-start | bytes 1548296 | tf_op jit(solution)/shard_map/ppermute | solution.py:40
  129.5 13.2 %collective-permute-start.32 = (bf16[504,512]{1,0:T(8,128)(2,1)S(1)}, bf16[504,512]{1,0:T(8,128)(2,1)S(1)}, u32[]{:S(2)}, u32[]{:S(2)}) collective-permute-start(bf16[504,512]{1,0:T(8,128)(2,1)S(1)} %get-tuple-element.68.refs_0_), channel_id=1, source_target_pairs={{192,0},{0,64},{64,128},{128,192},{193,1},{1,65},{65,129},{129,193... | collective-permute-start | bytes 1548296 | tf_op jit(solution)/shard_map/ppermute | solution.py:40
  129.5 13.2 %collective-permute-start.31 = (bf16[504,512]{1,0:T(8,128)(2,1)S(1)}, bf16[504,512]{1,0:T(8,128)(2,1)S(1)}, u32[]{:S(2)}, u32[]{:S(2)}) collective-permute-start(bf16[504,512]{1,0:T(8,128)(2,1)S(1)} %get-tuple-element.68.refs_0_), channel_id=1, source_target_pairs={{64,0},{128,64},{192,128},{0,192},{65,1},{129,65},{193,129},{1,193... | collective-permute-start | bytes 1548296 | tf_op jit(solution)/shard_map/ppermute | solution.py:40
  142.7 11.1 %collective-permute-start.35 = (bf16[504,512]{1,0:T(8,128)(2,1)S(1)}, bf16[504,512]{1,0:T(8,128)(2,1)S(1)}, u32[]{:S(2)}, u32[]{:S(2)}) collective-permute-start(bf16[504,512]{1,0:T(8,128)(2,1)S(1)} %collective-permute-done.33.refs_3_), channel_id=1, source_target_pairs={{64,0},{128,64},{192,128},{0,192},{65,1},{129,65},{193,129},{1,193... | collective-permute-start | bytes 1548296 | tf_op jit(solution)/shard_map/ppermute | solution.py:40
  145.1 11.7 %collective-permute-start.36 = (bf16[504,512]{1,0:T(8,128)(2,1)S(1)}, bf16[504,512]{1,0:T(8,128)(2,1)S(1)}, u32[]{:S(2)}, u32[]{:S(2)}) collective-permute-start(bf16[504,512]{1,0:T(8,128)(2,1)S(1)} %collective-permute-done.32.refs_2_), channel_id=1, source_target_pairs={{32,0},{0,32},{33,1},{1,33},{34,2},{2,34},{35,3},{3,35},{36,4},{4,... | collective-permute-start | bytes 1548296 | tf_op jit(solution)/shard_map/ppermute | solution.py:40
  147.1 12.4 %collective-permute-start.34 = (bf16[504,512]{1,0:T(8,128)(2,1)S(1)}, bf16[504,512]{1,0:T(8,128)(2,1)S(1)}, u32[]{:S(2)}, u32[]{:S(2)}) collective-permute-start(bf16[504,512]{1,0:T(8,128)(2,1)S(1)} %collective-permute-done.32.refs_2_), channel_id=1, source_target_pairs={{192,0},{0,64},{64,128},{128,192},{193,1},{1,65},{65,129},{129,193... | collective-permute-start | bytes 1548296 | tf_op jit(solution)/shard_map/ppermute | solution.py:40
  159.5 8.3 %collective-permute-start.37 = (bf16[256,512]{1,0:T(8,128)(2,1)S(1)}, bf16[256,512]{1,0:T(8,128)(2,1)S(1)}, u32[]{:S(2)}, u32[]{:S(2)}) collective-permute-start(bf16[256,512]{1,0:T(8,128)(2,1)S(1)} %slice.38), channel_id=1, source_target_pairs={{64,0},{128,64},{192,128},{0,192},{65,1},{129,65},{193,129},{1,193... | collective-permute-start | bytes 786440 | tf_op jit(solution)/shard_map/ppermute | solution.py:40
  159.6 8.2 %collective-permute-start.38 = (bf16[248,512]{1,0:T(8,128)(2,1)S(1)}, bf16[248,512]{1,0:T(8,128)(2,1)S(1)}, u32[]{:S(2)}, u32[]{:S(2)}) collective-permute-start(bf16[248,512]{1,0:T(8,128)(2,1)S(1)} %slice.39), channel_id=1, source_target_pairs={{192,0},{0,64},{64,128},{128,192},{193,1},{1,65},{65,129},{129,193... | collective-permute-start | bytes 761864 | tf_op jit(solution)/shard_map/ppermute | solution.py:40

commit v3 on v2

--- a/solution.py
+++ b/solution.py
@@ -192,40 +192,30 @@
 
 def pair_body(place, low, low_other, high, high_other, *outs):
     size = low.shape[1]
-    for d in range(RING):
-        lower = (low[d].astype(F32) + low_other[d].astype(F32)).astype(BF16)
-        upper = (high[d].astype(F32) + high_other[d].astype(F32)).astype(BF16)
-        if d == FAR:
-            outs[d][...] = lower
-            outs[d + 1][...] = upper
-        else:
-            out = outs[d if d < FAR else d + 1]
-            out[:size] = lower
-            out[size:] = upper
+    for d, out in enumerate(outs):
+        out[:size] = (low[d].astype(F32) + low_other[d].astype(F32)).astype(BF16)
+        out[size:] = (high[d].astype(F32) + high_other[d].astype(F32)).astype(BF16)
 
 
 def add(a, b):
     return (a.astype(F32) + b.astype(F32)).astype(BF16)
 
 
-def ring_sum(place, part, up, down):
-    size = up.shape[0]
-    for step in range(FAR - 1, -1, -1):
+def ring_sum(place, part):
+    up, down = part[FAR - 1], part[FAR + 1]
+    far = shift(part[FAR], "z", FAR)
+    for step in range(FAR - 2, -1, -1):
         up = shift(up, "z", -1)
         down = shift(down, "z", 1)
-        if step == 0:
-            return call(sum_body, place, (part[0], up, down), [array(part[0].shape), array((size, up.shape[1]))])
-        elif step == FAR - 1:
-            one, two = part[step], part[RING - step]
-            up = jnp.concatenate([add(one[:size], up), one[size:]], 0)
-            down = jnp.concatenate([two[:size], add(two[size:], down)], 0)
-        else:
+        if step > 0:
             up, down = add(part[step], up), add(part[RING - step], down)
-
-
-def sum_body(place, near, up, down, mine, ahead):
+    size, width = up.shape[0] // 2, up.shape[1]
+    return call(sum_body, place, (part[0], up, down, far), [array(up.shape), array((size, width))])
+
+
+def sum_body(place, near, up, down, far, mine, ahead):
     size = ahead.shape[0]
-    total = near[...].astype(F32) + up[...].astype(F32) + down[...].astype(F32)
+    total = near[...].astype(F32) + up[...].astype(F32) + down[...].astype(F32) + far[...].astype(F32)
     mine[...] = total.astype(BF16)
     ahead[...] = total[size:].astype(BF16)
 
@@ -248,15 +238,11 @@
 def lay(gram, side, group, z):
     size = gram.shape[1] // RING
 
-    @pl.loop(0, RING - 1)
-    def _(i):
-        where = chunk(z, i + jnp.where(i >= FAR, 1, 0), size)
+    @pl.loop(0, RING)
+    def _(i):
+        where = chunk(z, i, size)
         gram[side, where, :] = group[i, :size]
         gram[side + 2, where, :] = group[i, size:]
-
-    @pl.loop(0, 2)
-    def _(i):
-        gram[side + 2 * i, chunk(z, FAR, size), :] = jnp.zeros((size, gram.shape[2]), BF16)
 
 
 def own_rows_body(place, panel, group, gram, total):
@@ -269,30 +255,15 @@
         total[...] += jnp.dot(gram[c + 2 * i], panel[c + 2 * i], preferred_element_type=F32)
 
 
-def other_rows_body(place, panel, group, before_gram, before, gram, total):
+def other_rows_body(place, own, panel, group, before_gram, before, gram, w_high, w_low, total):
     z, side = place[0], 1 - place[1]
     lay(gram, side, group, z)
+    total[...] = before[...]
 
     @pl.loop(0, 2)
     def _(i):
         total[...] += jnp.dot(gram[side + 2 * i], panel[side + 2 * i], preferred_element_type=F32)
 
-
-def update_body(place, own, panel, before_gram, before, mine, other, gram, w_high, w_low, total, acc):
-    z, c = place[0], place[1]
-    size = gram.shape[1] // RING
-    where = chunk(z, FAR, size)
-    for side, ref in ((c, mine), (1 - c, other)):
-        gram[side, where, :] = ref[:size]
-        gram[side + 2, where, :] = ref[size:]
-    acc[...] = jnp.zeros(acc.shape, F32)
-
-    @pl.loop(0, 4)
-    def _(i):
-        acc[...] += jnp.dot(gram[i, where, :], panel[i], preferred_element_type=F32)
-
-    total[...] = before[...]
-    total[where, :] = acc[...]
     w = coef_b * own[...].astype(F32) + coef_c * total[...]
     pack(w, w_high)
     w_low[...] = (w - w.astype(BF16).astype(F32)).astype(BF16)
@@ -369,38 +340,32 @@
     r21 = jnp.concatenate(r20, 0)
     r21 = shift(r21, "yl", 1)
     panel = call(panel_body, place, (low, r11, r31, r21, *r20), array((4, 2 * rows, cols)), 0, [room(2)])
-    one, two = array((size, 2 * rows)), array((2 * size, 2 * rows))
-    parts = call(pair_body, place, halves, [two] * FAR + [one] * 2 + [two] * (FAR - 1))
-    part = {d: parts[d if d < FAR else d + 1] for d in range(RING) if d != FAR}
-    mine, ahead = ring_sum(place, part, parts[FAR], parts[FAR + 1])
+    two = array((2 * size, 2 * rows))
+    parts = call(pair_body, place, halves, [two] * RING)
+    mine, ahead = ring_sum(place, parts)
     across = shift(mine, "yh", 1)
     same = shift(ahead, "yl", 1)
     cross = fetch(ahead, ("yl", "yh"), lambda y, h: (y + 1, h + 1))
     mine = call(join_body, place, (mine, across, same, cross), array(mine.shape))
 
     ring = {0: mine}
+    ring[FAR] = shift(mine, "z", FAR)
     up, down = mine, mine
     for step in range(1, FAR):
         up = shift(up, "z", 1)
         down = shift(down, "z", -1)
         ring[step], ring[RING - step] = up, down
-    ends = [shift(up[:size], "z", 1)]
-    ends.append(shift(down[size:], "z", -1))
-    pieces = [ring[d] for d in range(RING) if d != FAR]
-    group = call(group_body, place, pieces, array((RING - 1, 2 * size, 2 * rows)))
-    ends = jnp.concatenate(ends, 0)
-
+    group = call(group_body, place, [ring[d] for d in range(RING)], array((RING, 2 * size, 2 * rows)))
     other = shift(group, "c", 1)
     gram, total = call(own_rows_body, place, (panel, group), [wide, sums], 2 * work)
-    gram, total = call(other_rows_body, place, (panel, other, gram, total), [wide, sums], 2 * work, alias={3: 0, 4: 1})
     gram, w_high, w_low = call(
-        update_body,
+        other_rows_body,
         place,
-        (own, panel, gram, total, ends, shift(ends, "c", 1)),
+        (own, panel, other, gram, total),
         [wide, flat, block],
-        work // 2,
-        [pltpu.VMEM((rows, cols), F32), pltpu.VMEM((size, cols), F32)],
-        alias={3: 0},
+        2 * work,
+        [pltpu.VMEM((rows, cols), F32)],
+        alias={4: 0},
     )
 
     near = near_blocks(w_high)

time: 171 us -> 176 us (1.029)
  the two profiles are of different devices: /device:TPU:1 before, /device:TPU:96 now
where the time goes in v3:
time: 176 us
  waiting for transfers between devices  102 us (58%)
  starting transfers between devices  46.5 us (26%)
  Pallas kernels  25.8 us (15%)
    ppermute x35, waiting for transfers between devices, shift(): lax.ppermute(value, axis, [((i + step) % size, i) for i in range(size)])  96.3 us
    ppermute x35, starting transfers between devices, shift(): lax.ppermute(value, axis, [((i + step) % size, i) for i in range(size)])  46.3 us
    pallas_call x13, Pallas kernels, call(): pl.pallas_call(body, out_shape=outs if home else [pltpu.VMEM(o.shape, o.d...  25.8 us
    ppermute x1, waiting for transfers between devices, fetch(): lax.ppermute(value, axes, [(flat(source(*p)), flat(p)) for p in places])  5.24 us
  transfers between devices with their start and end apart: 36, of which 24 were waited for; matrix products, arithmetic and copies ran while one was open for 0% of the time, Pallas kernels for 10%

profile of v3, /device:TPU:96, one launch (start us, length us, event | category | flops | bytes accessed | tf_op | source)
XLA Modules:
  0.0 175.5 jit_solution(12702603269737660494)
XLA Ops:
  0.1 1.1 copy-done
  1.1 0.6 shard_map.17
  1.8 1.7 collective-permute-start.2
  3.4 1.5 collective-permute-start.1
  4.9 1.7 collective-permute-start
  6.7 8.7 %collective-permute-done.2.refs_3_ = bf16[504,512]{1,0:T(8,128)(2,1)S(1)} collective-permute-done((bf16[504,512]{1,0:T(8,128)(2,1)S(1)}, bf16[504,512]{1,0:T(8,128)(2,1)S(1)}, u32[]{:S(2)}, u32[]{:S(2)}) %collective-permute-start.2) | collective-permute-done | bytes 516128 | tf_op jit(solution)/shard_map/ppermute | solution.py:40
  15.4 2.5 %collective-permute-done.1.refs_2_ = bf16[504,512]{1,0:T(8,128)(2,1)S(1)} collective-permute-done((bf16[504,512]{1,0:T(8,128)(2,1)S(1)}, bf16[504,512]{1,0:T(8,128)(2,1)S(1)}, u32[]{:S(2)}, u32[]{:S(2)}) %collective-permute-start.1) | collective-permute-done | bytes 516128 | tf_op jit(solution)/shard_map/ppermute | solution.py:40
  17.9 3.0 %collective-permute-start.5 = (bf16[256,512]{1,0:T(8,128)(2,1)S(1)}, bf16[256,512]{1,0:T(8,128)(2,1)S(1)}, u32[]{:S(2)}, u32[]{:S(2)}) collective-permute-start(bf16[256,512]{1,0:T(8,128)(2,1)S(1)} %slice.12), channel_id=1, source_target_pairs={{64,0},{128,64},{192,128},{0,192},{65,1},{129,65},{193,129},{1,193... | collective-permute-start | bytes 786440 | tf_op jit(solution)/shard_map/ppermute | solution.py:40
  21.0 4.2 %shard_map.18 = (bf16[8,56,896]{2,1,0:T(8,128)(2,1)S(1)}, bf16[8,56,896]{2,1,0:T(8,128)(2,1)S(1)}, bf16[3,896,576]{2,1,0:T(8,128)(2,1)S(1)}, f32[448,896]{1,0:T(8,128)S(1)}) custom-call(s32[2]{0:T(128)S(1)} %pad_add_fusion.place, bf16[448,576]{1,0:T(8,128)(2,1)S(1)} %get-tuple-element.37.own, bf16[504,512]{1,0:T(8,128)(2,1)S(1)} %get-tuple-element.38.refs_0_, ...), custom_call_target="tpu_custom_call" | custom-call | flops 1387266048 | bytes 8085504 | tf_op jit(solution)/shard_map/pallas_call | solution.py:62
  25.2 0.1 collective-permute-start.8
  25.3 3.2 %collective-permute-done.6.refs_4_.bottom = bf16[248,512]{1,0:T(8,128)(2,1)S(1)} collective-permute-done((bf16[248,512]{1,0:T(8,128)(2,1)S(1)}, bf16[248,512]{1,0:T(8,128)(2,1)S(1)}, u32[]{:S(2)}, u32[]{:S(2)}) %collective-permute-start.6) | collective-permute-done | bytes 253984 | tf_op jit(solution)/shard_map/ppermute | solution.py:40
  28.5 2.4 %shard_map.20 = (bf16[8,56,896]{2,1,0:T(8,128)(2,1)S(1)}, bf16[8,56,896]{2,1,0:T(8,128)(2,1)S(1)}) custom-call(s32[2]{0:T(128)S(1)} %pad_add_fusion.place, bf16[448,576]{1,0:T(8,128)(2,1)S(1)} %get-tuple-element.37.own, bf16[3,896,576]{2,1,0:T(8,128)(2,1)S(1)} %get-tuple-element.42.low, f32[448,896]{1,0:T(8,128)S(1)} %get-tuple-element.45.partner, ...), custom_call_target="tpu_custom_call" | custom-call | flops 462422016 | bytes 6537216 | tf_op jit(solution)/shard_map/pallas_call | solution.py:62
  30.9 0.1 collective-permute-start.9
  31.1 2.3 %collective-permute-done.9.high_other = bf16[8,56,896]{2,1,0:T(8,128)(2,1)S(1)} collective-permute-done((bf16[8,56,896]{2,1,0:T(8,128)(2,1)S(1)}, bf16[8,56,896]{2,1,0:T(8,128)(2,1)S(1)}, u32[]{:S(2)}, u32[]{:S(2)}) %collective-permute-start.9) | collective-permute-done | bytes 802848 | tf_op jit(solution)/shard_map/ppermute | solution.py:40
  33.3 0.9 shard_map.21
  34.3 3.2 %collective-permute-start.10 = (bf16[112,896]{1,0:T(8,128)(2,1)S(1)}, bf16[112,896]{1,0:T(8,128)(2,1)S(1)}, u32[]{:S(2)}, u32[]{:S(2)}) collective-permute-start(bf16[112,896]{1,0:T(8,128)(2,1)S(1)} %get-tuple-element.51), channel_id=1, source_target_pairs={{28,0},{0,4},{4,8},{8,12},{12,16},{16,20},{20,24},{24,28},{29,1},{... | collective-permute-start | bytes 602120 | tf_op jit(solution)/shard_map/ppermute | solution.py:40
  37.5 3.4 %collective-permute-start.16 = (bf16[112,896]{1,0:T(8,128)(2,1)S(1)}, bf16[112,896]{1,0:T(8,128)(2,1)S(1)}, u32[]{:S(2)}, u32[]{:S(2)}) collective-permute-start(bf16[112,896]{1,0:T(8,128)(2,1)S(1)} %get-tuple-element.55), channel_id=1, source_target_pairs={{16,0},{20,4},{24,8},{28,12},{0,16},{4,20},{8,24},{12,28},{17,1},{... | collective-permute-start | bytes 602120 | tf_op jit(solution)/shard_map/ppermute | solution.py:40
  40.9 7.0 %collective-permute-done.10 = bf16[112,896]{1,0:T(8,128)(2,1)S(1)} collective-permute-done((bf16[112,896]{1,0:T(8,128)(2,1)S(1)}, bf16[112,896]{1,0:T(8,128)(2,1)S(1)}, u32[]{:S(2)}, u32[]{:S(2)}) %collective-permute-start.10) | collective-permute-done | bytes 200736 | tf_op jit(solution)/shard_map/ppermute | solution.py:40
  47.9 3.9 %collective-permute-start.11 = (bf16[112,896]{1,0:T(8,128)(2,1)S(1)}, bf16[112,896]{1,0:T(8,128)(2,1)S(1)}, u32[]{:S(2)}, u32[]{:S(2)}) collective-permute-start(bf16[112,896]{1,0:T(8,128)(2,1)S(1)} %add_convert_fusion.3), channel_id=1, source_target_pairs={{28,0},{0,4},{4,8},{8,12},{12,16},{16,20},{20,24},{24,28},{29,1},{... | collective-permute-start | bytes 602120 | tf_op jit(solution)/shard_map/ppermute | solution.py:40
  51.8 1.3 collective-permute-done.13
  53.3 2.1 %collective-permute-done.11 = bf16[112,896]{1,0:T(8,128)(2,1)S(1)} collective-permute-done((bf16[112,896]{1,0:T(8,128)(2,1)S(1)}, bf16[112,896]{1,0:T(8,128)(2,1)S(1)}, u32[]{:S(2)}, u32[]{:S(2)}) %collective-permute-start.11) | collective-permute-done | bytes 200736 | tf_op jit(solution)/shard_map/ppermute | solution.py:40
  55.5 3.8 %collective-permute-start.12 = (bf16[112,896]{1,0:T(8,128)(2,1)S(1)}, bf16[112,896]{1,0:T(8,128)(2,1)S(1)}, u32[]{:S(2)}, u32[]{:S(2)}) collective-permute-start(bf16[112,896]{1,0:T(8,128)(2,1)S(1)} %add_convert_fusion.2), channel_id=1, source_target_pairs={{28,0},{0,4},{4,8},{8,12},{12,16},{16,20},{20,24},{24,28},{29,1},{... | collective-permute-start | bytes 602120 | tf_op jit(solution)/shard_map/ppermute | solution.py:40
  59.2 1.0 collective-permute-done.14
  60.3 0.3 collective-permute-start.15
  60.5 1.9 %collective-permute-done.12.up = bf16[112,896]{1,0:T(8,128)(2,1)S(1)} collective-permute-done((bf16[112,896]{1,0:T(8,128)(2,1)S(1)}, bf16[112,896]{1,0:T(8,128)(2,1)S(1)}, u32[]{:S(2)}, u32[]{:S(2)}) %collective-permute-start.12) | collective-permute-done | bytes 200736 | tf_op jit(solution)/shard_map/ppermute | solution.py:40
  62.5 5.0 %collective-permute-done.15.down = bf16[112,896]{1,0:T(8,128)(2,1)S(1)} collective-permute-done((bf16[112,896]{1,0:T(8,128)(2,1)S(1)}, bf16[112,896]{1,0:T(8,128)(2,1)S(1)}, u32[]{:S(2)}, u32[]{:S(2)}) %collective-permute-start.15) | collective-permute-done | bytes 200736 | tf_op jit(solution)/shard_map/ppermute | solution.py:40
  67.4 0.6 shard_map.22
  68.1 3.0 %collective-permute-start.17 = (bf16[112,896]{1,0:T(8,128)(2,1)S(1)}, bf16[112,896]{1,0:T(8,128)(2,1)S(1)}, u32[]{:S(2)}, u32[]{:S(2)}) collective-permute-start(bf16[112,896]{1,0:T(8,128)(2,1)S(1)} %get-tuple-element.56.mine), channel_id=1, source_target_pairs={{2,0},{0,2},{3,1},{1,3},{6,4},{4,6},{7,5},{5,7},{10,8},{8,10},{11,... | collective-permute-start | bytes 602120 | tf_op jit(solution)/shard_map/ppermute | solution.py:40
  71.1 0.2 collective-permute-start.19
  71.3 0.4 collective-permute-start.18
  71.7 5.2 %collective-permute-done.19.cross = bf16[56,896]{1,0:T(8,128)(2,1)S(1)} collective-permute-done((bf16[56,896]{1,0:T(8,128)(2,1)S(1)}, bf16[56,896]{1,0:T(8,128)(2,1)S(1)}, u32[]{:S(2)}, u32[]{:S(2)}) %collective-permute-start.19) | collective-permute-done | bytes 100384 | tf_op jit(solution)/shard_map/ppermute | solution.py:53
  76.9 0.6 shard_map.23.refs_0_
  77.6 2.0 %collective-permute-start.20 = (bf16[112,896]{1,0:T(8,128)(2,1)S(1)}, bf16[112,896]{1,0:T(8,128)(2,1)S(1)}, u32[]{:S(2)}, u32[]{:S(2)}) collective-permute-start(bf16[112,896]{1,0:T(8,128)(2,1)S(1)} %shard_map.23.refs_0_), channel_id=1, source_target_pairs={{4,0},{8,4},{12,8},{16,12},{20,16},{24,20},{28,24},{0,28},{5,1},{9... | collective-permute-start | bytes 602120 | tf_op jit(solution)/shard_map/ppermute | solution.py:40
  79.6 4.8 %collective-permute-done.24.refs_7_ = bf16[112,896]{1,0:T(8,128)(2,1)S(1)} collective-permute-done((bf16[112,896]{1,0:T(8,128)(2,1)S(1)}, bf16[112,896]{1,0:T(8,128)(2,1)S(1)}, u32[]{:S(2)}, u32[]{:S(2)}) %collective-permute-start.24) | collective-permute-done | bytes 200736 | tf_op jit(solution)/shard_map/ppermute | solution.py:40
  84.5 0.4 collective-permute-start.25
  84.9 0.4 collective-permute-done.20.refs_1_
  85.3 2.0 %collective-permute-start.21 = (bf16[112,896]{1,0:T(8,128)(2,1)S(1)}, bf16[112,896]{1,0:T(8,128)(2,1)S(1)}, u32[]{:S(2)}, u32[]{:S(2)}) collective-permute-start(bf16[112,896]{1,0:T(8,128)(2,1)S(1)} %collective-permute-done.20.refs_1_), channel_id=1, source_target_pairs={{4,0},{8,4},{12,8},{16,12},{20,16},{24,20},{28,24},{0,28},{5,1},{9... | collective-permute-start | bytes 602120 | tf_op jit(solution)/shard_map/ppermute | solution.py:40
  87.3 1.8 collective-permute-start.23
  89.0 6.3 %collective-permute-done.25.refs_6_ = bf16[112,896]{1,0:T(8,128)(2,1)S(1)} collective-permute-done((bf16[112,896]{1,0:T(8,128)(2,1)S(1)}, bf16[112,896]{1,0:T(8,128)(2,1)S(1)}, u32[]{:S(2)}, u32[]{:S(2)}) %collective-permute-start.25) | collective-permute-done | bytes 200736 | tf_op jit(solution)/shard_map/ppermute | solution.py:40
  95.3 6.8 %collective-permute-done.21.refs_2_ = bf16[112,896]{1,0:T(8,128)(2,1)S(1)} collective-permute-done((bf16[112,896]{1,0:T(8,128)(2,1)S(1)}, bf16[112,896]{1,0:T(8,128)(2,1)S(1)}, u32[]{:S(2)}, u32[]{:S(2)}) %collective-permute-start.21) | collective-permute-done | bytes 200736 | tf_op jit(solution)/shard_map/ppermute | solution.py:40
  102.1 0.9 collective-permute-done.26.refs_5_
  103.1 6.0 %collective-permute-done.22.refs_3_ = bf16[112,896]{1,0:T(8,128)(2,1)S(1)} collective-permute-done((bf16[112,896]{1,0:T(8,128)(2,1)S(1)}, bf16[112,896]{1,0:T(8,128)(2,1)S(1)}, u32[]{:S(2)}, u32[]{:S(2)}) %collective-permute-start.22) | collective-permute-done | bytes 200736 | tf_op jit(solution)/shard_map/ppermute | solution.py:40
  109.1 0.7 shard_map.24.group
  109.7 0.1 collective-permute-start.27
  109.9 3.2 %collective-permute-start.3 = (bf16[504,512]{1,0:T(8,128)(2,1)S(1)}, bf16[504,512]{1,0:T(8,128)(2,1)S(1)}, u32[]{:S(2)}, u32[]{:S(2)}) collective-permute-start(bf16[504,512]{1,0:T(8,128)(2,1)S(1)} %collective-permute-done.2.refs_3_), channel_id=1, source_target_pairs={{64,0},{128,64},{192,128},{0,192},{65,1},{129,65},{193,129},{1,193... | collective-permute-start | bytes 1548296 | tf_op jit(solution)/shard_map/ppermute | solution.py:40
  113.2 0.3 collective-permute-start.7
  113.5 11.7 %collective-permute-done.4.refs_1_ = bf16[504,512]{1,0:T(8,128)(2,1)S(1)} collective-permute-done((bf16[504,512]{1,0:T(8,128)(2,1)S(1)}, bf16[504,512]{1,0:T(8,128)(2,1)S(1)}, u32[]{:S(2)}, u32[]{:S(2)}) %collective-permute-start.4) | collective-permute-done | bytes 516128 | tf_op jit(solution)/shard_map/ppermute | solution.py:40
  125.2 1.8 %collective-permute-done.7.refs_2_ = bf16[504,512]{1,0:T(8,128)(2,1)S(1)} collective-permute-done((bf16[504,512]{1,0:T(8,128)(2,1)S(1)}, bf16[504,512]{1,0:T(8,128)(2,1)S(1)}, u32[]{:S(2)}, u32[]{:S(2)}) %collective-permute-start.7) | collective-permute-done | bytes 516128 | tf_op jit(solution)/shard_map/ppermute | solution.py:40
  127.0 1.5 shard_map.19.panel
  128.5 2.6 %shard_map.25 = (bf16[4,448,896]{2,1,0:T(8,128)(2,1)S(1)}, f32[448,576]{1,0:T(8,128)S(1)}) custom-call(s32[2]{0:T(128)S(1)} %pad_add_fusion.place, bf16[4,896,576]{2,1,0:T(8,128)(2,1)S(1)} %shard_map.19.panel, bf16[8,112,896]{2,1,0:T(8,128)(2,1)S(1)} %shard_map.24.group), custom_call_target="tpu_custom_call" | custom-call | flops 924844032 | bytes 9461760 | tf_op jit(solution)/shard_map/pallas_call | solution.py:62
  131.0 3.1 %shard_map.26 = (bf16[4,448,896]{2,1,0:T(8,128)(2,1)S(1)}, bf16[504,512]{1,0:T(8,128)(2,1)S(1)}, bf16[448,576]{1,0:T(8,128)(2,1)S(1)}) custom-call(s32[2]{0:T(128)S(1)} %pad_add_fusion.place, bf16[448,576]{1,0:T(8,128)(2,1)S(1)} %get-tuple-element.37.own, bf16[4,896,576]{2,1,0:T(8,128)(2,1)S(1)} %shard_map.19.panel, ...), custom_call_target="tpu_custom_call", output_to_operand_aliasing={{0}: (4, {})} | custom-call | flops 924844032 | bytes 14221312 | tf_op jit(solution)/shard_map/pallas_call | solution.py:62
  134.1 0.4 collective-permute-start.30
  134.5 3.2 %collective-permute-start.28 = (bf16[504,512]{1,0:T(8,128)(2,1)S(1)}, bf16[504,512]{1,0:T(8,128)(2,1)S(1)}, u32[]{:S(2)}, u32[]{:S(2)}) collective-permute-start(bf16[504,512]{1,0:T(8,128)(2,1)S(1)} %get-tuple-element.62.refs_0_), channel_id=1, source_target_pairs={{64,0},{128,64},{192,128},{0,192},{65,1},{129,65},{193,129},{1,193... | collective-permute-start | bytes 1548296 | tf_op jit(solution)/shard_map/ppermute | solution.py:40
  137.7 9.1 %collective-permute-done.30.refs_3_ = bf16[504,512]{1,0:T(8,128)(2,1)S(1)} collective-permute-done((bf16[504,512]{1,0:T(8,128)(2,1)S(1)}, bf16[504,512]{1,0:T(8,128)(2,1)S(1)}, u32[]{:S(2)}, u32[]{:S(2)}) %collective-permute-start.30) | collective-permute-done | bytes 516128 | tf_op jit(solution)/shard_map/ppermute | solution.py:40
  146.9 1.5 collective-permute-done.29.refs_2_
  148.4 3.0 %collective-permute-start.32 = (bf16[504,512]{1,0:T(8,128)(2,1)S(1)}, bf16[504,512]{1,0:T(8,128)(2,1)S(1)}, u32[]{:S(2)}, u32[]{:S(2)}) collective-permute-start(bf16[504,512]{1,0:T(8,128)(2,1)S(1)} %collective-permute-done.30.refs_3_), channel_id=1, source_target_pairs={{64,0},{128,64},{192,128},{0,192},{65,1},{129,65},{193,129},{1,193... | collective-permute-start | bytes 1548296 | tf_op jit(solution)/shard_map/ppermute | solution.py:40
  151.3 1.5 collective-permute-start.33
  152.8 7.6 %collective-permute-done.32.r11 = bf16[504,512]{1,0:T(8,128)(2,1)S(1)} collective-permute-done((bf16[504,512]{1,0:T(8,128)(2,1)S(1)}, bf16[504,512]{1,0:T(8,128)(2,1)S(1)}, u32[]{:S(2)}, u32[]{:S(2)}) %collective-permute-start.32) | collective-permute-done | bytes 516128 | tf_op jit(solution)/shard_map/ppermute | solution.py:40
  160.3 2.2 %collective-permute-done.33.r31 = bf16[504,512]{1,0:T(8,128)(2,1)S(1)} collective-permute-done((bf16[504,512]{1,0:T(8,128)(2,1)S(1)}, bf16[504,512]{1,0:T(8,128)(2,1)S(1)}, u32[]{:S(2)}, u32[]{:S(2)}) %collective-permute-start.33) | collective-permute-done | bytes 516128 | tf_op jit(solution)/shard_map/ppermute | solution.py:40
  162.5 2.1 %collective-permute-done.31.r20 = bf16[504,512]{1,0:T(8,128)(2,1)S(1)} collective-permute-done((bf16[504,512]{1,0:T(8,128)(2,1)S(1)}, bf16[504,512]{1,0:T(8,128)(2,1)S(1)}, u32[]{:S(2)}, u32[]{:S(2)}) %collective-permute-start.31) | collective-permute-done | bytes 516128 | tf_op jit(solution)/shard_map/ppermute | solution.py:40
  164.8 2.1 %collective-permute-start.35 = (bf16[248,512]{1,0:T(8,128)(2,1)S(1)}, bf16[248,512]{1,0:T(8,128)(2,1)S(1)}, u32[]{:S(2)}, u32[]{:S(2)}) collective-permute-start(bf16[248,512]{1,0:T(8,128)(2,1)S(1)} %slice.15), channel_id=1, source_target_pairs={{192,0},{0,64},{64,128},{128,192},{193,1},{1,65},{65,129},{129,193... | collective-permute-start | bytes 761864 | tf_op jit(solution)/shard_map/ppermute | solution.py:40
  166.9 3.9 %shard_map.27.before = f32[448,576]{1,0:T(8,128)S(1)} custom-call(s32[2]{0:T(128)S(1)} %pad_add_fusion.place, bf16[448,576]{1,0:T(8,128)(2,1)S(1)} %get-tuple-element.37.own, bf16[448,576]{1,0:T(8,128)(2,1)S(1)} %get-tuple-element.60.w_low, bf16[4,448,896]{2,1,0:T(8,128)(2,1)S(1)} %get-tuple-element.61.gram, bf16[504,512]{1,0:T(8,128)(2,1)S(1)} %get-tuple-element.62.refs_0_, ...), custom_call_target="tpu_custom_call" | custom-call | flops 1387266048 | bytes 6823936 | tf_op jit(solution)/shard_map/pallas_call | solution.py:62
  170.8 2.8 %shard_map.28.before = f32[448,576]{1,0:T(8,128)S(1)} custom-call(s32[2]{0:T(128)S(1)} %pad_add_fusion.place, f32[448,576]{1,0:T(8,128)S(1)} %shard_map.27.before, bf16[4,448,896]{2,1,0:T(8,128)(2,1)S(1)} %get-tuple-element.61.gram, bf16[504,512]{1,0:T(8,128)(2,1)S(1)} %collective-permute-done.32.r11, bf16[504,512]{1,0:T(8,128)(2,1)S(1)} %collective-permute-done.33.r31, ...), custom_call_target="tpu_custom_call" | custom-call | flops 924844032 | bytes 5791744 | tf_op jit(solution)/shard_map/pallas_call | solution.py:62
  173.6 2.0 %shard_map.29 = bf16[448,576]{1,0:T(8,128)(2,1)} custom-call(s32[2]{0:T(128)S(1)} %pad_add_fusion.place, f32[448,576]{1,0:T(8,128)S(1)} %shard_map.28.before, bf16[4,448,896]{2,1,0:T(8,128)(2,1)S(1)} %get-tuple-element.61.gram, bf16[256,512]{1,0:T(8,128)(2,1)S(1)} %collective-permute-done.34.refs_0_, bf16[248,512]{1,0:T(8,128)(2,1)S(1)} %collective-permute-done.35.refs_1_), custom_call_target="tpu_custom_call" | custom-call | flops 231211008 | bytes 4759552 | tf_op jit(solution)/shard_map/pallas_call | solution.py:62
  (33 shorter events, 0.9 us)
Async XLA Ops:
  0.1 1.1 copy-start
  1.8 13.6 %collective-permute-start.2 = (bf16[504,512]{1,0:T(8,128)(2,1)S(1)}, bf16[504,512]{1,0:T(8,128)(2,1)S(1)}, u32[]{:S(2)}, u32[]{:S(2)}) collective-permute-start(bf16[504,512]{1,0:T(8,128)(2,1)S(1)} %get-tuple-element.38.refs_0_), channel_id=1, source_target_pairs={{32,0},{0,32},{33,1},{1,33},{34,2},{2,34},{35,3},{3,35},{36,4},{4,... | collective-permute-start | bytes 1548296 | tf_op jit(solution)/shard_map/ppermute | solution.py:40
  3.4 14.4 %collective-permute-start.1 = (bf16[504,512]{1,0:T(8,128)(2,1)S(1)}, bf16[504,512]{1,0:T(8,128)(2,1)S(1)}, u32[]{:S(2)}, u32[]{:S(2)}) collective-permute-start(bf16[504,512]{1,0:T(8,128)(2,1)S(1)} %get-tuple-element.38.refs_0_), channel_id=1, source_target_pairs={{192,0},{0,64},{64,128},{128,192},{193,1},{1,65},{65,129},{129,193... | collective-permute-start | bytes 1548296 | tf_op jit(solution)/shard_map/ppermute | solution.py:40
  4.9 12.9 %collective-permute-start = (bf16[504,512]{1,0:T(8,128)(2,1)S(1)}, bf16[504,512]{1,0:T(8,128)(2,1)S(1)}, u32[]{:S(2)}, u32[]{:S(2)}) collective-permute-start(bf16[504,512]{1,0:T(8,128)(2,1)S(1)} %get-tuple-element.38.refs_0_), channel_id=1, source_target_pairs={{64,0},{128,64},{192,128},{0,192},{65,1},{129,65},{193,129},{1,193... | collective-permute-start | bytes 1548296 | tf_op jit(solution)/shard_map/ppermute | solution.py:40
  17.9 10.6 %collective-permute-start.5 = (bf16[256,512]{1,0:T(8,128)(2,1)S(1)}, bf16[256,512]{1,0:T(8,128)(2,1)S(1)}, u32[]{:S(2)}, u32[]{:S(2)}) collective-permute-start(bf16[256,512]{1,0:T(8,128)(2,1)S(1)} %slice.12), channel_id=1, source_target_pairs={{64,0},{128,64},{192,128},{0,192},{65,1},{129,65},{193,129},{1,193... | collective-permute-start | bytes 786440 | tf_op jit(solution)/shard_map/ppermute | solution.py:40
  20.9 7.6 %collective-permute-start.6 = (bf16[248,512]{1,0:T(8,128)(2,1)S(1)}, bf16[248,512]{1,0:T(8,128)(2,1)S(1)}, u32[]{:S(2)}, u32[]{:S(2)}) collective-permute-start(bf16[248,512]{1,0:T(8,128)(2,1)S(1)} %slice.13), channel_id=1, source_target_pairs={{192,0},{0,64},{64,128},{128,192},{193,1},{1,65},{65,129},{129,193... | collective-permute-start | bytes 761864 | tf_op jit(solution)/shard_map/ppermute | solution.py:40
  25.2 5.8 %collective-permute-start.8 = (bf16[8,56,896]{2,1,0:T(8,128)(2,1)S(1)}, bf16[8,56,896]{2,1,0:T(8,128)(2,1)S(1)}, u32[]{:S(2)}, u32[]{:S(2)}) collective-permute-start(bf16[8,56,896]{2,1,0:T(8,128)(2,1)S(1)} %get-tuple-element.44), channel_id=1, source_target_pairs={{1,0},{0,1},{3,2},{2,3},{5,4},{4,5},{7,6},{6,7},{9,8},{8,9},{11,10... | collective-permute-start | bytes 2408456 | tf_op jit(solution)/shard_map/ppermute | solution.py:40
  30.9 2.4 %collective-permute-start.9 = (bf16[8,56,896]{2,1,0:T(8,128)(2,1)S(1)}, bf16[8,56,896]{2,1,0:T(8,128)(2,1)S(1)}, u32[]{:S(2)}, u32[]{:S(2)}) collective-permute-start(bf16[8,56,896]{2,1,0:T(8,128)(2,1)S(1)} %get-tuple-element.47), channel_id=1, source_target_pairs={{1,0},{0,1},{3,2},{2,3},{5,4},{4,5},{7,6},{6,7},{9,8},{8,9},{11,10... | collective-permute-start | bytes 2408456 | tf_op jit(solution)/shard_map/ppermute | solution.py:40
  34.3 13.6 %collective-permute-start.10 = (bf16[112,896]{1,0:T(8,128)(2,1)S(1)}, bf16[112,896]{1,0:T(8,128)(2,1)S(1)}, u32[]{:S(2)}, u32[]{:S(2)}) collective-permute-start(bf16[112,896]{1,0:T(8,128)(2,1)S(1)} %get-tuple-element.51), channel_id=1, source_target_pairs={{28,0},{0,4},{4,8},{8,12},{12,16},{16,20},{20,24},{24,28},{29,1},{... | collective-permute-start | bytes 602120 | tf_op jit(solution)/shard_map/ppermute | solution.py:40
  37.5 15.7 %collective-permute-start.13 = (bf16[112,896]{1,0:T(8,128)(2,1)S(1)}, bf16[112,896]{1,0:T(8,128)(2,1)S(1)}, u32[]{:S(2)}, u32[]{:S(2)}) collective-permute-start(bf16[112,896]{1,0:T(8,128)(2,1)S(1)} %get-tuple-element.54), channel_id=1, source_target_pairs={{4,0},{8,4},{12,8},{16,12},{20,16},{24,20},{28,24},{0,28},{5,1},{9... | collective-permute-start | bytes 602120 | tf_op jit(solution)/shard_map/ppermute | solution.py:40
  37.5 23.1 %collective-permute-start.16 = (bf16[112,896]{1,0:T(8,128)(2,1)S(1)}, bf16[112,896]{1,0:T(8,128)(2,1)S(1)}, u32[]{:S(2)}, u32[]{:S(2)}) collective-permute-start(bf16[112,896]{1,0:T(8,128)(2,1)S(1)} %get-tuple-element.55), channel_id=1, source_target_pairs={{16,0},{20,4},{24,8},{28,12},{0,16},{4,20},{8,24},{12,28},{17,1},{... | collective-permute-start | bytes 602120 | tf_op jit(solution)/shard_map/ppermute | solution.py:40
  47.9 7.5 %collective-permute-start.11 = (bf16[112,896]{1,0:T(8,128)(2,1)S(1)}, bf16[112,896]{1,0:T(8,128)(2,1)S(1)}, u32[]{:S(2)}, u32[]{:S(2)}) collective-permute-start(bf16[112,896]{1,0:T(8,128)(2,1)S(1)} %add_convert_fusion.3), channel_id=1, source_target_pairs={{28,0},{0,4},{4,8},{8,12},{12,16},{16,20},{20,24},{24,28},{29,1},{... | collective-permute-start | bytes 602120 | tf_op jit(solution)/shard_map/ppermute | solution.py:40
  53.2 7.0 %collective-permute-start.14 = (bf16[112,896]{1,0:T(8,128)(2,1)S(1)}, bf16[112,896]{1,0:T(8,128)(2,1)S(1)}, u32[]{:S(2)}, u32[]{:S(2)}) collective-permute-start(bf16[112,896]{1,0:T(8,128)(2,1)S(1)} %add_convert_fusion.1), channel_id=1, source_target_pairs={{4,0},{8,4},{12,8},{16,12},{20,16},{24,20},{28,24},{0,28},{5,1},{9... | collective-permute-start | bytes 602120 | tf_op jit(solution)/shard_map/ppermute | solution.py:40
  55.5 7.0 %collective-permute-start.12 = (bf16[112,896]{1,0:T(8,128)(2,1)S(1)}, bf16[112,896]{1,0:T(8,128)(2,1)S(1)}, u32[]{:S(2)}, u32[]{:S(2)}) collective-permute-start(bf16[112,896]{1,0:T(8,128)(2,1)S(1)} %add_convert_fusion.2), channel_id=1, source_target_pairs={{28,0},{0,4},{4,8},{8,12},{12,16},{16,20},{20,24},{24,28},{29,1},{... | collective-permute-start | bytes 602120 | tf_op jit(solution)/shard_map/ppermute | solution.py:40
  60.3 7.2 %collective-permute-start.15 = (bf16[112,896]{1,0:T(8,128)(2,1)S(1)}, bf16[112,896]{1,0:T(8,128)(2,1)S(1)}, u32[]{:S(2)}, u32[]{:S(2)}) collective-permute-start(bf16[112,896]{1,0:T(8,128)(2,1)S(1)} %add_convert_fusion), channel_id=1, source_target_pairs={{4,0},{8,4},{12,8},{16,12},{20,16},{24,20},{28,24},{0,28},{5,1},{9... | collective-permute-start | bytes 602120 | tf_op jit(solution)/shard_map/ppermute | solution.py:40
  68.1 8.8 %collective-permute-start.17 = (bf16[112,896]{1,0:T(8,128)(2,1)S(1)}, bf16[112,896]{1,0:T(8,128)(2,1)S(1)}, u32[]{:S(2)}, u32[]{:S(2)}) collective-permute-start(bf16[112,896]{1,0:T(8,128)(2,1)S(1)} %get-tuple-element.56.mine), channel_id=1, source_target_pairs={{2,0},{0,2},{3,1},{1,3},{6,4},{4,6},{7,5},{5,7},{10,8},{8,10},{11,... | collective-permute-start | bytes 602120 | tf_op jit(solution)/shard_map/ppermute | solution.py:40
  71.1 5.8 %collective-permute-start.19 = (bf16[56,896]{1,0:T(8,128)(2,1)S(1)}, bf16[56,896]{1,0:T(8,128)(2,1)S(1)}, u32[]{:S(2)}, u32[]{:S(2)}) collective-permute-start(bf16[56,896]{1,0:T(8,128)(2,1)S(1)} %get-tuple-element.57), channel_id=1, source_target_pairs={{34,0},{32,2},{2,32},{0,34},{35,1},{33,3},{3,33},{1,35},{38,4},{36... | collective-permute-start | bytes 301064 | tf_op jit(solution)/shard_map/ppermute | solution.py:53
  71.3 5.6 %collective-permute-start.18 = (bf16[56,896]{1,0:T(8,128)(2,1)S(1)}, bf16[56,896]{1,0:T(8,128)(2,1)S(1)}, u32[]{:S(2)}, u32[]{:S(2)}) collective-permute-start(bf16[56,896]{1,0:T(8,128)(2,1)S(1)} %get-tuple-element.57), channel_id=1, source_target_pairs={{32,0},{0,32},{33,1},{1,33},{34,2},{2,34},{35,3},{3,35},{36,4},{4,... | collective-permute-start | bytes 301064 | tf_op jit(solution)/shard_map/ppermute | solution.py:40
  77.5 6.9 %collective-permute-start.24 = (bf16[112,896]{1,0:T(8,128)(2,1)S(1)}, bf16[112,896]{1,0:T(8,128)(2,1)S(1)}, u32[]{:S(2)}, u32[]{:S(2)}) collective-permute-start(bf16[112,896]{1,0:T(8,128)(2,1)S(1)} %shard_map.23.refs_0_), channel_id=1, source_target_pairs={{28,0},{0,4},{4,8},{8,12},{12,16},{16,20},{20,24},{24,28},{29,1},{... | collective-permute-start | bytes 602120 | tf_op jit(solution)/shard_map/ppermute | solution.py:40
  77.6 7.7 %collective-permute-start.20 = (bf16[112,896]{1,0:T(8,128)(2,1)S(1)}, bf16[112,896]{1,0:T(8,128)(2,1)S(1)}, u32[]{:S(2)}, u32[]{:S(2)}) collective-permute-start(bf16[112,896]{1,0:T(8,128)(2,1)S(1)} %shard_map.23.refs_0_), channel_id=1, source_target_pairs={{4,0},{8,4},{12,8},{16,12},{20,16},{24,20},{28,24},{0,28},{5,1},{9... | collective-permute-start | bytes 602120 | tf_op jit(solution)/shard_map/ppermute | solution.py:40
  84.5 10.8 %collective-permute-start.25 = (bf16[112,896]{1,0:T(8,128)(2,1)S(1)}, bf16[112,896]{1,0:T(8,128)(2,1)S(1)}, u32[]{:S(2)}, u32[]{:S(2)}) collective-permute-start(bf16[112,896]{1,0:T(8,128)(2,1)S(1)} %collective-permute-done.24.refs_7_), channel_id=1, source_target_pairs={{28,0},{0,4},{4,8},{8,12},{12,16},{16,20},{20,24},{24,28},{29,1},{... | collective-permute-start | bytes 602120 | tf_op jit(solution)/shard_map/ppermute | solution.py:40
  85.3 16.8 %collective-permute-start.21 = (bf16[112,896]{1,0:T(8,128)(2,1)S(1)}, bf16[112,896]{1,0:T(8,128)(2,1)S(1)}, u32[]{:S(2)}, u32[]{:S(2)}) collective-permute-start(bf16[112,896]{1,0:T(8,128)(2,1)S(1)} %collective-permute-done.20.refs_1_), channel_id=1, source_target_pairs={{4,0},{8,4},{12,8},{16,12},{20,16},{24,20},{28,24},{0,28},{5,1},{9... | collective-permute-start | bytes 602120 | tf_op jit(solution)/shard_map/ppermute | solution.py:40
  87.3 14.9 %collective-permute-start.23 = (bf16[112,896]{1,0:T(8,128)(2,1)S(1)}, bf16[112,896]{1,0:T(8,128)(2,1)S(1)}, u32[]{:S(2)}, u32[]{:S(2)}) collective-permute-start(bf16[112,896]{1,0:T(8,128)(2,1)S(1)} %shard_map.23.refs_0_), channel_id=1, source_target_pairs={{16,0},{20,4},{24,8},{28,12},{0,16},{4,20},{8,24},{12,28},{17,1},{... | collective-permute-start | bytes 602120 | tf_op jit(solution)/shard_map/ppermute | solution.py:40
  95.3 7.7 %collective-permute-start.26 = (bf16[112,896]{1,0:T(8,128)(2,1)S(1)}, bf16[112,896]{1,0:T(8,128)(2,1)S(1)}, u32[]{:S(2)}, u32[]{:S(2)}) collective-permute-start(bf16[112,896]{1,0:T(8,128)(2,1)S(1)} %collective-permute-done.25.refs_6_), channel_id=1, source_target_pairs={{28,0},{0,4},{4,8},{8,12},{12,16},{16,20},{20,24},{24,28},{29,1},{... | collective-permute-start | bytes 602120 | tf_op jit(solution)/shard_map/ppermute | solution.py:40
  102.1 6.9 %collective-permute-start.22 = (bf16[112,896]{1,0:T(8,128)(2,1)S(1)}, bf16[112,896]{1,0:T(8,128)(2,1)S(1)}, u32[]{:S(2)}, u32[]{:S(2)}) collective-permute-start(bf16[112,896]{1,0:T(8,128)(2,1)S(1)} %collective-permute-done.21.refs_2_), channel_id=1, source_target_pairs={{4,0},{8,4},{12,8},{16,12},{20,16},{24,20},{28,24},{0,28},{5,1},{9... | collective-permute-start | bytes 602120 | tf_op jit(solution)/shard_map/ppermute | solution.py:40
  109.7 21.3 %collective-permute-start.27 = (bf16[8,112,896]{2,1,0:T(8,128)(2,1)S(1)}, bf16[8,112,896]{2,1,0:T(8,128)(2,1)S(1)}, u32[]{:S(2)}, u32[]{:S(2)}) collective-permute-start(bf16[8,112,896]{2,1,0:T(8,128)(2,1)S(1)} %shard_map.24.group), channel_id=1, source_target_pairs={{1,0},{0,1},{3,2},{2,3},{5,4},{4,5},{7,6},{6,7},{9,8},{8,9},{11,10... | collective-permute-start | bytes 4816904 | tf_op jit(solution)/shard_map/ppermute | solution.py:40
  109.8 15.4 %collective-permute-start.4 = (bf16[504,512]{1,0:T(8,128)(2,1)S(1)}, bf16[504,512]{1,0:T(8,128)(2,1)S(1)}, u32[]{:S(2)}, u32[]{:S(2)}) collective-permute-start(bf16[504,512]{1,0:T(8,128)(2,1)S(1)} %collective-permute-done.2.refs_3_), channel_id=1, source_target_pairs={{192,0},{0,64},{64,128},{128,192},{193,1},{1,65},{65,129},{129,193... | collective-permute-start | bytes 1548296 | tf_op jit(solution)/shard_map/ppermute | solution.py:40
  109.9 15.3 %collective-permute-start.3 = (bf16[504,512]{1,0:T(8,128)(2,1)S(1)}, bf16[504,512]{1,0:T(8,128)(2,1)S(1)}, u32[]{:S(2)}, u32[]{:S(2)}) collective-permute-start(bf16[504,512]{1,0:T(8,128)(2,1)S(1)} %collective-permute-done.2.refs_3_), channel_id=1, source_target_pairs={{64,0},{128,64},{192,128},{0,192},{65,1},{129,65},{193,129},{1,193... | collective-permute-start | bytes 1548296 | tf_op jit(solution)/shard_map/ppermute | solution.py:40
  113.2 13.8 %collective-permute-start.7 = (bf16[504,512]{1,0:T(8,128)(2,1)S(1)}, bf16[504,512]{1,0:T(8,128)(2,1)S(1)}, u32[]{:S(2)}, u32[]{:S(2)}) collective-permute-start(bf16[504,512]{1,0:T(8,128)(2,1)S(1)} %pad_maximum_fusion), channel_id=1, source_target_pairs={{32,0},{0,32},{33,1},{1,33},{34,2},{2,34},{35,3},{3,35},{36,4},{4,... | collective-permute-start | bytes 1548296 | tf_op jit(solution)/shard_map/ppermute | solution.py:40
  134.1 12.7 %collective-permute-start.30 = (bf16[504,512]{1,0:T(8,128)(2,1)S(1)}, bf16[504,512]{1,0:T(8,128)(2,1)S(1)}, u32[]{:S(2)}, u32[]{:S(2)}) collective-permute-start(bf16[504,512]{1,0:T(8,128)(2,1)S(1)} %get-tuple-element.62.refs_0_), channel_id=1, source_target_pairs={{32,0},{0,32},{33,1},{1,33},{34,2},{2,34},{35,3},{3,35},{36,4},{4,... | collective-permute-start | bytes 1548296 | tf_op jit(solution)/shard_map/ppermute | solution.py:40
  134.5 13.9 %collective-permute-start.29 = (bf16[504,512]{1,0:T(8,128)(2,1)S(1)}, bf16[504,512]{1,0:T(8,128)(2,1)S(1)}, u32[]{:S(2)}, u32[]{:S(2)}) collective-permute-start(bf16[504,512]{1,0:T(8,128)(2,1)S(1)} %get-tuple-element.62.refs_0_), channel_id=1, source_target_pairs={{192,0},{0,64},{64,128},{128,192},{193,1},{1,65},{65,129},{129,193... | collective-permute-start | bytes 1548296 | tf_op jit(solution)/shard_map/ppermute | solution.py:40
  134.5 13.9 %collective-permute-start.28 = (bf16[504,512]{1,0:T(8,128)(2,1)S(1)}, bf16[504,512]{1,0:T(8,128)(2,1)S(1)}, u32[]{:S(2)}, u32[]{:S(2)}) collective-permute-start(bf16[504,512]{1,0:T(8,128)(2,1)S(1)} %get-tuple-element.62.refs_0_), channel_id=1, source_target_pairs={{64,0},{128,64},{192,128},{0,192},{65,1},{129,65},{193,129},{1,193... | collective-permute-start | bytes 1548296 | tf_op jit(solution)/shard_map/ppermute | solution.py:40
  148.4 12.0 %collective-permute-start.32 = (bf16[504,512]{1,0:T(8,128)(2,1)S(1)}, bf16[504,512]{1,0:T(8,128)(2,1)S(1)}, u32[]{:S(2)}, u32[]{:S(2)}) collective-permute-start(bf16[504,512]{1,0:T(8,128)(2,1)S(1)} %collective-permute-done.30.refs_3_), channel_id=1, source_target_pairs={{64,0},{128,64},{192,128},{0,192},{65,1},{129,65},{193,129},{1,193... | collective-permute-start | bytes 1548296 | tf_op jit(solution)/shard_map/ppermute | solution.py:40
  151.3 11.2 %collective-permute-start.33 = (bf16[504,512]{1,0:T(8,128)(2,1)S(1)}, bf16[504,512]{1,0:T(8,128)(2,1)S(1)}, u32[]{:S(2)}, u32[]{:S(2)}) collective-permute-start(bf16[504,512]{1,0:T(8,128)(2,1)S(1)} %collective-permute-done.29.refs_2_), channel_id=1, source_target_pairs={{32,0},{0,32},{33,1},{1,33},{34,2},{2,34},{35,3},{3,35},{36,4},{4,... | collective-permute-start | bytes 1548296 | tf_op jit(solution)/shard_map/ppermute | solution.py:40
  152.8 11.9 %collective-permute-start.31 = (bf16[504,512]{1,0:T(8,128)(2,1)S(1)}, bf16[504,512]{1,0:T(8,128)(2,1)S(1)}, u32[]{:S(2)}, u32[]{:S(2)}) collective-permute-start(bf16[504,512]{1,0:T(8,128)(2,1)S(1)} %collective-permute-done.29.refs_2_), channel_id=1, source_target_pairs={{192,0},{0,64},{64,128},{128,192},{193,1},{1,65},{65,129},{129,193... | collective-permute-start | bytes 1548296 | tf_op jit(solution)/shard_map/ppermute | solution.py:40
  164.7 8.9 %collective-permute-start.34 = (bf16[256,512]{1,0:T(8,128)(2,1)S(1)}, bf16[256,512]{1,0:T(8,128)(2,1)S(1)}, u32[]{:S(2)}, u32[]{:S(2)}) collective-permute-start(bf16[256,512]{1,0:T(8,128)(2,1)S(1)} %slice.14), channel_id=1, source_target_pairs={{64,0},{128,64},{192,128},{0,192},{65,1},{129,65},{193,129},{1,193... | collective-permute-start | bytes 786440 | tf_op jit(solution)/shard_map/ppermute | solution.py:40
  164.8 8.8 %collective-permute-start.35 = (bf16[248,512]{1,0:T(8,128)(2,1)S(1)}, bf16[248,512]{1,0:T(8,128)(2,1)S(1)}, u32[]{:S(2)}, u32[]{:S(2)}) collective-permute-start(bf16[248,512]{1,0:T(8,128)(2,1)S(1)} %slice.15), channel_id=1, source_target_pairs={{192,0},{0,64},{64,128},{128,192},{193,1},{1,65},{65,129},{129,193... | collective-permute-start | bytes 761864 | tf_op jit(solution)/shard_map/ppermute | solution.py:40

commit v4 on v3

--- a/solution.py
+++ b/solution.py
@@ -192,30 +192,40 @@
 
 def pair_body(place, low, low_other, high, high_other, *outs):
     size = low.shape[1]
-    for d, out in enumerate(outs):
-        out[:size] = (low[d].astype(F32) + low_other[d].astype(F32)).astype(BF16)
-        out[size:] = (high[d].astype(F32) + high_other[d].astype(F32)).astype(BF16)
+    for d in range(RING):
+        lower = (low[d].astype(F32) + low_other[d].astype(F32)).astype(BF16)
+        upper = (high[d].astype(F32) + high_other[d].astype(F32)).astype(BF16)
+        if d == FAR:
+            outs[d][...] = lower
+            outs[d + 1][...] = upper
+        else:
+            out = outs[d if d < FAR else d + 1]
+            out[:size] = lower
+            out[size:] = upper
 
 
 def add(a, b):
     return (a.astype(F32) + b.astype(F32)).astype(BF16)
 
 
-def ring_sum(place, part):
-    up, down = part[FAR - 1], part[FAR + 1]
-    far = shift(part[FAR], "z", FAR)
-    for step in range(FAR - 2, -1, -1):
+def ring_sum(place, part, up, down):
+    size = up.shape[0]
+    for step in range(FAR - 1, -1, -1):
         up = shift(up, "z", -1)
         down = shift(down, "z", 1)
-        if step > 0:
+        if step == 0:
+            return call(sum_body, place, (part[0], up, down), [array(part[0].shape), array((size, up.shape[1]))])
+        elif step == FAR - 1:
+            one, two = part[step], part[RING - step]
+            up = jnp.concatenate([add(one[:size], up), one[size:]], 0)
+            down = jnp.concatenate([two[:size], add(two[size:], down)], 0)
+        else:
             up, down = add(part[step], up), add(part[RING - step], down)
-    size, width = up.shape[0] // 2, up.shape[1]
-    return call(sum_body, place, (part[0], up, down, far), [array(up.shape), array((size, width))])
-
-
-def sum_body(place, near, up, down, far, mine, ahead):
+
+
+def sum_body(place, near, up, down, mine, ahead):
     size = ahead.shape[0]
-    total = near[...].astype(F32) + up[...].astype(F32) + down[...].astype(F32) + far[...].astype(F32)
+    total = near[...].astype(F32) + up[...].astype(F32) + down[...].astype(F32)
     mine[...] = total.astype(BF16)
     ahead[...] = total[size:].astype(BF16)
 
@@ -340,9 +350,10 @@
     r21 = jnp.concatenate(r20, 0)
     r21 = shift(r21, "yl", 1)
     panel = call(panel_body, place, (low, r11, r31, r21, *r20), array((4, 2 * rows, cols)), 0, [room(2)])
-    two = array((2 * size, 2 * rows))
-    parts = call(pair_body, place, halves, [two] * RING)
-    mine, ahead = ring_sum(place, parts)
+    one, two = array((size, 2 * rows)), array((2 * size, 2 * rows))
+    parts = call(pair_body, place, halves, [two] * FAR + [one] * 2 + [two] * (FAR - 1))
+    part = {d: parts[d if d < FAR else d + 1] for d in range(RING) if d != FAR}
+    mine, ahead = ring_sum(place, part, parts[FAR], parts[FAR + 1])
     across = shift(mine, "yh", 1)
     same = shift(ahead, "yl", 1)
     cross = fetch(ahead, ("yl", "yh"), lambda y, h: (y + 1, h + 1))

time: 176 us -> 174 us (0.989)
  the two profiles are of different devices: /device:TPU:96 before, /device:TPU:1 now
where the time goes in v4:
time: 174 us; the launch traced here: 172 us
  waiting for transfers between devices  74.4 us (43%)
  starting transfers between devices  69.6 us (40%)
  Pallas kernels  25.8 us (15%)
    ppermute x36, waiting for transfers between devices, shift(): lax.ppermute(value, axis, [((i + step) % size, i) for i in range(size)])  69.7 us
    ppermute x36, starting transfers between devices, shift(): lax.ppermute(value, axis, [((i + step) % size, i) for i in range(size)])  69.6 us
    pallas_call x13, Pallas kernels, call(): pl.pallas_call(body, out_shape=outs if home else [pltpu.VMEM(o.shape, o.d...  25.8 us
    ppermute x1, waiting for transfers between devices, fetch(): lax.ppermute(value, axes, [(flat(source(*p)), flat(p)) for p in places])  4.67 us
  transfers between devices with their start and end apart: 37, of which 21 were waited for; matrix products, arithmetic and copies ran while one was open for 0% of the time, Pallas kernels for 10%

profile of v4, /device:TPU:1, one launch (start us, length us, event | category | flops | bytes accessed | tf_op | source)
XLA Modules:
  0.0 171.6 jit_solution(14568184078258368973)
XLA Ops:
  0.1 1.1 copy-done
  1.1 0.6 shard_map.17
  1.8 2.2 %collective-permute-start.2 = (bf16[504,512]{1,0:T(8,128)(2,1)S(1)}, bf16[504,512]{1,0:T(8,128)(2,1)S(1)}, u32[]{:S(2)}, u32[]{:S(2)}) collective-permute-start(bf16[504,512]{1,0:T(8,128)(2,1)S(1)} %get-tuple-element.39.refs_0_), channel_id=1, source_target_pairs={{32,0},{0,32},{33,1},{1,33},{34,2},{2,34},{35,3},{3,35},{36,4},{4,... | collective-permute-start | bytes 1548296 | tf_op jit(solution)/shard_map/ppermute | solution.py:40
  4.0 1.2 collective-permute-start.1
  5.2 1.5 collective-permute-start
  6.7 7.6 %collective-permute-done.2.refs_3_ = bf16[504,512]{1,0:T(8,128)(2,1)S(1)} collective-permute-done((bf16[504,512]{1,0:T(8,128)(2,1)S(1)}, bf16[504,512]{1,0:T(8,128)(2,1)S(1)}, u32[]{:S(2)}, u32[]{:S(2)}) %collective-permute-start.2) | collective-permute-done | bytes 516128 | tf_op jit(solution)/shard_map/ppermute | solution.py:40
  14.3 3.0 %collective-permute-done.1.refs_2_ = bf16[504,512]{1,0:T(8,128)(2,1)S(1)} collective-permute-done((bf16[504,512]{1,0:T(8,128)(2,1)S(1)}, bf16[504,512]{1,0:T(8,128)(2,1)S(1)}, u32[]{:S(2)}, u32[]{:S(2)}) %collective-permute-start.1) | collective-permute-done | bytes 516128 | tf_op jit(solution)/shard_map/ppermute | solution.py:40
  17.3 2.5 %collective-permute-start.5 = (bf16[256,512]{1,0:T(8,128)(2,1)S(1)}, bf16[256,512]{1,0:T(8,128)(2,1)S(1)}, u32[]{:S(2)}, u32[]{:S(2)}) collective-permute-start(bf16[256,512]{1,0:T(8,128)(2,1)S(1)} %slice.24), channel_id=1, source_target_pairs={{64,0},{128,64},{192,128},{0,192},{65,1},{129,65},{193,129},{1,193... | collective-permute-start | bytes 786440 | tf_op jit(solution)/shard_map/ppermute | solution.py:40
  19.8 0.1 collective-permute-start.6
  19.9 4.2 %shard_map.18 = (bf16[8,56,896]{2,1,0:T(8,128)(2,1)S(1)}, bf16[8,56,896]{2,1,0:T(8,128)(2,1)S(1)}, bf16[3,896,576]{2,1,0:T(8,128)(2,1)S(1)}, f32[448,896]{1,0:T(8,128)S(1)}) custom-call(s32[2]{0:T(128)S(1)} %pad_add_fusion.place, bf16[448,576]{1,0:T(8,128)(2,1)S(1)} %get-tuple-element.38.own, bf16[504,512]{1,0:T(8,128)(2,1)S(1)} %get-tuple-element.39.refs_0_, ...), custom_call_target="tpu_custom_call" | custom-call | flops 1387266048 | bytes 8085504 | tf_op jit(solution)/shard_map/pallas_call | solution.py:62
  24.1 2.7 %collective-permute-start.8 = (bf16[8,56,896]{2,1,0:T(8,128)(2,1)S(1)}, bf16[8,56,896]{2,1,0:T(8,128)(2,1)S(1)}, u32[]{:S(2)}, u32[]{:S(2)}) collective-permute-start(bf16[8,56,896]{2,1,0:T(8,128)(2,1)S(1)} %get-tuple-element.45), channel_id=1, source_target_pairs={{1,0},{0,1},{3,2},{2,3},{5,4},{4,5},{7,6},{6,7},{9,8},{8,9},{11,10... | collective-permute-start | bytes 2408456 | tf_op jit(solution)/shard_map/ppermute | solution.py:40
  26.8 2.4 %shard_map.20 = (bf16[8,56,896]{2,1,0:T(8,128)(2,1)S(1)}, bf16[8,56,896]{2,1,0:T(8,128)(2,1)S(1)}) custom-call(s32[2]{0:T(128)S(1)} %pad_add_fusion.place, bf16[448,576]{1,0:T(8,128)(2,1)S(1)} %get-tuple-element.38.own, bf16[3,896,576]{2,1,0:T(8,128)(2,1)S(1)} %get-tuple-element.43.low, f32[448,896]{1,0:T(8,128)S(1)} %get-tuple-element.46.partner, ...), custom_call_target="tpu_custom_call" | custom-call | flops 462422016 | bytes 6537216 | tf_op jit(solution)/shard_map/pallas_call | solution.py:62
  29.2 3.3 %collective-permute-start.9 = (bf16[8,56,896]{2,1,0:T(8,128)(2,1)S(1)}, bf16[8,56,896]{2,1,0:T(8,128)(2,1)S(1)}, u32[]{:S(2)}, u32[]{:S(2)}) collective-permute-start(bf16[8,56,896]{2,1,0:T(8,128)(2,1)S(1)} %get-tuple-element.48), channel_id=1, source_target_pairs={{1,0},{0,1},{3,2},{2,3},{5,4},{4,5},{7,6},{6,7},{9,8},{8,9},{11,10... | collective-permute-start | bytes 2408456 | tf_op jit(solution)/shard_map/ppermute | solution.py:40
  32.5 1.9 %collective-permute-done.9.high_other = bf16[8,56,896]{2,1,0:T(8,128)(2,1)S(1)} collective-permute-done((bf16[8,56,896]{2,1,0:T(8,128)(2,1)S(1)}, bf16[8,56,896]{2,1,0:T(8,128)(2,1)S(1)}, u32[]{:S(2)}, u32[]{:S(2)}) %collective-permute-start.9) | collective-permute-done | bytes 802848 | tf_op jit(solution)/shard_map/ppermute | solution.py:40
  34.5 0.9 shard_map.21
  35.4 5.7 %collective-permute-start.14 = (bf16[56,896]{1,0:T(8,128)(2,1)S(1)}, bf16[56,896]{1,0:T(8,128)(2,1)S(1)}, u32[]{:S(2)}, u32[]{:S(2)}) collective-permute-start(bf16[56,896]{1,0:T(8,128)(2,1)S(1)} %get-tuple-element.57), channel_id=1, source_target_pairs={{4,0},{8,4},{12,8},{16,12},{20,16},{24,20},{28,24},{0,28},{5,1},{9... | collective-permute-start | bytes 301064 | tf_op jit(solution)/shard_map/ppermute | solution.py:40
  41.1 0.1 collective-permute-start.10
  41.2 1.7 collective-permute-done.14
  42.9 3.5 %collective-permute-start.15 = (bf16[112,896]{1,0:T(8,128)(2,1)S(1)}, bf16[112,896]{1,0:T(8,128)(2,1)S(1)}, u32[]{:S(2)}, u32[]{:S(2)}) collective-permute-start(bf16[112,896]{1,0:T(8,128)(2,1)S(1)} %pad_maximum_fusion.2), channel_id=1, source_target_pairs={{4,0},{8,4},{12,8},{16,12},{20,16},{24,20},{28,24},{0,28},{5,1},{9... | collective-permute-start | bytes 602120 | tf_op jit(solution)/shard_map/ppermute | solution.py:40
  46.5 0.1 collective-permute-start.11
  46.6 3.0 %collective-permute-done.15 = bf16[112,896]{1,0:T(8,128)(2,1)S(1)} collective-permute-done((bf16[112,896]{1,0:T(8,128)(2,1)S(1)}, bf16[112,896]{1,0:T(8,128)(2,1)S(1)}, u32[]{:S(2)}, u32[]{:S(2)}) %collective-permute-start.15) | collective-permute-done | bytes 200736 | tf_op jit(solution)/shard_map/ppermute | solution.py:40
  49.6 3.5 %collective-permute-start.16 = (bf16[112,896]{1,0:T(8,128)(2,1)S(1)}, bf16[112,896]{1,0:T(8,128)(2,1)S(1)}, u32[]{:S(2)}, u32[]{:S(2)}) collective-permute-start(bf16[112,896]{1,0:T(8,128)(2,1)S(1)} %add_convert_fusion.1), channel_id=1, source_target_pairs={{4,0},{8,4},{12,8},{16,12},{20,16},{24,20},{28,24},{0,28},{5,1},{9... | collective-permute-start | bytes 602120 | tf_op jit(solution)/shard_map/ppermute | solution.py:40
  53.1 0.3 collective-permute-start.12
  53.4 2.3 %collective-permute-done.16 = bf16[112,896]{1,0:T(8,128)(2,1)S(1)} collective-permute-done((bf16[112,896]{1,0:T(8,128)(2,1)S(1)}, bf16[112,896]{1,0:T(8,128)(2,1)S(1)}, u32[]{:S(2)}, u32[]{:S(2)}) %collective-permute-start.16) | collective-permute-done | bytes 200736 | tf_op jit(solution)/shard_map/ppermute | solution.py:40
  55.8 3.2 %collective-permute-start.17 = (bf16[112,896]{1,0:T(8,128)(2,1)S(1)}, bf16[112,896]{1,0:T(8,128)(2,1)S(1)}, u32[]{:S(2)}, u32[]{:S(2)}) collective-permute-start(bf16[112,896]{1,0:T(8,128)(2,1)S(1)} %add_convert_fusion), channel_id=1, source_target_pairs={{4,0},{8,4},{12,8},{16,12},{20,16},{24,20},{28,24},{0,28},{5,1},{9... | collective-permute-start | bytes 602120 | tf_op jit(solution)/shard_map/ppermute | solution.py:40
  59.0 0.2 collective-permute-done.12
  59.2 0.1 collective-permute-start.13
  59.3 2.3 %collective-permute-done.17.down = bf16[112,896]{1,0:T(8,128)(2,1)S(1)} collective-permute-done((bf16[112,896]{1,0:T(8,128)(2,1)S(1)}, bf16[112,896]{1,0:T(8,128)(2,1)S(1)}, u32[]{:S(2)}, u32[]{:S(2)}) %collective-permute-start.17) | collective-permute-done | bytes 200736 | tf_op jit(solution)/shard_map/ppermute | solution.py:40
  61.6 3.4 %collective-permute-done.13.up = bf16[112,896]{1,0:T(8,128)(2,1)S(1)} collective-permute-done((bf16[112,896]{1,0:T(8,128)(2,1)S(1)}, bf16[112,896]{1,0:T(8,128)(2,1)S(1)}, u32[]{:S(2)}, u32[]{:S(2)}) %collective-permute-start.13) | collective-permute-done | bytes 200736 | tf_op jit(solution)/shard_map/ppermute | solution.py:40
  65.1 0.6 shard_map.22
  65.7 2.7 %collective-permute-start.18 = (bf16[112,896]{1,0:T(8,128)(2,1)S(1)}, bf16[112,896]{1,0:T(8,128)(2,1)S(1)}, u32[]{:S(2)}, u32[]{:S(2)}) collective-permute-start(bf16[112,896]{1,0:T(8,128)(2,1)S(1)} %get-tuple-element.58.mine), channel_id=1, source_target_pairs={{2,0},{0,2},{3,1},{1,3},{6,4},{4,6},{7,5},{5,7},{10,8},{8,10},{11,... | collective-permute-start | bytes 602120 | tf_op jit(solution)/shard_map/ppermute | solution.py:40
  68.4 4.7 %collective-permute-done.20.cross = bf16[56,896]{1,0:T(8,128)(2,1)S(1)} collective-permute-done((bf16[56,896]{1,0:T(8,128)(2,1)S(1)}, bf16[56,896]{1,0:T(8,128)(2,1)S(1)}, u32[]{:S(2)}, u32[]{:S(2)}) %collective-permute-start.20) | collective-permute-done | bytes 100384 | tf_op jit(solution)/shard_map/ppermute | solution.py:53
  73.1 0.6 shard_map.23.refs_0_
  73.7 0.1 collective-permute-start.25
  73.8 2.7 %collective-permute-start.21 = (bf16[112,896]{1,0:T(8,128)(2,1)S(1)}, bf16[112,896]{1,0:T(8,128)(2,1)S(1)}, u32[]{:S(2)}, u32[]{:S(2)}) collective-permute-start(bf16[112,896]{1,0:T(8,128)(2,1)S(1)} %shard_map.23.refs_0_), channel_id=1, source_target_pairs={{4,0},{8,4},{12,8},{16,12},{20,16},{24,20},{28,24},{0,28},{5,1},{9... | collective-permute-start | bytes 602120 | tf_op jit(solution)/shard_map/ppermute | solution.py:40
  76.5 3.1 %collective-permute-done.25.refs_7_ = bf16[112,896]{1,0:T(8,128)(2,1)S(1)} collective-permute-done((bf16[112,896]{1,0:T(8,128)(2,1)S(1)}, bf16[112,896]{1,0:T(8,128)(2,1)S(1)}, u32[]{:S(2)}, u32[]{:S(2)}) %collective-permute-start.25) | collective-permute-done | bytes 200736 | tf_op jit(solution)/shard_map/ppermute | solution.py:40
  79.6 2.7 %collective-permute-start.22 = (bf16[112,896]{1,0:T(8,128)(2,1)S(1)}, bf16[112,896]{1,0:T(8,128)(2,1)S(1)}, u32[]{:S(2)}, u32[]{:S(2)}) collective-permute-start(bf16[112,896]{1,0:T(8,128)(2,1)S(1)} %collective-permute-done.21.refs_1_), channel_id=1, source_target_pairs={{4,0},{8,4},{12,8},{16,12},{20,16},{24,20},{28,24},{0,28},{5,1},{9... | collective-permute-start | bytes 602120 | tf_op jit(solution)/shard_map/ppermute | solution.py:40
  82.3 1.7 collective-permute-start.24
  84.0 5.2 %collective-permute-done.26.refs_6_ = bf16[112,896]{1,0:T(8,128)(2,1)S(1)} collective-permute-done((bf16[112,896]{1,0:T(8,128)(2,1)S(1)}, bf16[112,896]{1,0:T(8,128)(2,1)S(1)}, u32[]{:S(2)}, u32[]{:S(2)}) %collective-permute-start.26) | collective-permute-done | bytes 200736 | tf_op jit(solution)/shard_map/ppermute | solution.py:40
  89.2 3.7 %collective-permute-start.23 = (bf16[112,896]{1,0:T(8,128)(2,1)S(1)}, bf16[112,896]{1,0:T(8,128)(2,1)S(1)}, u32[]{:S(2)}, u32[]{:S(2)}) collective-permute-start(bf16[112,896]{1,0:T(8,128)(2,1)S(1)} %collective-permute-done.22.refs_2_), channel_id=1, source_target_pairs={{4,0},{8,4},{12,8},{16,12},{20,16},{24,20},{28,24},{0,28},{5,1},{9... | collective-permute-start | bytes 602120 | tf_op jit(solution)/shard_map/ppermute | solution.py:40
  92.8 2.1 %collective-permute-done.27.refs_5_ = bf16[112,896]{1,0:T(8,128)(2,1)S(1)} collective-permute-done((bf16[112,896]{1,0:T(8,128)(2,1)S(1)}, bf16[112,896]{1,0:T(8,128)(2,1)S(1)}, u32[]{:S(2)}, u32[]{:S(2)}) %collective-permute-start.27) | collective-permute-done | bytes 200736 | tf_op jit(solution)/shard_map/ppermute | solution.py:40
  95.0 0.5 collective-permute-done.23.refs_3_
  95.5 0.7 shard_map.24.group
  96.2 14.6 %collective-permute-start.28 = (bf16[8,112,896]{2,1,0:T(8,128)(2,1)S(1)}, bf16[8,112,896]{2,1,0:T(8,128)(2,1)S(1)}, u32[]{:S(2)}, u32[]{:S(2)}) collective-permute-start(bf16[8,112,896]{2,1,0:T(8,128)(2,1)S(1)} %shard_map.24.group), channel_id=1, source_target_pairs={{1,0},{0,1},{3,2},{2,3},{5,4},{4,5},{7,6},{6,7},{9,8},{8,9},{11,10... | collective-permute-start | bytes 4816904 | tf_op jit(solution)/shard_map/ppermute | solution.py:40
  110.8 2.7 %collective-permute-start.3 = (bf16[504,512]{1,0:T(8,128)(2,1)S(1)}, bf16[504,512]{1,0:T(8,128)(2,1)S(1)}, u32[]{:S(2)}, u32[]{:S(2)}) collective-permute-start(bf16[504,512]{1,0:T(8,128)(2,1)S(1)} %collective-permute-done.2.refs_3_), channel_id=1, source_target_pairs={{64,0},{128,64},{192,128},{0,192},{65,1},{129,65},{193,129},{1,193... | collective-permute-start | bytes 1548296 | tf_op jit(solution)/shard_map/ppermute | solution.py:40
  113.5 0.9 collective-permute-start.7
  114.4 10.8 %collective-permute-done.4.refs_1_ = bf16[504,512]{1,0:T(8,128)(2,1)S(1)} collective-permute-done((bf16[504,512]{1,0:T(8,128)(2,1)S(1)}, bf16[504,512]{1,0:T(8,128)(2,1)S(1)}, u32[]{:S(2)}, u32[]{:S(2)}) %collective-permute-start.4) | collective-permute-done | bytes 516128 | tf_op jit(solution)/shard_map/ppermute | solution.py:40
  125.2 1.2 collective-permute-done.7.refs_2_
  126.5 1.5 shard_map.19.panel
  127.9 2.6 %shard_map.25 = (bf16[4,448,896]{2,1,0:T(8,128)(2,1)S(1)}, f32[448,576]{1,0:T(8,128)S(1)}) custom-call(s32[2]{0:T(128)S(1)} %pad_add_fusion.place, bf16[4,896,576]{2,1,0:T(8,128)(2,1)S(1)} %shard_map.19.panel, bf16[8,112,896]{2,1,0:T(8,128)(2,1)S(1)} %shard_map.24.group), custom_call_target="tpu_custom_call" | custom-call | flops 924844032 | bytes 9461760 | tf_op jit(solution)/shard_map/pallas_call | solution.py:62
  130.5 3.1 %shard_map.26 = (bf16[4,448,896]{2,1,0:T(8,128)(2,1)S(1)}, bf16[504,512]{1,0:T(8,128)(2,1)S(1)}, bf16[448,576]{1,0:T(8,128)(2,1)S(1)}) custom-call(s32[2]{0:T(128)S(1)} %pad_add_fusion.place, bf16[448,576]{1,0:T(8,128)(2,1)S(1)} %get-tuple-element.38.own, bf16[4,896,576]{2,1,0:T(8,128)(2,1)S(1)} %shard_map.19.panel, ...), custom_call_target="tpu_custom_call", output_to_operand_aliasing={{0}: (4, {})} | custom-call | flops 924844032 | bytes 14221312 | tf_op jit(solution)/shard_map/pallas_call | solution.py:62
  133.6 0.6 collective-permute-start.31
  134.2 2.7 %collective-permute-start.29 = (bf16[504,512]{1,0:T(8,128)(2,1)S(1)}, bf16[504,512]{1,0:T(8,128)(2,1)S(1)}, u32[]{:S(2)}, u32[]{:S(2)}) collective-permute-start(bf16[504,512]{1,0:T(8,128)(2,1)S(1)} %get-tuple-element.64.refs_0_), channel_id=1, source_target_pairs={{64,0},{128,64},{192,128},{0,192},{65,1},{129,65},{193,129},{1,193... | collective-permute-start | bytes 1548296 | tf_op jit(solution)/shard_map/ppermute | solution.py:40
  136.9 8.6 %collective-permute-done.31.refs_3_ = bf16[504,512]{1,0:T(8,128)(2,1)S(1)} collective-permute-done((bf16[504,512]{1,0:T(8,128)(2,1)S(1)}, bf16[504,512]{1,0:T(8,128)(2,1)S(1)}, u32[]{:S(2)}, u32[]{:S(2)}) %collective-permute-start.31) | collective-permute-done | bytes 516128 | tf_op jit(solution)/shard_map/ppermute | solution.py:40
  145.5 1.5 collective-permute-done.30.refs_2_
  147.0 2.4 %collective-permute-start.33 = (bf16[504,512]{1,0:T(8,128)(2,1)S(1)}, bf16[504,512]{1,0:T(8,128)(2,1)S(1)}, u32[]{:S(2)}, u32[]{:S(2)}) collective-permute-start(bf16[504,512]{1,0:T(8,128)(2,1)S(1)} %collective-permute-done.31.refs_3_), channel_id=1, source_target_pairs={{64,0},{128,64},{192,128},{0,192},{65,1},{129,65},{193,129},{1,193... | collective-permute-start | bytes 1548296 | tf_op jit(solution)/shard_map/ppermute | solution.py:40
  149.4 0.9 collective-permute-start.34
  150.3 7.4 %collective-permute-done.33.r11 = bf16[504,512]{1,0:T(8,128)(2,1)S(1)} collective-permute-done((bf16[504,512]{1,0:T(8,128)(2,1)S(1)}, bf16[504,512]{1,0:T(8,128)(2,1)S(1)}, u32[]{:S(2)}, u32[]{:S(2)}) %collective-permute-start.33) | collective-permute-done | bytes 516128 | tf_op jit(solution)/shard_map/ppermute | solution.py:40
  157.6 1.8 %collective-permute-done.34.r31 = bf16[504,512]{1,0:T(8,128)(2,1)S(1)} collective-permute-done((bf16[504,512]{1,0:T(8,128)(2,1)S(1)}, bf16[504,512]{1,0:T(8,128)(2,1)S(1)}, u32[]{:S(2)}, u32[]{:S(2)}) %collective-permute-start.34) | collective-permute-done | bytes 516128 | tf_op jit(solution)/shard_map/ppermute | solution.py:40
  159.5 1.8 %collective-permute-done.32.r20 = bf16[504,512]{1,0:T(8,128)(2,1)S(1)} collective-permute-done((bf16[504,512]{1,0:T(8,128)(2,1)S(1)}, bf16[504,512]{1,0:T(8,128)(2,1)S(1)}, u32[]{:S(2)}, u32[]{:S(2)}) %collective-permute-start.32) | collective-permute-done | bytes 516128 | tf_op jit(solution)/shard_map/ppermute | solution.py:40
  161.4 1.5 collective-permute-start.36
  163.0 3.9 %shard_map.27.before = f32[448,576]{1,0:T(8,128)S(1)} custom-call(s32[2]{0:T(128)S(1)} %pad_add_fusion.place, bf16[448,576]{1,0:T(8,128)(2,1)S(1)} %get-tuple-element.38.own, bf16[448,576]{1,0:T(8,128)(2,1)S(1)} %get-tuple-element.62.w_low, bf16[4,448,896]{2,1,0:T(8,128)(2,1)S(1)} %get-tuple-element.63.gram, bf16[504,512]{1,0:T(8,128)(2,1)S(1)} %get-tuple-element.64.refs_0_, ...), custom_call_target="tpu_custom_call" | custom-call | flops 1387266048 | bytes 6823936 | tf_op jit(solution)/shard_map/pallas_call | solution.py:62
  166.9 2.8 %shard_map.28.before = f32[448,576]{1,0:T(8,128)S(1)} custom-call(s32[2]{0:T(128)S(1)} %pad_add_fusion.place, f32[448,576]{1,0:T(8,128)S(1)} %shard_map.27.before, bf16[4,448,896]{2,1,0:T(8,128)(2,1)S(1)} %get-tuple-element.63.gram, bf16[504,512]{1,0:T(8,128)(2,1)S(1)} %collective-permute-done.33.r11, bf16[504,512]{1,0:T(8,128)(2,1)S(1)} %collective-permute-done.34.r31, ...), custom_call_target="tpu_custom_call" | custom-call | flops 924844032 | bytes 5791744 | tf_op jit(solution)/shard_map/pallas_call | solution.py:62
  169.7 2.0 %shard_map.29 = bf16[448,576]{1,0:T(8,128)(2,1)} custom-call(s32[2]{0:T(128)S(1)} %pad_add_fusion.place, f32[448,576]{1,0:T(8,128)S(1)} %shard_map.28.before, bf16[4,448,896]{2,1,0:T(8,128)(2,1)S(1)} %get-tuple-element.63.gram, bf16[256,512]{1,0:T(8,128)(2,1)S(1)} %collective-permute-done.35.refs_0_, bf16[248,512]{1,0:T(8,128)(2,1)S(1)} %collective-permute-done.36.refs_1_), custom_call_target="tpu_custom_call" | custom-call | flops 231211008 | bytes 4759552 | tf_op jit(solution)/shard_map/pallas_call | solution.py:62
  (41 shorter events, 0.7 us)
Async XLA Ops:
  0.1 1.1 copy-start
  1.8 12.5 %collective-permute-start.2 = (bf16[504,512]{1,0:T(8,128)(2,1)S(1)}, bf16[504,512]{1,0:T(8,128)(2,1)S(1)}, u32[]{:S(2)}, u32[]{:S(2)}) collective-permute-start(bf16[504,512]{1,0:T(8,128)(2,1)S(1)} %get-tuple-element.39.refs_0_), channel_id=1, source_target_pairs={{32,0},{0,32},{33,1},{1,33},{34,2},{2,34},{35,3},{3,35},{36,4},{4,... | collective-permute-start | bytes 1548296 | tf_op jit(solution)/shard_map/ppermute | solution.py:40
  4.0 13.3 %collective-permute-start.1 = (bf16[504,512]{1,0:T(8,128)(2,1)S(1)}, bf16[504,512]{1,0:T(8,128)(2,1)S(1)}, u32[]{:S(2)}, u32[]{:S(2)}) collective-permute-start(bf16[504,512]{1,0:T(8,128)(2,1)S(1)} %get-tuple-element.39.refs_0_), channel_id=1, source_target_pairs={{192,0},{0,64},{64,128},{128,192},{193,1},{1,65},{65,129},{129,193... | collective-permute-start | bytes 1548296 | tf_op jit(solution)/shard_map/ppermute | solution.py:40
  5.2 12.1 %collective-permute-start = (bf16[504,512]{1,0:T(8,128)(2,1)S(1)}, bf16[504,512]{1,0:T(8,128)(2,1)S(1)}, u32[]{:S(2)}, u32[]{:S(2)}) collective-permute-start(bf16[504,512]{1,0:T(8,128)(2,1)S(1)} %get-tuple-element.39.refs_0_), channel_id=1, source_target_pairs={{64,0},{128,64},{192,128},{0,192},{65,1},{129,65},{193,129},{1,193... | collective-permute-start | bytes 1548296 | tf_op jit(solution)/shard_map/ppermute | solution.py:40
  17.3 9.5 %collective-permute-start.5 = (bf16[256,512]{1,0:T(8,128)(2,1)S(1)}, bf16[256,512]{1,0:T(8,128)(2,1)S(1)}, u32[]{:S(2)}, u32[]{:S(2)}) collective-permute-start(bf16[256,512]{1,0:T(8,128)(2,1)S(1)} %slice.24), channel_id=1, source_target_pairs={{64,0},{128,64},{192,128},{0,192},{65,1},{129,65},{193,129},{1,193... | collective-permute-start | bytes 786440 | tf_op jit(solution)/shard_map/ppermute | solution.py:40
  19.8 7.0 %collective-permute-start.6 = (bf16[248,512]{1,0:T(8,128)(2,1)S(1)}, bf16[248,512]{1,0:T(8,128)(2,1)S(1)}, u32[]{:S(2)}, u32[]{:S(2)}) collective-permute-start(bf16[248,512]{1,0:T(8,128)(2,1)S(1)} %slice.25), channel_id=1, source_target_pairs={{192,0},{0,64},{64,128},{128,192},{193,1},{1,65},{65,129},{129,193... | collective-permute-start | bytes 761864 | tf_op jit(solution)/shard_map/ppermute | solution.py:40
  24.1 8.4 %collective-permute-start.8 = (bf16[8,56,896]{2,1,0:T(8,128)(2,1)S(1)}, bf16[8,56,896]{2,1,0:T(8,128)(2,1)S(1)}, u32[]{:S(2)}, u32[]{:S(2)}) collective-permute-start(bf16[8,56,896]{2,1,0:T(8,128)(2,1)S(1)} %get-tuple-element.45), channel_id=1, source_target_pairs={{1,0},{0,1},{3,2},{2,3},{5,4},{4,5},{7,6},{6,7},{9,8},{8,9},{11,10... | collective-permute-start | bytes 2408456 | tf_op jit(solution)/shard_map/ppermute | solution.py:40
  29.2 5.2 %collective-permute-start.9 = (bf16[8,56,896]{2,1,0:T(8,128)(2,1)S(1)}, bf16[8,56,896]{2,1,0:T(8,128)(2,1)S(1)}, u32[]{:S(2)}, u32[]{:S(2)}) collective-permute-start(bf16[8,56,896]{2,1,0:T(8,128)(2,1)S(1)} %get-tuple-element.48), channel_id=1, source_target_pairs={{1,0},{0,1},{3,2},{2,3},{5,4},{4,5},{7,6},{6,7},{9,8},{8,9},{11,10... | collective-permute-start | bytes 2408456 | tf_op jit(solution)/shard_map/ppermute | solution.py:40
  35.4 7.5 %collective-permute-start.14 = (bf16[56,896]{1,0:T(8,128)(2,1)S(1)}, bf16[56,896]{1,0:T(8,128)(2,1)S(1)}, u32[]{:S(2)}, u32[]{:S(2)}) collective-permute-start(bf16[56,896]{1,0:T(8,128)(2,1)S(1)} %get-tuple-element.57), channel_id=1, source_target_pairs={{4,0},{8,4},{12,8},{16,12},{20,16},{24,20},{28,24},{0,28},{5,1},{9... | collective-permute-start | bytes 301064 | tf_op jit(solution)/shard_map/ppermute | solution.py:40
  41.1 5.3 %collective-permute-start.10 = (bf16[56,896]{1,0:T(8,128)(2,1)S(1)}, bf16[56,896]{1,0:T(8,128)(2,1)S(1)}, u32[]{:S(2)}, u32[]{:S(2)}) collective-permute-start(bf16[56,896]{1,0:T(8,128)(2,1)S(1)} %get-tuple-element.53), channel_id=1, source_target_pairs={{28,0},{0,4},{4,8},{8,12},{12,16},{16,20},{20,24},{24,28},{29,1},{... | collective-permute-start | bytes 301064 | tf_op jit(solution)/shard_map/ppermute | solution.py:40
  42.9 6.6 %collective-permute-start.15 = (bf16[112,896]{1,0:T(8,128)(2,1)S(1)}, bf16[112,896]{1,0:T(8,128)(2,1)S(1)}, u32[]{:S(2)}, u32[]{:S(2)}) collective-permute-start(bf16[112,896]{1,0:T(8,128)(2,1)S(1)} %pad_maximum_fusion.2), channel_id=1, source_target_pairs={{4,0},{8,4},{12,8},{16,12},{20,16},{24,20},{28,24},{0,28},{5,1},{9... | collective-permute-start | bytes 602120 | tf_op jit(solution)/shard_map/ppermute | solution.py:40
  46.5 6.6 %collective-permute-start.11 = (bf16[112,896]{1,0:T(8,128)(2,1)S(1)}, bf16[112,896]{1,0:T(8,128)(2,1)S(1)}, u32[]{:S(2)}, u32[]{:S(2)}) collective-permute-start(bf16[112,896]{1,0:T(8,128)(2,1)S(1)} %pad_maximum_fusion.1), channel_id=1, source_target_pairs={{28,0},{0,4},{4,8},{8,12},{12,16},{16,20},{20,24},{24,28},{29,1},{... | collective-permute-start | bytes 602120 | tf_op jit(solution)/shard_map/ppermute | solution.py:40
  49.6 6.1 %collective-permute-start.16 = (bf16[112,896]{1,0:T(8,128)(2,1)S(1)}, bf16[112,896]{1,0:T(8,128)(2,1)S(1)}, u32[]{:S(2)}, u32[]{:S(2)}) collective-permute-start(bf16[112,896]{1,0:T(8,128)(2,1)S(1)} %add_convert_fusion.1), channel_id=1, source_target_pairs={{4,0},{8,4},{12,8},{16,12},{20,16},{24,20},{28,24},{0,28},{5,1},{9... | collective-permute-start | bytes 602120 | tf_op jit(solution)/shard_map/ppermute | solution.py:40
  53.1 6.0 %collective-permute-start.12 = (bf16[112,896]{1,0:T(8,128)(2,1)S(1)}, bf16[112,896]{1,0:T(8,128)(2,1)S(1)}, u32[]{:S(2)}, u32[]{:S(2)}) collective-permute-start(bf16[112,896]{1,0:T(8,128)(2,1)S(1)} %add_convert_fusion.3), channel_id=1, source_target_pairs={{28,0},{0,4},{4,8},{8,12},{12,16},{16,20},{20,24},{24,28},{29,1},{... | collective-permute-start | bytes 602120 | tf_op jit(solution)/shard_map/ppermute | solution.py:40
  55.8 5.9 %collective-permute-start.17 = (bf16[112,896]{1,0:T(8,128)(2,1)S(1)}, bf16[112,896]{1,0:T(8,128)(2,1)S(1)}, u32[]{:S(2)}, u32[]{:S(2)}) collective-permute-start(bf16[112,896]{1,0:T(8,128)(2,1)S(1)} %add_convert_fusion), channel_id=1, source_target_pairs={{4,0},{8,4},{12,8},{16,12},{20,16},{24,20},{28,24},{0,28},{5,1},{9... | collective-permute-start | bytes 602120 | tf_op jit(solution)/shard_map/ppermute | solution.py:40
  59.2 5.9 %collective-permute-start.13 = (bf16[112,896]{1,0:T(8,128)(2,1)S(1)}, bf16[112,896]{1,0:T(8,128)(2,1)S(1)}, u32[]{:S(2)}, u32[]{:S(2)}) collective-permute-start(bf16[112,896]{1,0:T(8,128)(2,1)S(1)} %add_convert_fusion.2), channel_id=1, source_target_pairs={{28,0},{0,4},{4,8},{8,12},{12,16},{16,20},{20,24},{24,28},{29,1},{... | collective-permute-start | bytes 602120 | tf_op jit(solution)/shard_map/ppermute | solution.py:40
  65.7 7.4 %collective-permute-start.18 = (bf16[112,896]{1,0:T(8,128)(2,1)S(1)}, bf16[112,896]{1,0:T(8,128)(2,1)S(1)}, u32[]{:S(2)}, u32[]{:S(2)}) collective-permute-start(bf16[112,896]{1,0:T(8,128)(2,1)S(1)} %get-tuple-element.58.mine), channel_id=1, source_target_pairs={{2,0},{0,2},{3,1},{1,3},{6,4},{4,6},{7,5},{5,7},{10,8},{8,10},{11,... | collective-permute-start | bytes 602120 | tf_op jit(solution)/shard_map/ppermute | solution.py:40
  68.4 4.7 %collective-permute-start.20 = (bf16[56,896]{1,0:T(8,128)(2,1)S(1)}, bf16[56,896]{1,0:T(8,128)(2,1)S(1)}, u32[]{:S(2)}, u32[]{:S(2)}) collective-permute-start(bf16[56,896]{1,0:T(8,128)(2,1)S(1)} %get-tuple-element.59), channel_id=1, source_target_pairs={{34,0},{32,2},{2,32},{0,34},{35,1},{33,3},{3,33},{1,35},{38,4},{36... | collective-permute-start | bytes 301064 | tf_op jit(solution)/shard_map/ppermute | solution.py:53
  68.4 4.7 %collective-permute-start.19 = (bf16[56,896]{1,0:T(8,128)(2,1)S(1)}, bf16[56,896]{1,0:T(8,128)(2,1)S(1)}, u32[]{:S(2)}, u32[]{:S(2)}) collective-permute-start(bf16[56,896]{1,0:T(8,128)(2,1)S(1)} %get-tuple-element.59), channel_id=1, source_target_pairs={{32,0},{0,32},{33,1},{1,33},{34,2},{2,34},{35,3},{3,35},{36,4},{4,... | collective-permute-start | bytes 301064 | tf_op jit(solution)/shard_map/ppermute | solution.py:40
  73.7 5.9 %collective-permute-start.25 = (bf16[112,896]{1,0:T(8,128)(2,1)S(1)}, bf16[112,896]{1,0:T(8,128)(2,1)S(1)}, u32[]{:S(2)}, u32[]{:S(2)}) collective-permute-start(bf16[112,896]{1,0:T(8,128)(2,1)S(1)} %shard_map.23.refs_0_), channel_id=1, source_target_pairs={{28,0},{0,4},{4,8},{8,12},{12,16},{16,20},{20,24},{24,28},{29,1},{... | collective-permute-start | bytes 602120 | tf_op jit(solution)/shard_map/ppermute | solution.py:40
  73.8 5.8 %collective-permute-start.21 = (bf16[112,896]{1,0:T(8,128)(2,1)S(1)}, bf16[112,896]{1,0:T(8,128)(2,1)S(1)}, u32[]{:S(2)}, u32[]{:S(2)}) collective-permute-start(bf16[112,896]{1,0:T(8,128)(2,1)S(1)} %shard_map.23.refs_0_), channel_id=1, source_target_pairs={{4,0},{8,4},{12,8},{16,12},{20,16},{24,20},{28,24},{0,28},{5,1},{9... | collective-permute-start | bytes 602120 | tf_op jit(solution)/shard_map/ppermute | solution.py:40
  79.6 9.6 %collective-permute-start.26 = (bf16[112,896]{1,0:T(8,128)(2,1)S(1)}, bf16[112,896]{1,0:T(8,128)(2,1)S(1)}, u32[]{:S(2)}, u32[]{:S(2)}) collective-permute-start(bf16[112,896]{1,0:T(8,128)(2,1)S(1)} %collective-permute-done.25.refs_7_), channel_id=1, source_target_pairs={{28,0},{0,4},{4,8},{8,12},{12,16},{16,20},{20,24},{24,28},{29,1},{... | collective-permute-start | bytes 602120 | tf_op jit(solution)/shard_map/ppermute | solution.py:40
  79.6 9.6 %collective-permute-start.22 = (bf16[112,896]{1,0:T(8,128)(2,1)S(1)}, bf16[112,896]{1,0:T(8,128)(2,1)S(1)}, u32[]{:S(2)}, u32[]{:S(2)}) collective-permute-start(bf16[112,896]{1,0:T(8,128)(2,1)S(1)} %collective-permute-done.21.refs_1_), channel_id=1, source_target_pairs={{4,0},{8,4},{12,8},{16,12},{20,16},{24,20},{28,24},{0,28},{5,1},{9... | collective-permute-start | bytes 602120 | tf_op jit(solution)/shard_map/ppermute | solution.py:40
  82.3 10.6 %collective-permute-start.24 = (bf16[112,896]{1,0:T(8,128)(2,1)S(1)}, bf16[112,896]{1,0:T(8,128)(2,1)S(1)}, u32[]{:S(2)}, u32[]{:S(2)}) collective-permute-start(bf16[112,896]{1,0:T(8,128)(2,1)S(1)} %shard_map.23.refs_0_), channel_id=1, source_target_pairs={{16,0},{20,4},{24,8},{28,12},{0,16},{4,20},{8,24},{12,28},{17,1},{... | collective-permute-start | bytes 602120 | tf_op jit(solution)/shard_map/ppermute | solution.py:40
  89.2 5.8 %collective-permute-start.27 = (bf16[112,896]{1,0:T(8,128)(2,1)S(1)}, bf16[112,896]{1,0:T(8,128)(2,1)S(1)}, u32[]{:S(2)}, u32[]{:S(2)}) collective-permute-start(bf16[112,896]{1,0:T(8,128)(2,1)S(1)} %collective-permute-done.26.refs_6_), channel_id=1, source_target_pairs={{28,0},{0,4},{4,8},{8,12},{12,16},{16,20},{20,24},{24,28},{29,1},{... | collective-permute-start | bytes 602120 | tf_op jit(solution)/shard_map/ppermute | solution.py:40
  89.2 6.3 %collective-permute-start.23 = (bf16[112,896]{1,0:T(8,128)(2,1)S(1)}, bf16[112,896]{1,0:T(8,128)(2,1)S(1)}, u32[]{:S(2)}, u32[]{:S(2)}) collective-permute-start(bf16[112,896]{1,0:T(8,128)(2,1)S(1)} %collective-permute-done.22.refs_2_), channel_id=1, source_target_pairs={{4,0},{8,4},{12,8},{16,12},{20,16},{24,20},{28,24},{0,28},{5,1},{9... | collective-permute-start | bytes 602120 | tf_op jit(solution)/shard_map/ppermute | solution.py:40
  96.2 34.3 %collective-permute-start.28 = (bf16[8,112,896]{2,1,0:T(8,128)(2,1)S(1)}, bf16[8,112,896]{2,1,0:T(8,128)(2,1)S(1)}, u32[]{:S(2)}, u32[]{:S(2)}) collective-permute-start(bf16[8,112,896]{2,1,0:T(8,128)(2,1)S(1)} %shard_map.24.group), channel_id=1, source_target_pairs={{1,0},{0,1},{3,2},{2,3},{5,4},{4,5},{7,6},{6,7},{9,8},{8,9},{11,10... | collective-permute-start | bytes 4816904 | tf_op jit(solution)/shard_map/ppermute | solution.py:40
  110.8 14.4 %collective-permute-start.4 = (bf16[504,512]{1,0:T(8,128)(2,1)S(1)}, bf16[504,512]{1,0:T(8,128)(2,1)S(1)}, u32[]{:S(2)}, u32[]{:S(2)}) collective-permute-start(bf16[504,512]{1,0:T(8,128)(2,1)S(1)} %collective-permute-done.2.refs_3_), channel_id=1, source_target_pairs={{192,0},{0,64},{64,128},{128,192},{193,1},{1,65},{65,129},{129,193... | collective-permute-start | bytes 1548296 | tf_op jit(solution)/shard_map/ppermute | solution.py:40
  110.8 14.4 %collective-permute-start.3 = (bf16[504,512]{1,0:T(8,128)(2,1)S(1)}, bf16[504,512]{1,0:T(8,128)(2,1)S(1)}, u32[]{:S(2)}, u32[]{:S(2)}) collective-permute-start(bf16[504,512]{1,0:T(8,128)(2,1)S(1)} %collective-permute-done.2.refs_3_), channel_id=1, source_target_pairs={{64,0},{128,64},{192,128},{0,192},{65,1},{129,65},{193,129},{1,193... | collective-permute-start | bytes 1548296 | tf_op jit(solution)/shard_map/ppermute | solution.py:40
  113.5 13.0 %collective-permute-start.7 = (bf16[504,512]{1,0:T(8,128)(2,1)S(1)}, bf16[504,512]{1,0:T(8,128)(2,1)S(1)}, u32[]{:S(2)}, u32[]{:S(2)}) collective-permute-start(bf16[504,512]{1,0:T(8,128)(2,1)S(1)} %pad_maximum_fusion), channel_id=1, source_target_pairs={{32,0},{0,32},{33,1},{1,33},{34,2},{2,34},{35,3},{3,35},{36,4},{4,... | collective-permute-start | bytes 1548296 | tf_op jit(solution)/shard_map/ppermute | solution.py:40
  133.6 11.9 %collective-permute-start.31 = (bf16[504,512]{1,0:T(8,128)(2,1)S(1)}, bf16[504,512]{1,0:T(8,128)(2,1)S(1)}, u32[]{:S(2)}, u32[]{:S(2)}) collective-permute-start(bf16[504,512]{1,0:T(8,128)(2,1)S(1)} %get-tuple-element.64.refs_0_), channel_id=1, source_target_pairs={{32,0},{0,32},{33,1},{1,33},{34,2},{2,34},{35,3},{3,35},{36,4},{4,... | collective-permute-start | bytes 1548296 | tf_op jit(solution)/shard_map/ppermute | solution.py:40
  134.2 12.7 %collective-permute-start.30 = (bf16[504,512]{1,0:T(8,128)(2,1)S(1)}, bf16[504,512]{1,0:T(8,128)(2,1)S(1)}, u32[]{:S(2)}, u32[]{:S(2)}) collective-permute-start(bf16[504,512]{1,0:T(8,128)(2,1)S(1)} %get-tuple-element.64.refs_0_), channel_id=1, source_target_pairs={{192,0},{0,64},{64,128},{128,192},{193,1},{1,65},{65,129},{129,193... | collective-permute-start | bytes 1548296 | tf_op jit(solution)/shard_map/ppermute | solution.py:40
  134.2 12.7 %collective-permute-start.29 = (bf16[504,512]{1,0:T(8,128)(2,1)S(1)}, bf16[504,512]{1,0:T(8,128)(2,1)S(1)}, u32[]{:S(2)}, u32[]{:S(2)}) collective-permute-start(bf16[504,512]{1,0:T(8,128)(2,1)S(1)} %get-tuple-element.64.refs_0_), channel_id=1, source_target_pairs={{64,0},{128,64},{192,128},{0,192},{65,1},{129,65},{193,129},{1,193... | collective-permute-start | bytes 1548296 | tf_op jit(solution)/shard_map/ppermute | solution.py:40
  147.0 10.7 %collective-permute-start.33 = (bf16[504,512]{1,0:T(8,128)(2,1)S(1)}, bf16[504,512]{1,0:T(8,128)(2,1)S(1)}, u32[]{:S(2)}, u32[]{:S(2)}) collective-permute-start(bf16[504,512]{1,0:T(8,128)(2,1)S(1)} %collective-permute-done.31.refs_3_), channel_id=1, source_target_pairs={{64,0},{128,64},{192,128},{0,192},{65,1},{129,65},{193,129},{1,193... | collective-permute-start | bytes 1548296 | tf_op jit(solution)/shard_map/ppermute | solution.py:40
  149.4 10.1 %collective-permute-start.34 = (bf16[504,512]{1,0:T(8,128)(2,1)S(1)}, bf16[504,512]{1,0:T(8,128)(2,1)S(1)}, u32[]{:S(2)}, u32[]{:S(2)}) collective-permute-start(bf16[504,512]{1,0:T(8,128)(2,1)S(1)} %collective-permute-done.30.refs_2_), channel_id=1, source_target_pairs={{32,0},{0,32},{33,1},{1,33},{34,2},{2,34},{35,3},{3,35},{36,4},{4,... | collective-permute-start | bytes 1548296 | tf_op jit(solution)/shard_map/ppermute | solution.py:40
  150.3 11.0 %collective-permute-start.32 = (bf16[504,512]{1,0:T(8,128)(2,1)S(1)}, bf16[504,512]{1,0:T(8,128)(2,1)S(1)}, u32[]{:S(2)}, u32[]{:S(2)}) collective-permute-start(bf16[504,512]{1,0:T(8,128)(2,1)S(1)} %collective-permute-done.30.refs_2_), channel_id=1, source_target_pairs={{192,0},{0,64},{64,128},{128,192},{193,1},{1,65},{65,129},{129,193... | collective-permute-start | bytes 1548296 | tf_op jit(solution)/shard_map/ppermute | solution.py:40
  161.3 8.3 %collective-permute-start.35 = (bf16[256,512]{1,0:T(8,128)(2,1)S(1)}, bf16[256,512]{1,0:T(8,128)(2,1)S(1)}, u32[]{:S(2)}, u32[]{:S(2)}) collective-permute-start(bf16[256,512]{1,0:T(8,128)(2,1)S(1)} %slice.30), channel_id=1, source_target_pairs={{64,0},{128,64},{192,128},{0,192},{65,1},{129,65},{193,129},{1,193... | collective-permute-start | bytes 786440 | tf_op jit(solution)/shard_map/ppermute | solution.py:40
  161.4 8.2 %collective-permute-start.36 = (bf16[248,512]{1,0:T(8,128)(2,1)S(1)}, bf16[248,512]{1,0:T(8,128)(2,1)S(1)}, u32[]{:S(2)}, u32[]{:S(2)}) collective-permute-start(bf16[248,512]{1,0:T(8,128)(2,1)S(1)} %slice.31), channel_id=1, source_target_pairs={{192,0},{0,64},{64,128},{128,192},{193,1},{1,65},{65,129},{129,193... | collective-permute-start | bytes 761864 | tf_op jit(solution)/shard_map/ppermute | solution.py:40

commit v5 on v2

--- a/solution.py
+++ b/solution.py
@@ -164,19 +164,13 @@
             out[far] = rows[side, chunk(z, far, size), :].astype(BF16)
 
 
-def late_body(place, own, low, partner, top, bottom, keep, send, rows, panel, left, blocks):
+def late_body(place, own, low, partner, top, bottom, keep, send, rows, panel):
     z, c = place[0], place[1]
     height = own.shape[0]
     fill(panel, [top, bottom])
     rows[0] = partner[...]
-    left[0], left[1] = low[1, height:], own[...]
-
-    @pl.loop(0, 2)
-    def _(i):
-        blocks[i] = lax.dot_general(left[i], panel[0, :height], DIMS, preferred_element_type=F32)
-
-    rows[1, :, :height] = blocks[0]
-    rows[1, :, height:] = blocks[1]
+    rows[1, :, :height] = lax.dot_general(low[1, height:], panel[0, :height], DIMS, preferred_element_type=F32)
+    rows[1, :, height:] = lax.dot_general(own[...], panel[0, :height], DIMS, preferred_element_type=F32)
     split_units(z, c, rows, keep, send)
 
 
@@ -361,7 +355,7 @@
         [pltpu.VMEM((3, rows, 2 * rows), F32), pltpu.VMEM((2, rows, cols), BF16)],
     )
     halves = [keep, shift(send, "c", 1)]
-    scratch = [pairs, room(1), pltpu.VMEM((2, rows, cols), BF16), pltpu.VMEM((2, rows, rows), F32)]
+    scratch = [pairs, room(1)]
     keep, send = call(late_body, place, (own, low, partner, *r20), [part, part], work, scratch)
     halves += [keep, shift(send, "c", 1)]
     r11 = shift(near[2], "x", 1)

time: 171 us -> 170 us (level)
  transfers between devices with their start and end apart: 39 -> 39, of which waited for: 20 -> 20; matrix products, arithmetic and copies ran while one was open for 0% -> 0% of each run, Pallas kernels for 12% -> 11%
where the time goes in v5:
time: 170 us; the launch traced here: 169 us
  waiting for transfers between devices  72.2 us (42%)
  starting transfers between devices  68.1 us (40%)
  Pallas kernels  27.1 us (16%)
    ppermute x38, starting transfers between devices, shift(): lax.ppermute(value, axis, [((i + step) % size, i) for i in range(size)])  68.1 us
    ppermute x38, waiting for transfers between devices, shift(): lax.ppermute(value, axis, [((i + step) % size, i) for i in range(size)])  67.5 us
    pallas_call x14, Pallas kernels, call(): pl.pallas_call(body, out_shape=outs if home else [pltpu.VMEM(o.shape, o.d...  27.1 us
    ppermute x1, waiting for transfers between devices, fetch(): lax.ppermute(value, axes, [(flat(source(*p)), flat(p)) for p in places])  4.67 us
  transfers between devices with their start and end apart: 39, of which 20 were waited for; matrix products, arithmetic and copies ran while one was open for 0% of the time, Pallas kernels for 11%

profile of v5, /device:TPU:1, one launch (start us, length us, event | category | flops | bytes accessed | tf_op | source)
XLA Modules:
  0.0 169.4 jit_solution(2311037236785584724)
XLA Ops:
  0.1 1.1 copy-done
  1.1 0.6 shard_map.17
  1.8 2.2 %collective-permute-start.2 = (bf16[504,512]{1,0:T(8,128)(2,1)S(1)}, bf16[504,512]{1,0:T(8,128)(2,1)S(1)}, u32[]{:S(2)}, u32[]{:S(2)}) collective-permute-start(bf16[504,512]{1,0:T(8,128)(2,1)S(1)} %get-tuple-element.41.refs_0_), channel_id=1, source_target_pairs={{32,0},{0,32},{33,1},{1,33},{34,2},{2,34},{35,3},{3,35},{36,4},{4,... | collective-permute-start | bytes 1548296 | tf_op jit(solution)/shard_map/ppermute | solution.py:40
  4.0 1.2 collective-permute-start.1
  5.2 1.5 collective-permute-start
  6.7 7.6 %collective-permute-done.2.refs_3_ = bf16[504,512]{1,0:T(8,128)(2,1)S(1)} collective-permute-done((bf16[504,512]{1,0:T(8,128)(2,1)S(1)}, bf16[504,512]{1,0:T(8,128)(2,1)S(1)}, u32[]{:S(2)}, u32[]{:S(2)}) %collective-permute-start.2) | collective-permute-done | bytes 516128 | tf_op jit(solution)/shard_map/ppermute | solution.py:40
  14.3 3.0 %collective-permute-done.1.refs_2_ = bf16[504,512]{1,0:T(8,128)(2,1)S(1)} collective-permute-done((bf16[504,512]{1,0:T(8,128)(2,1)S(1)}, bf16[504,512]{1,0:T(8,128)(2,1)S(1)}, u32[]{:S(2)}, u32[]{:S(2)}) %collective-permute-start.1) | collective-permute-done | bytes 516128 | tf_op jit(solution)/shard_map/ppermute | solution.py:40
  17.3 2.5 %collective-permute-start.5 = (bf16[256,512]{1,0:T(8,128)(2,1)S(1)}, bf16[256,512]{1,0:T(8,128)(2,1)S(1)}, u32[]{:S(2)}, u32[]{:S(2)}) collective-permute-start(bf16[256,512]{1,0:T(8,128)(2,1)S(1)} %slice.30), channel_id=1, source_target_pairs={{64,0},{128,64},{192,128},{0,192},{65,1},{129,65},{193,129},{1,193... | collective-permute-start | bytes 786440 | tf_op jit(solution)/shard_map/ppermute | solution.py:40
  19.9 4.2 %shard_map.18 = (bf16[8,56,896]{2,1,0:T(8,128)(2,1)S(1)}, bf16[8,56,896]{2,1,0:T(8,128)(2,1)S(1)}, bf16[3,896,576]{2,1,0:T(8,128)(2,1)S(1)}, f32[448,896]{1,0:T(8,128)S(1)}) custom-call(s32[2]{0:T(128)S(1)} %pad_add_fusion.place, bf16[448,576]{1,0:T(8,128)(2,1)S(1)} %get-tuple-element.40.own, bf16[504,512]{1,0:T(8,128)(2,1)S(1)} %get-tuple-element.41.refs_0_, ...), custom_call_target="tpu_custom_call" | custom-call | flops 1387266048 | bytes 8085504 | tf_op jit(solution)/shard_map/pallas_call | solution.py:62
  24.1 2.7 %collective-permute-start.8 = (bf16[8,56,896]{2,1,0:T(8,128)(2,1)S(1)}, bf16[8,56,896]{2,1,0:T(8,128)(2,1)S(1)}, u32[]{:S(2)}, u32[]{:S(2)}) collective-permute-start(bf16[8,56,896]{2,1,0:T(8,128)(2,1)S(1)} %get-tuple-element.47), channel_id=1, source_target_pairs={{1,0},{0,1},{3,2},{2,3},{5,4},{4,5},{7,6},{6,7},{9,8},{8,9},{11,10... | collective-permute-start | bytes 2408456 | tf_op jit(solution)/shard_map/ppermute | solution.py:40
  26.8 2.0 %shard_map.20 = (bf16[8,56,896]{2,1,0:T(8,128)(2,1)S(1)}, bf16[8,56,896]{2,1,0:T(8,128)(2,1)S(1)}) custom-call(s32[2]{0:T(128)S(1)} %pad_add_fusion.place, bf16[448,576]{1,0:T(8,128)(2,1)S(1)} %get-tuple-element.40.own, bf16[3,896,576]{2,1,0:T(8,128)(2,1)S(1)} %get-tuple-element.45.low, f32[448,896]{1,0:T(8,128)S(1)} %get-tuple-element.48.partner, ...), custom_call_target="tpu_custom_call" | custom-call | flops 462422016 | bytes 6537216 | tf_op jit(solution)/shard_map/pallas_call | solution.py:62
  28.8 3.3 %collective-permute-start.9 = (bf16[8,56,896]{2,1,0:T(8,128)(2,1)S(1)}, bf16[8,56,896]{2,1,0:T(8,128)(2,1)S(1)}, u32[]{:S(2)}, u32[]{:S(2)}) collective-permute-start(bf16[8,56,896]{2,1,0:T(8,128)(2,1)S(1)} %get-tuple-element.50), channel_id=1, source_target_pairs={{1,0},{0,1},{3,2},{2,3},{5,4},{4,5},{7,6},{6,7},{9,8},{8,9},{11,10... | collective-permute-start | bytes 2408456 | tf_op jit(solution)/shard_map/ppermute | solution.py:40
  32.1 1.9 %collective-permute-done.9.high_other = bf16[8,56,896]{2,1,0:T(8,128)(2,1)S(1)} collective-permute-done((bf16[8,56,896]{2,1,0:T(8,128)(2,1)S(1)}, bf16[8,56,896]{2,1,0:T(8,128)(2,1)S(1)}, u32[]{:S(2)}, u32[]{:S(2)}) %collective-permute-start.9) | collective-permute-done | bytes 802848 | tf_op jit(solution)/shard_map/ppermute | solution.py:40
  34.0 0.9 shard_map.21
  35.0 5.7 %collective-permute-start.14 = (bf16[56,896]{1,0:T(8,128)(2,1)S(1)}, bf16[56,896]{1,0:T(8,128)(2,1)S(1)}, u32[]{:S(2)}, u32[]{:S(2)}) collective-permute-start(bf16[56,896]{1,0:T(8,128)(2,1)S(1)} %get-tuple-element.59), channel_id=1, source_target_pairs={{4,0},{8,4},{12,8},{16,12},{20,16},{24,20},{28,24},{0,28},{5,1},{9... | collective-permute-start | bytes 301064 | tf_op jit(solution)/shard_map/ppermute | solution.py:40
  40.6 0.1 collective-permute-start.10
  40.7 1.7 %collective-permute-done.14 = bf16[56,896]{1,0:T(8,128)(2,1)S(1)} collective-permute-done((bf16[56,896]{1,0:T(8,128)(2,1)S(1)}, bf16[56,896]{1,0:T(8,128)(2,1)S(1)}, u32[]{:S(2)}, u32[]{:S(2)}) %collective-permute-start.14) | collective-permute-done | bytes 100384 | tf_op jit(solution)/shard_map/ppermute | solution.py:40
  42.5 3.5 %collective-permute-start.15 = (bf16[112,896]{1,0:T(8,128)(2,1)S(1)}, bf16[112,896]{1,0:T(8,128)(2,1)S(1)}, u32[]{:S(2)}, u32[]{:S(2)}) collective-permute-start(bf16[112,896]{1,0:T(8,128)(2,1)S(1)} %pad_maximum_fusion.2), channel_id=1, source_target_pairs={{4,0},{8,4},{12,8},{16,12},{20,16},{24,20},{28,24},{0,28},{5,1},{9... | collective-permute-start | bytes 602120 | tf_op jit(solution)/shard_map/ppermute | solution.py:40
  46.1 0.1 collective-permute-start.11
  46.1 3.0 %collective-permute-done.15 = bf16[112,896]{1,0:T(8,128)(2,1)S(1)} collective-permute-done((bf16[112,896]{1,0:T(8,128)(2,1)S(1)}, bf16[112,896]{1,0:T(8,128)(2,1)S(1)}, u32[]{:S(2)}, u32[]{:S(2)}) %collective-permute-start.15) | collective-permute-done | bytes 200736 | tf_op jit(solution)/shard_map/ppermute | solution.py:40
  49.2 3.5 %collective-permute-start.16 = (bf16[112,896]{1,0:T(8,128)(2,1)S(1)}, bf16[112,896]{1,0:T(8,128)(2,1)S(1)}, u32[]{:S(2)}, u32[]{:S(2)}) collective-permute-start(bf16[112,896]{1,0:T(8,128)(2,1)S(1)} %add_convert_fusion.1), channel_id=1, source_target_pairs={{4,0},{8,4},{12,8},{16,12},{20,16},{24,20},{28,24},{0,28},{5,1},{9... | collective-permute-start | bytes 602120 | tf_op jit(solution)/shard_map/ppermute | solution.py:40
  52.7 0.3 collective-permute-start.12
  53.0 2.3 %collective-permute-done.16 = bf16[112,896]{1,0:T(8,128)(2,1)S(1)} collective-permute-done((bf16[112,896]{1,0:T(8,128)(2,1)S(1)}, bf16[112,896]{1,0:T(8,128)(2,1)S(1)}, u32[]{:S(2)}, u32[]{:S(2)}) %collective-permute-start.16) | collective-permute-done | bytes 200736 | tf_op jit(solution)/shard_map/ppermute | solution.py:40
  55.4 3.2 %collective-permute-start.17 = (bf16[112,896]{1,0:T(8,128)(2,1)S(1)}, bf16[112,896]{1,0:T(8,128)(2,1)S(1)}, u32[]{:S(2)}, u32[]{:S(2)}) collective-permute-start(bf16[112,896]{1,0:T(8,128)(2,1)S(1)} %add_convert_fusion), channel_id=1, source_target_pairs={{4,0},{8,4},{12,8},{16,12},{20,16},{24,20},{28,24},{0,28},{5,1},{9... | collective-permute-start | bytes 602120 | tf_op jit(solution)/shard_map/ppermute | solution.py:40
  58.6 0.2 collective-permute-done.12
  58.8 0.1 collective-permute-start.13
  58.9 2.3 %collective-permute-done.17.down = bf16[112,896]{1,0:T(8,128)(2,1)S(1)} collective-permute-done((bf16[112,896]{1,0:T(8,128)(2,1)S(1)}, bf16[112,896]{1,0:T(8,128)(2,1)S(1)}, u32[]{:S(2)}, u32[]{:S(2)}) %collective-permute-start.17) | collective-permute-done | bytes 200736 | tf_op jit(solution)/shard_map/ppermute | solution.py:40
  61.2 3.4 %collective-permute-done.13.up = bf16[112,896]{1,0:T(8,128)(2,1)S(1)} collective-permute-done((bf16[112,896]{1,0:T(8,128)(2,1)S(1)}, bf16[112,896]{1,0:T(8,128)(2,1)S(1)}, u32[]{:S(2)}, u32[]{:S(2)}) %collective-permute-start.13) | collective-permute-done | bytes 200736 | tf_op jit(solution)/shard_map/ppermute | solution.py:40
  64.6 0.6 shard_map.22
  65.3 2.7 %collective-permute-start.18 = (bf16[112,896]{1,0:T(8,128)(2,1)S(1)}, bf16[112,896]{1,0:T(8,128)(2,1)S(1)}, u32[]{:S(2)}, u32[]{:S(2)}) collective-permute-start(bf16[112,896]{1,0:T(8,128)(2,1)S(1)} %get-tuple-element.60.mine), channel_id=1, source_target_pairs={{2,0},{0,2},{3,1},{1,3},{6,4},{4,6},{7,5},{5,7},{10,8},{8,10},{11,... | collective-permute-start | bytes 602120 | tf_op jit(solution)/shard_map/ppermute | solution.py:40
  68.0 4.7 %collective-permute-done.20.cross = bf16[56,896]{1,0:T(8,128)(2,1)S(1)} collective-permute-done((bf16[56,896]{1,0:T(8,128)(2,1)S(1)}, bf16[56,896]{1,0:T(8,128)(2,1)S(1)}, u32[]{:S(2)}, u32[]{:S(2)}) %collective-permute-start.20) | collective-permute-done | bytes 100384 | tf_op jit(solution)/shard_map/ppermute | solution.py:53
  72.7 0.6 shard_map.23.refs_0_
  73.3 0.1 collective-permute-start.24
  73.4 2.7 %collective-permute-start.21 = (bf16[112,896]{1,0:T(8,128)(2,1)S(1)}, bf16[112,896]{1,0:T(8,128)(2,1)S(1)}, u32[]{:S(2)}, u32[]{:S(2)}) collective-permute-start(bf16[112,896]{1,0:T(8,128)(2,1)S(1)} %shard_map.23.refs_0_), channel_id=1, source_target_pairs={{4,0},{8,4},{12,8},{16,12},{20,16},{24,20},{28,24},{0,28},{5,1},{9... | collective-permute-start | bytes 602120 | tf_op jit(solution)/shard_map/ppermute | solution.py:40
  76.1 3.1 %collective-permute-done.24.refs_6_ = bf16[112,896]{1,0:T(8,128)(2,1)S(1)} collective-permute-done((bf16[112,896]{1,0:T(8,128)(2,1)S(1)}, bf16[112,896]{1,0:T(8,128)(2,1)S(1)}, u32[]{:S(2)}, u32[]{:S(2)}) %collective-permute-start.24) | collective-permute-done | bytes 200736 | tf_op jit(solution)/shard_map/ppermute | solution.py:40
  79.2 2.7 %collective-permute-start.22 = (bf16[112,896]{1,0:T(8,128)(2,1)S(1)}, bf16[112,896]{1,0:T(8,128)(2,1)S(1)}, u32[]{:S(2)}, u32[]{:S(2)}) collective-permute-start(bf16[112,896]{1,0:T(8,128)(2,1)S(1)} %collective-permute-done.21.refs_1_), channel_id=1, source_target_pairs={{4,0},{8,4},{12,8},{16,12},{20,16},{24,20},{28,24},{0,28},{5,1},{9... | collective-permute-start | bytes 602120 | tf_op jit(solution)/shard_map/ppermute | solution.py:40
  81.8 4.8 %collective-permute-done.25.refs_5_ = bf16[112,896]{1,0:T(8,128)(2,1)S(1)} collective-permute-done((bf16[112,896]{1,0:T(8,128)(2,1)S(1)}, bf16[112,896]{1,0:T(8,128)(2,1)S(1)}, u32[]{:S(2)}, u32[]{:S(2)}) %collective-permute-start.25) | collective-permute-done | bytes 200736 | tf_op jit(solution)/shard_map/ppermute | solution.py:40
  86.6 2.7 %collective-permute-start.23 = (bf16[112,896]{1,0:T(8,128)(2,1)S(1)}, bf16[112,896]{1,0:T(8,128)(2,1)S(1)}, u32[]{:S(2)}, u32[]{:S(2)}) collective-permute-start(bf16[112,896]{1,0:T(8,128)(2,1)S(1)} %collective-permute-done.22.refs_2_), channel_id=1, source_target_pairs={{4,0},{8,4},{12,8},{16,12},{20,16},{24,20},{28,24},{0,28},{5,1},{9... | collective-permute-start | bytes 602120 | tf_op jit(solution)/shard_map/ppermute | solution.py:40
  89.3 3.9 %collective-permute-done.26.refs_4_ = bf16[112,896]{1,0:T(8,128)(2,1)S(1)} collective-permute-done((bf16[112,896]{1,0:T(8,128)(2,1)S(1)}, bf16[112,896]{1,0:T(8,128)(2,1)S(1)}, u32[]{:S(2)}, u32[]{:S(2)}) %collective-permute-start.26) | collective-permute-done | bytes 200736 | tf_op jit(solution)/shard_map/ppermute | solution.py:40
  93.2 0.6 shard_map.24.group
  93.8 9.0 %collective-permute-start.27 = (bf16[7,112,896]{2,1,0:T(8,128)(2,1)S(1)}, bf16[7,112,896]{2,1,0:T(8,128)(2,1)S(1)}, u32[]{:S(2)}, u32[]{:S(2)}) collective-permute-start(bf16[7,112,896]{2,1,0:T(8,128)(2,1)S(1)} %shard_map.24.group), channel_id=1, source_target_pairs={{1,0},{0,1},{3,2},{2,3},{5,4},{4,5},{7,6},{6,7},{9,8},{8,9},{11,10... | collective-permute-start | bytes 4214792 | tf_op jit(solution)/shard_map/ppermute | solution.py:40
  102.9 2.7 %collective-permute-start.3 = (bf16[504,512]{1,0:T(8,128)(2,1)S(1)}, bf16[504,512]{1,0:T(8,128)(2,1)S(1)}, u32[]{:S(2)}, u32[]{:S(2)}) collective-permute-start(bf16[504,512]{1,0:T(8,128)(2,1)S(1)} %collective-permute-done.2.refs_3_), channel_id=1, source_target_pairs={{64,0},{128,64},{192,128},{0,192},{65,1},{129,65},{193,129},{1,193... | collective-permute-start | bytes 1548296 | tf_op jit(solution)/shard_map/ppermute | solution.py:40
  105.6 1.3 collective-permute-start.7
  106.9 3.0 %collective-permute-start.28 = (bf16[56,896]{1,0:T(8,128)(2,1)S(1)}, bf16[56,896]{1,0:T(8,128)(2,1)S(1)}, u32[]{:S(2)}, u32[]{:S(2)}) collective-permute-start(bf16[56,896]{1,0:T(8,128)(2,1)S(1)} %slice.40), channel_id=1, source_target_pairs={{4,0},{8,4},{12,8},{16,12},{20,16},{24,20},{28,24},{0,28},{5,1},{9... | collective-permute-start | bytes 301064 | tf_op jit(solution)/shard_map/ppermute | solution.py:40
  109.9 1.6 collective-permute-done.28
  111.6 5.6 %collective-permute-done.29 = bf16[56,896]{1,0:T(8,128)(2,1)S(1)} collective-permute-done((bf16[56,896]{1,0:T(8,128)(2,1)S(1)}, bf16[56,896]{1,0:T(8,128)(2,1)S(1)}, u32[]{:S(2)}, u32[]{:S(2)}) %collective-permute-start.29) | collective-permute-done | bytes 100384 | tf_op jit(solution)/shard_map/ppermute | solution.py:40
  117.2 2.4 %collective-permute-start.30 = (bf16[112,896]{1,0:T(8,128)(2,1)S(1)}, bf16[112,896]{1,0:T(8,128)(2,1)S(1)}, u32[]{:S(2)}, u32[]{:S(2)}) collective-permute-start(bf16[112,896]{1,0:T(8,128)(2,1)S(1)} %constant_dynamic-update-slice_fusion.mine), channel_id=1, source_target_pairs={{1,0},{0,1},{3,2},{2,3},{5,4},{4,5},{7,6},{6,7},{9,8},{8,9},{11,10... | collective-permute-start | bytes 602120 | tf_op jit(solution)/shard_map/ppermute | solution.py:40
  119.7 1.5 shard_map.19.panel
  121.1 2.5 %shard_map.25 = (bf16[4,448,896]{2,1,0:T(8,128)(2,1)S(1)}, f32[448,576]{1,0:T(8,128)S(1)}) custom-call(s32[2]{0:T(128)S(1)} %pad_add_fusion.place, bf16[4,896,576]{2,1,0:T(8,128)(2,1)S(1)} %shard_map.19.panel, bf16[7,112,896]{2,1,0:T(8,128)(2,1)S(1)} %shard_map.24.group), custom_call_target="tpu_custom_call" | custom-call | flops 924844032 | bytes 9261056 | tf_op jit(solution)/shard_map/pallas_call | solution.py:62
  123.7 2.5 %shard_map.26 = (bf16[4,448,896]{2,1,0:T(8,128)(2,1)S(1)}, f32[448,576]{1,0:T(8,128)S(1)}) custom-call(s32[2]{0:T(128)S(1)} %pad_add_fusion.place, bf16[4,896,576]{2,1,0:T(8,128)(2,1)S(1)} %shard_map.19.panel, bf16[7,112,896]{2,1,0:T(8,128)(2,1)S(1)} %collective-permute-done.27.group, ...), custom_call_target="tpu_custom_call", output_to_operand_aliasing={{0}: (3, {}), {1}: (4, {})} | custom-call | flops 924844032 | bytes 12988416 | tf_op jit(solution)/shard_map/pallas_call | solution.py:62
  126.2 2.5 %shard_map.27 = (bf16[4,448,896]{2,1,0:T(8,128)(2,1)S(1)}, bf16[504,512]{1,0:T(8,128)(2,1)S(1)}, bf16[448,576]{1,0:T(8,128)(2,1)S(1)}) custom-call(s32[2]{0:T(128)S(1)} %pad_add_fusion.place, bf16[448,576]{1,0:T(8,128)(2,1)S(1)} %get-tuple-element.40.own, bf16[4,896,576]{2,1,0:T(8,128)(2,1)S(1)} %shard_map.19.panel, ...), custom_call_target="tpu_custom_call", output_to_operand_aliasing={{0}: (3, {})} | custom-call | flops 231211008 | bytes 13017088 | tf_op jit(solution)/shard_map/pallas_call | solution.py:62
  128.7 0.4 collective-permute-start.33
  129.1 2.7 %collective-permute-start.31 = (bf16[504,512]{1,0:T(8,128)(2,1)S(1)}, bf16[504,512]{1,0:T(8,128)(2,1)S(1)}, u32[]{:S(2)}, u32[]{:S(2)}) collective-permute-start(bf16[504,512]{1,0:T(8,128)(2,1)S(1)} %get-tuple-element.68.refs_0_), channel_id=1, source_target_pairs={{64,0},{128,64},{192,128},{0,192},{65,1},{129,65},{193,129},{1,193... | collective-permute-start | bytes 1548296 | tf_op jit(solution)/shard_map/ppermute | solution.py:40
  131.7 10.2 %collective-permute-done.33.refs_3_ = bf16[504,512]{1,0:T(8,128)(2,1)S(1)} collective-permute-done((bf16[504,512]{1,0:T(8,128)(2,1)S(1)}, bf16[504,512]{1,0:T(8,128)(2,1)S(1)}, u32[]{:S(2)}, u32[]{:S(2)}) %collective-permute-start.33) | collective-permute-done | bytes 516128 | tf_op jit(solution)/shard_map/ppermute | solution.py:40
  141.9 0.4 collective-permute-done.32.refs_2_
  142.3 2.4 %collective-permute-start.35 = (bf16[504,512]{1,0:T(8,128)(2,1)S(1)}, bf16[504,512]{1,0:T(8,128)(2,1)S(1)}, u32[]{:S(2)}, u32[]{:S(2)}) collective-permute-start(bf16[504,512]{1,0:T(8,128)(2,1)S(1)} %collective-permute-done.33.refs_3_), channel_id=1, source_target_pairs={{64,0},{128,64},{192,128},{0,192},{65,1},{129,65},{193,129},{1,193... | collective-permute-start | bytes 1548296 | tf_op jit(solution)/shard_map/ppermute | solution.py:40
  144.7 2.0 %collective-permute-start.36 = (bf16[504,512]{1,0:T(8,128)(2,1)S(1)}, bf16[504,512]{1,0:T(8,128)(2,1)S(1)}, u32[]{:S(2)}, u32[]{:S(2)}) collective-permute-start(bf16[504,512]{1,0:T(8,128)(2,1)S(1)} %collective-permute-done.32.refs_2_), channel_id=1, source_target_pairs={{32,0},{0,32},{33,1},{1,33},{34,2},{2,34},{35,3},{3,35},{36,4},{4,... | collective-permute-start | bytes 1548296 | tf_op jit(solution)/shard_map/ppermute | solution.py:40
  146.7 6.7 %collective-permute-done.35.r11 = bf16[504,512]{1,0:T(8,128)(2,1)S(1)} collective-permute-done((bf16[504,512]{1,0:T(8,128)(2,1)S(1)}, bf16[504,512]{1,0:T(8,128)(2,1)S(1)}, u32[]{:S(2)}, u32[]{:S(2)}) %collective-permute-start.35) | collective-permute-done | bytes 516128 | tf_op jit(solution)/shard_map/ppermute | solution.py:40
  153.4 3.0 %collective-permute-done.36.r31 = bf16[504,512]{1,0:T(8,128)(2,1)S(1)} collective-permute-done((bf16[504,512]{1,0:T(8,128)(2,1)S(1)}, bf16[504,512]{1,0:T(8,128)(2,1)S(1)}, u32[]{:S(2)}, u32[]{:S(2)}) %collective-permute-start.36) | collective-permute-done | bytes 516128 | tf_op jit(solution)/shard_map/ppermute | solution.py:40
  156.4 2.7 %collective-permute-done.34.r20 = bf16[504,512]{1,0:T(8,128)(2,1)S(1)} collective-permute-done((bf16[504,512]{1,0:T(8,128)(2,1)S(1)}, bf16[504,512]{1,0:T(8,128)(2,1)S(1)}, u32[]{:S(2)}, u32[]{:S(2)}) %collective-permute-start.34) | collective-permute-done | bytes 516128 | tf_op jit(solution)/shard_map/ppermute | solution.py:40
  159.2 1.5 collective-permute-start.38
  160.7 3.9 %shard_map.28.before = f32[448,576]{1,0:T(8,128)S(1)} custom-call(s32[2]{0:T(128)S(1)} %pad_add_fusion.place, bf16[448,576]{1,0:T(8,128)(2,1)S(1)} %get-tuple-element.40.own, bf16[448,576]{1,0:T(8,128)(2,1)S(1)} %get-tuple-element.66.w_low, bf16[4,448,896]{2,1,0:T(8,128)(2,1)S(1)} %get-tuple-element.67.gram, bf16[504,512]{1,0:T(8,128)(2,1)S(1)} %get-tuple-element.68.refs_0_, ...), custom_call_target="tpu_custom_call" | custom-call | flops 1387266048 | bytes 6823936 | tf_op jit(solution)/shard_map/pallas_call | solution.py:62
  164.6 2.8 %shard_map.29.before = f32[448,576]{1,0:T(8,128)S(1)} custom-call(s32[2]{0:T(128)S(1)} %pad_add_fusion.place, f32[448,576]{1,0:T(8,128)S(1)} %shard_map.28.before, bf16[4,448,896]{2,1,0:T(8,128)(2,1)S(1)} %get-tuple-element.67.gram, bf16[504,512]{1,0:T(8,128)(2,1)S(1)} %collective-permute-done.35.r11, bf16[504,512]{1,0:T(8,128)(2,1)S(1)} %collective-permute-done.36.r31, ...), custom_call_target="tpu_custom_call" | custom-call | flops 924844032 | bytes 5791744 | tf_op jit(solution)/shard_map/pallas_call | solution.py:62
  167.4 2.0 %shard_map.30 = bf16[448,576]{1,0:T(8,128)(2,1)} custom-call(s32[2]{0:T(128)S(1)} %pad_add_fusion.place, f32[448,576]{1,0:T(8,128)S(1)} %shard_map.29.before, bf16[4,448,896]{2,1,0:T(8,128)(2,1)S(1)} %get-tuple-element.67.gram, bf16[256,512]{1,0:T(8,128)(2,1)S(1)} %collective-permute-done.37.refs_0_, bf16[248,512]{1,0:T(8,128)(2,1)S(1)} %collective-permute-done.38.refs_1_), custom_call_target="tpu_custom_call" | custom-call | flops 231211008 | bytes 4759552 | tf_op jit(solution)/shard_map/pallas_call | solution.py:62
  (50 shorter events, 0.8 us)
Async XLA Ops:
  0.1 1.1 copy-start
  1.8 12.5 %collective-permute-start.2 = (bf16[504,512]{1,0:T(8,128)(2,1)S(1)}, bf16[504,512]{1,0:T(8,128)(2,1)S(1)}, u32[]{:S(2)}, u32[]{:S(2)}) collective-permute-start(bf16[504,512]{1,0:T(8,128)(2,1)S(1)} %get-tuple-element.41.refs_0_), channel_id=1, source_target_pairs={{32,0},{0,32},{33,1},{1,33},{34,2},{2,34},{35,3},{3,35},{36,4},{4,... | collective-permute-start | bytes 1548296 | tf_op jit(solution)/shard_map/ppermute | solution.py:40
  4.0 13.3 %collective-permute-start.1 = (bf16[504,512]{1,0:T(8,128)(2,1)S(1)}, bf16[504,512]{1,0:T(8,128)(2,1)S(1)}, u32[]{:S(2)}, u32[]{:S(2)}) collective-permute-start(bf16[504,512]{1,0:T(8,128)(2,1)S(1)} %get-tuple-element.41.refs_0_), channel_id=1, source_target_pairs={{192,0},{0,64},{64,128},{128,192},{193,1},{1,65},{65,129},{129,193... | collective-permute-start | bytes 1548296 | tf_op jit(solution)/shard_map/ppermute | solution.py:40
  5.2 12.1 %collective-permute-start = (bf16[504,512]{1,0:T(8,128)(2,1)S(1)}, bf16[504,512]{1,0:T(8,128)(2,1)S(1)}, u32[]{:S(2)}, u32[]{:S(2)}) collective-permute-start(bf16[504,512]{1,0:T(8,128)(2,1)S(1)} %get-tuple-element.41.refs_0_), channel_id=1, source_target_pairs={{64,0},{128,64},{192,128},{0,192},{65,1},{129,65},{193,129},{1,193... | collective-permute-start | bytes 1548296 | tf_op jit(solution)/shard_map/ppermute | solution.py:40
  17.3 9.5 %collective-permute-start.5 = (bf16[256,512]{1,0:T(8,128)(2,1)S(1)}, bf16[256,512]{1,0:T(8,128)(2,1)S(1)}, u32[]{:S(2)}, u32[]{:S(2)}) collective-permute-start(bf16[256,512]{1,0:T(8,128)(2,1)S(1)} %slice.30), channel_id=1, source_target_pairs={{64,0},{128,64},{192,128},{0,192},{65,1},{129,65},{193,129},{1,193... | collective-permute-start | bytes 786440 | tf_op jit(solution)/shard_map/ppermute | solution.py:40
  19.8 7.0 %collective-permute-start.6 = (bf16[248,512]{1,0:T(8,128)(2,1)S(1)}, bf16[248,512]{1,0:T(8,128)(2,1)S(1)}, u32[]{:S(2)}, u32[]{:S(2)}) collective-permute-start(bf16[248,512]{1,0:T(8,128)(2,1)S(1)} %slice.31), channel_id=1, source_target_pairs={{192,0},{0,64},{64,128},{128,192},{193,1},{1,65},{65,129},{129,193... | collective-permute-start | bytes 761864 | tf_op jit(solution)/shard_map/ppermute | solution.py:40
  24.1 8.0 %collective-permute-start.8 = (bf16[8,56,896]{2,1,0:T(8,128)(2,1)S(1)}, bf16[8,56,896]{2,1,0:T(8,128)(2,1)S(1)}, u32[]{:S(2)}, u32[]{:S(2)}) collective-permute-start(bf16[8,56,896]{2,1,0:T(8,128)(2,1)S(1)} %get-tuple-element.47), channel_id=1, source_target_pairs={{1,0},{0,1},{3,2},{2,3},{5,4},{4,5},{7,6},{6,7},{9,8},{8,9},{11,10... | collective-permute-start | bytes 2408456 | tf_op jit(solution)/shard_map/ppermute | solution.py:40
  28.8 5.2 %collective-permute-start.9 = (bf16[8,56,896]{2,1,0:T(8,128)(2,1)S(1)}, bf16[8,56,896]{2,1,0:T(8,128)(2,1)S(1)}, u32[]{:S(2)}, u32[]{:S(2)}) collective-permute-start(bf16[8,56,896]{2,1,0:T(8,128)(2,1)S(1)} %get-tuple-element.50), channel_id=1, source_target_pairs={{1,0},{0,1},{3,2},{2,3},{5,4},{4,5},{7,6},{6,7},{9,8},{8,9},{11,10... | collective-permute-start | bytes 2408456 | tf_op jit(solution)/shard_map/ppermute | solution.py:40
  35.0 7.5 %collective-permute-start.14 = (bf16[56,896]{1,0:T(8,128)(2,1)S(1)}, bf16[56,896]{1,0:T(8,128)(2,1)S(1)}, u32[]{:S(2)}, u32[]{:S(2)}) collective-permute-start(bf16[56,896]{1,0:T(8,128)(2,1)S(1)} %get-tuple-element.59), channel_id=1, source_target_pairs={{4,0},{8,4},{12,8},{16,12},{20,16},{24,20},{28,24},{0,28},{5,1},{9... | collective-permute-start | bytes 301064 | tf_op jit(solution)/shard_map/ppermute | solution.py:40
  40.6 5.3 %collective-permute-start.10 = (bf16[56,896]{1,0:T(8,128)(2,1)S(1)}, bf16[56,896]{1,0:T(8,128)(2,1)S(1)}, u32[]{:S(2)}, u32[]{:S(2)}) collective-permute-start(bf16[56,896]{1,0:T(8,128)(2,1)S(1)} %get-tuple-element.55), channel_id=1, source_target_pairs={{28,0},{0,4},{4,8},{8,12},{12,16},{16,20},{20,24},{24,28},{29,1},{... | collective-permute-start | bytes 301064 | tf_op jit(solution)/shard_map/ppermute | solution.py:40
  42.5 6.6 %collective-permute-start.15 = (bf16[112,896]{1,0:T(8,128)(2,1)S(1)}, bf16[112,896]{1,0:T(8,128)(2,1)S(1)}, u32[]{:S(2)}, u32[]{:S(2)}) collective-permute-start(bf16[112,896]{1,0:T(8,128)(2,1)S(1)} %pad_maximum_fusion.2), channel_id=1, source_target_pairs={{4,0},{8,4},{12,8},{16,12},{20,16},{24,20},{28,24},{0,28},{5,1},{9... | collective-permute-start | bytes 602120 | tf_op jit(solution)/shard_map/ppermute | solution.py:40
  46.1 6.6 %collective-permute-start.11 = (bf16[112,896]{1,0:T(8,128)(2,1)S(1)}, bf16[112,896]{1,0:T(8,128)(2,1)S(1)}, u32[]{:S(2)}, u32[]{:S(2)}) collective-permute-start(bf16[112,896]{1,0:T(8,128)(2,1)S(1)} %pad_maximum_fusion.1), channel_id=1, source_target_pairs={{28,0},{0,4},{4,8},{8,12},{12,16},{16,20},{20,24},{24,28},{29,1},{... | collective-permute-start | bytes 602120 | tf_op jit(solution)/shard_map/ppermute | solution.py:40
  49.2 6.1 %collective-permute-start.16 = (bf16[112,896]{1,0:T(8,128)(2,1)S(1)}, bf16[112,896]{1,0:T(8,128)(2,1)S(1)}, u32[]{:S(2)}, u32[]{:S(2)}) collective-permute-start(bf16[112,896]{1,0:T(8,128)(2,1)S(1)} %add_convert_fusion.1), channel_id=1, source_target_pairs={{4,0},{8,4},{12,8},{16,12},{20,16},{24,20},{28,24},{0,28},{5,1},{9... | collective-permute-start | bytes 602120 | tf_op jit(solution)/shard_map/ppermute | solution.py:40
  52.7 6.0 %collective-permute-start.12 = (bf16[112,896]{1,0:T(8,128)(2,1)S(1)}, bf16[112,896]{1,0:T(8,128)(2,1)S(1)}, u32[]{:S(2)}, u32[]{:S(2)}) collective-permute-start(bf16[112,896]{1,0:T(8,128)(2,1)S(1)} %add_convert_fusion.3), channel_id=1, source_target_pairs={{28,0},{0,4},{4,8},{8,12},{12,16},{16,20},{20,24},{24,28},{29,1},{... | collective-permute-start | bytes 602120 | tf_op jit(solution)/shard_map/ppermute | solution.py:40
  55.4 5.9 %collective-permute-start.17 = (bf16[112,896]{1,0:T(8,128)(2,1)S(1)}, bf16[112,896]{1,0:T(8,128)(2,1)S(1)}, u32[]{:S(2)}, u32[]{:S(2)}) collective-permute-start(bf16[112,896]{1,0:T(8,128)(2,1)S(1)} %add_convert_fusion), channel_id=1, source_target_pairs={{4,0},{8,4},{12,8},{16,12},{20,16},{24,20},{28,24},{0,28},{5,1},{9... | collective-permute-start | bytes 602120 | tf_op jit(solution)/shard_map/ppermute | solution.py:40
  58.8 5.9 %collective-permute-start.13 = (bf16[112,896]{1,0:T(8,128)(2,1)S(1)}, bf16[112,896]{1,0:T(8,128)(2,1)S(1)}, u32[]{:S(2)}, u32[]{:S(2)}) collective-permute-start(bf16[112,896]{1,0:T(8,128)(2,1)S(1)} %add_convert_fusion.2), channel_id=1, source_target_pairs={{28,0},{0,4},{4,8},{8,12},{12,16},{16,20},{20,24},{24,28},{29,1},{... | collective-permute-start | bytes 602120 | tf_op jit(solution)/shard_map/ppermute | solution.py:40
  65.3 7.4 %collective-permute-start.18 = (bf16[112,896]{1,0:T(8,128)(2,1)S(1)}, bf16[112,896]{1,0:T(8,128)(2,1)S(1)}, u32[]{:S(2)}, u32[]{:S(2)}) collective-permute-start(bf16[112,896]{1,0:T(8,128)(2,1)S(1)} %get-tuple-element.60.mine), channel_id=1, source_target_pairs={{2,0},{0,2},{3,1},{1,3},{6,4},{4,6},{7,5},{5,7},{10,8},{8,10},{11,... | collective-permute-start | bytes 602120 | tf_op jit(solution)/shard_map/ppermute | solution.py:40
  68.0 4.7 %collective-permute-start.20 = (bf16[56,896]{1,0:T(8,128)(2,1)S(1)}, bf16[56,896]{1,0:T(8,128)(2,1)S(1)}, u32[]{:S(2)}, u32[]{:S(2)}) collective-permute-start(bf16[56,896]{1,0:T(8,128)(2,1)S(1)} %get-tuple-element.61), channel_id=1, source_target_pairs={{34,0},{32,2},{2,32},{0,34},{35,1},{33,3},{3,33},{1,35},{38,4},{36... | collective-permute-start | bytes 301064 | tf_op jit(solution)/shard_map/ppermute | solution.py:53
  68.0 4.7 %collective-permute-start.19 = (bf16[56,896]{1,0:T(8,128)(2,1)S(1)}, bf16[56,896]{1,0:T(8,128)(2,1)S(1)}, u32[]{:S(2)}, u32[]{:S(2)}) collective-permute-start(bf16[56,896]{1,0:T(8,128)(2,1)S(1)} %get-tuple-element.61), channel_id=1, source_target_pairs={{32,0},{0,32},{33,1},{1,33},{34,2},{2,34},{35,3},{3,35},{36,4},{4,... | collective-permute-start | bytes 301064 | tf_op jit(solution)/shard_map/ppermute | solution.py:40
  73.3 5.9 %collective-permute-start.24 = (bf16[112,896]{1,0:T(8,128)(2,1)S(1)}, bf16[112,896]{1,0:T(8,128)(2,1)S(1)}, u32[]{:S(2)}, u32[]{:S(2)}) collective-permute-start(bf16[112,896]{1,0:T(8,128)(2,1)S(1)} %shard_map.23.refs_0_), channel_id=1, source_target_pairs={{28,0},{0,4},{4,8},{8,12},{12,16},{16,20},{20,24},{24,28},{29,1},{... | collective-permute-start | bytes 602120 | tf_op jit(solution)/shard_map/ppermute | solution.py:40
  73.4 5.8 %collective-permute-start.21 = (bf16[112,896]{1,0:T(8,128)(2,1)S(1)}, bf16[112,896]{1,0:T(8,128)(2,1)S(1)}, u32[]{:S(2)}, u32[]{:S(2)}) collective-permute-start(bf16[112,896]{1,0:T(8,128)(2,1)S(1)} %shard_map.23.refs_0_), channel_id=1, source_target_pairs={{4,0},{8,4},{12,8},{16,12},{20,16},{24,20},{28,24},{0,28},{5,1},{9... | collective-permute-start | bytes 602120 | tf_op jit(solution)/shard_map/ppermute | solution.py:40
  79.2 7.4 %collective-permute-start.25 = (bf16[112,896]{1,0:T(8,128)(2,1)S(1)}, bf16[112,896]{1,0:T(8,128)(2,1)S(1)}, u32[]{:S(2)}, u32[]{:S(2)}) collective-permute-start(bf16[112,896]{1,0:T(8,128)(2,1)S(1)} %collective-permute-done.24.refs_6_), channel_id=1, source_target_pairs={{28,0},{0,4},{4,8},{8,12},{12,16},{16,20},{20,24},{24,28},{29,1},{... | collective-permute-start | bytes 602120 | tf_op jit(solution)/shard_map/ppermute | solution.py:40
  79.2 7.4 %collective-permute-start.22 = (bf16[112,896]{1,0:T(8,128)(2,1)S(1)}, bf16[112,896]{1,0:T(8,128)(2,1)S(1)}, u32[]{:S(2)}, u32[]{:S(2)}) collective-permute-start(bf16[112,896]{1,0:T(8,128)(2,1)S(1)} %collective-permute-done.21.refs_1_), channel_id=1, source_target_pairs={{4,0},{8,4},{12,8},{16,12},{20,16},{24,20},{28,24},{0,28},{5,1},{9... | collective-permute-start | bytes 602120 | tf_op jit(solution)/shard_map/ppermute | solution.py:40
  86.6 6.6 %collective-permute-start.26 = (bf16[112,896]{1,0:T(8,128)(2,1)S(1)}, bf16[112,896]{1,0:T(8,128)(2,1)S(1)}, u32[]{:S(2)}, u32[]{:S(2)}) collective-permute-start(bf16[112,896]{1,0:T(8,128)(2,1)S(1)} %collective-permute-done.25.refs_5_), channel_id=1, source_target_pairs={{28,0},{0,4},{4,8},{8,12},{12,16},{16,20},{20,24},{24,28},{29,1},{... | collective-permute-start | bytes 602120 | tf_op jit(solution)/shard_map/ppermute | solution.py:40
  86.6 6.6 %collective-permute-start.23 = (bf16[112,896]{1,0:T(8,128)(2,1)S(1)}, bf16[112,896]{1,0:T(8,128)(2,1)S(1)}, u32[]{:S(2)}, u32[]{:S(2)}) collective-permute-start(bf16[112,896]{1,0:T(8,128)(2,1)S(1)} %collective-permute-done.22.refs_2_), channel_id=1, source_target_pairs={{4,0},{8,4},{12,8},{16,12},{20,16},{24,20},{28,24},{0,28},{5,1},{9... | collective-permute-start | bytes 602120 | tf_op jit(solution)/shard_map/ppermute | solution.py:40
  93.8 29.9 %collective-permute-start.27 = (bf16[7,112,896]{2,1,0:T(8,128)(2,1)S(1)}, bf16[7,112,896]{2,1,0:T(8,128)(2,1)S(1)}, u32[]{:S(2)}, u32[]{:S(2)}) collective-permute-start(bf16[7,112,896]{2,1,0:T(8,128)(2,1)S(1)} %shard_map.24.group), channel_id=1, source_target_pairs={{1,0},{0,1},{3,2},{2,3},{5,4},{4,5},{7,6},{6,7},{9,8},{8,9},{11,10... | collective-permute-start | bytes 4214792 | tf_op jit(solution)/shard_map/ppermute | solution.py:40
  102.9 16.8 %collective-permute-start.4 = (bf16[504,512]{1,0:T(8,128)(2,1)S(1)}, bf16[504,512]{1,0:T(8,128)(2,1)S(1)}, u32[]{:S(2)}, u32[]{:S(2)}) collective-permute-start(bf16[504,512]{1,0:T(8,128)(2,1)S(1)} %collective-permute-done.2.refs_3_), channel_id=1, source_target_pairs={{192,0},{0,64},{64,128},{128,192},{193,1},{1,65},{65,129},{129,193... | collective-permute-start | bytes 1548296 | tf_op jit(solution)/shard_map/ppermute | solution.py:40
  102.9 16.8 %collective-permute-start.3 = (bf16[504,512]{1,0:T(8,128)(2,1)S(1)}, bf16[504,512]{1,0:T(8,128)(2,1)S(1)}, u32[]{:S(2)}, u32[]{:S(2)}) collective-permute-start(bf16[504,512]{1,0:T(8,128)(2,1)S(1)} %collective-permute-done.2.refs_3_), channel_id=1, source_target_pairs={{64,0},{128,64},{192,128},{0,192},{65,1},{129,65},{193,129},{1,193... | collective-permute-start | bytes 1548296 | tf_op jit(solution)/shard_map/ppermute | solution.py:40
  105.6 14.1 %collective-permute-start.7 = (bf16[504,512]{1,0:T(8,128)(2,1)S(1)}, bf16[504,512]{1,0:T(8,128)(2,1)S(1)}, u32[]{:S(2)}, u32[]{:S(2)}) collective-permute-start(bf16[504,512]{1,0:T(8,128)(2,1)S(1)} %pad_maximum_fusion), channel_id=1, source_target_pairs={{32,0},{0,32},{33,1},{1,33},{34,2},{2,34},{35,3},{3,35},{36,4},{4,... | collective-permute-start | bytes 1548296 | tf_op jit(solution)/shard_map/ppermute | solution.py:40
  106.9 4.7 %collective-permute-start.28 = (bf16[56,896]{1,0:T(8,128)(2,1)S(1)}, bf16[56,896]{1,0:T(8,128)(2,1)S(1)}, u32[]{:S(2)}, u32[]{:S(2)}) collective-permute-start(bf16[56,896]{1,0:T(8,128)(2,1)S(1)} %slice.40), channel_id=1, source_target_pairs={{4,0},{8,4},{12,8},{16,12},{20,16},{24,20},{28,24},{0,28},{5,1},{9... | collective-permute-start | bytes 301064 | tf_op jit(solution)/shard_map/ppermute | solution.py:40
  111.5 5.7 %collective-permute-start.29 = (bf16[56,896]{1,0:T(8,128)(2,1)S(1)}, bf16[56,896]{1,0:T(8,128)(2,1)S(1)}, u32[]{:S(2)}, u32[]{:S(2)}) collective-permute-start(bf16[56,896]{1,0:T(8,128)(2,1)S(1)} %slice.41), channel_id=1, source_target_pairs={{28,0},{0,4},{4,8},{8,12},{12,16},{16,20},{20,24},{24,28},{29,1},{... | collective-permute-start | bytes 301064 | tf_op jit(solution)/shard_map/ppermute | solution.py:40
  117.2 9.0 %collective-permute-start.30 = (bf16[112,896]{1,0:T(8,128)(2,1)S(1)}, bf16[112,896]{1,0:T(8,128)(2,1)S(1)}, u32[]{:S(2)}, u32[]{:S(2)}) collective-permute-start(bf16[112,896]{1,0:T(8,128)(2,1)S(1)} %constant_dynamic-update-slice_fusion.mine), channel_id=1, source_target_pairs={{1,0},{0,1},{3,2},{2,3},{5,4},{4,5},{7,6},{6,7},{9,8},{8,9},{11,10... | collective-permute-start | bytes 602120 | tf_op jit(solution)/shard_map/ppermute | solution.py:40
  128.7 13.2 %collective-permute-start.33 = (bf16[504,512]{1,0:T(8,128)(2,1)S(1)}, bf16[504,512]{1,0:T(8,128)(2,1)S(1)}, u32[]{:S(2)}, u32[]{:S(2)}) collective-permute-start(bf16[504,512]{1,0:T(8,128)(2,1)S(1)} %get-tuple-element.68.refs_0_), channel_id=1, source_target_pairs={{32,0},{0,32},{33,1},{1,33},{34,2},{2,34},{35,3},{3,35},{36,4},{4,... | collective-permute-start | bytes 1548296 | tf_op jit(solution)/shard_map/ppermute | solution.py:40
  129.1 13.2 %collective-permute-start.32 = (bf16[504,512]{1,0:T(8,128)(2,1)S(1)}, bf16[504,512]{1,0:T(8,128)(2,1)S(1)}, u32[]{:S(2)}, u32[]{:S(2)}) collective-permute-start(bf16[504,512]{1,0:T(8,128)(2,1)S(1)} %get-tuple-element.68.refs_0_), channel_id=1, source_target_pairs={{192,0},{0,64},{64,128},{128,192},{193,1},{1,65},{65,129},{129,193... | collective-permute-start | bytes 1548296 | tf_op jit(solution)/shard_map/ppermute | solution.py:40
  129.1 13.2 %collective-permute-start.31 = (bf16[504,512]{1,0:T(8,128)(2,1)S(1)}, bf16[504,512]{1,0:T(8,128)(2,1)S(1)}, u32[]{:S(2)}, u32[]{:S(2)}) collective-permute-start(bf16[504,512]{1,0:T(8,128)(2,1)S(1)} %get-tuple-element.68.refs_0_), channel_id=1, source_target_pairs={{64,0},{128,64},{192,128},{0,192},{65,1},{129,65},{193,129},{1,193... | collective-permute-start | bytes 1548296 | tf_op jit(solution)/shard_map/ppermute | solution.py:40
  142.3 11.1 %collective-permute-start.35 = (bf16[504,512]{1,0:T(8,128)(2,1)S(1)}, bf16[504,512]{1,0:T(8,128)(2,1)S(1)}, u32[]{:S(2)}, u32[]{:S(2)}) collective-permute-start(bf16[504,512]{1,0:T(8,128)(2,1)S(1)} %collective-permute-done.33.refs_3_), channel_id=1, source_target_pairs={{64,0},{128,64},{192,128},{0,192},{65,1},{129,65},{193,129},{1,193... | collective-permute-start | bytes 1548296 | tf_op jit(solution)/shard_map/ppermute | solution.py:40
  144.7 11.7 %collective-permute-start.36 = (bf16[504,512]{1,0:T(8,128)(2,1)S(1)}, bf16[504,512]{1,0:T(8,128)(2,1)S(1)}, u32[]{:S(2)}, u32[]{:S(2)}) collective-permute-start(bf16[504,512]{1,0:T(8,128)(2,1)S(1)} %collective-permute-done.32.refs_2_), channel_id=1, source_target_pairs={{32,0},{0,32},{33,1},{1,33},{34,2},{2,34},{35,3},{3,35},{36,4},{4,... | collective-permute-start | bytes 1548296 | tf_op jit(solution)/shard_map/ppermute | solution.py:40
  146.7 12.4 %collective-permute-start.34 = (bf16[504,512]{1,0:T(8,128)(2,1)S(1)}, bf16[504,512]{1,0:T(8,128)(2,1)S(1)}, u32[]{:S(2)}, u32[]{:S(2)}) collective-permute-start(bf16[504,512]{1,0:T(8,128)(2,1)S(1)} %collective-permute-done.32.refs_2_), channel_id=1, source_target_pairs={{192,0},{0,64},{64,128},{128,192},{193,1},{1,65},{65,129},{129,193... | collective-permute-start | bytes 1548296 | tf_op jit(solution)/shard_map/ppermute | solution.py:40
  159.1 8.3 %collective-permute-start.37 = (bf16[256,512]{1,0:T(8,128)(2,1)S(1)}, bf16[256,512]{1,0:T(8,128)(2,1)S(1)}, u32[]{:S(2)}, u32[]{:S(2)}) collective-permute-start(bf16[256,512]{1,0:T(8,128)(2,1)S(1)} %slice.38), channel_id=1, source_target_pairs={{64,0},{128,64},{192,128},{0,192},{65,1},{129,65},{193,129},{1,193... | collective-permute-start | bytes 786440 | tf_op jit(solution)/shard_map/ppermute | solution.py:40
  159.2 8.2 %collective-permute-start.38 = (bf16[248,512]{1,0:T(8,128)(2,1)S(1)}, bf16[248,512]{1,0:T(8,128)(2,1)S(1)}, u32[]{:S(2)}, u32[]{:S(2)}) collective-permute-start(bf16[248,512]{1,0:T(8,128)(2,1)S(1)} %slice.39), channel_id=1, source_target_pairs={{192,0},{0,64},{64,128},{128,192},{193,1},{1,65},{65,129},{129,193... | collective-permute-start | bytes 761864 | tf_op jit(solution)/shard_map/ppermute | solution.py:40
